TPU v7x, 32 devices: a whole 2x2x4 slice. The times are simulated.
32 devices in a mesh: sec: 2 (over core), lat: 8 (over z, y), head: 2 (over x).
Axes of the slice: x: 2, y: 2, z: 4, core: 2. Of those that a mesh axis runs over, the one named last changes fastest.
Arguments:
- fields: bfloat16 [2, 96, 96, 192], P(None, 'lat', ('sec', 'head')), may hold values from -6 to 6
- land_sea: int32 [96, 96], P('lat', ('sec', 'head')), may hold values 0 or 1
- land_embed: float32 [192], replicated, may hold values from -4 to 4
- bias_index: int32 [144, 144], replicated, may hold values from 0 to 3311
- fine_bias: float32 [2, 6, 3312], replicated, may hold values from -4 to 254
- fine_gains: float32 [2, 2, 192], replicated, may hold values from 0.1 to 1.9
- fine_query_key_value: bfloat16 [2, 192, 576], replicated, may hold values from -0.4375 to 0.4375
- fine_project: bfloat16 [2, 192, 192], replicated, may hold values from -0.4375 to 0.4375
- fine_widen: bfloat16 [2, 192, 768], replicated, may hold values from -0.4375 to 0.4375
- fine_narrow: bfloat16 [2, 768, 192], replicated, may hold values from -0.21875 to 0.21875
- merge_gain: float32 [768], replicated, may hold values from 0.1 to 1.9
- merge_weight: bfloat16 [768, 384], replicated, may hold values from -0.21875 to 0.21875
- coarse_bias: float32 [2, 12, 3312], replicated, may hold values from -4 to 254
- coarse_gains: float32 [2, 2, 384], replicated, may hold values from 0.1 to 1.9
- coarse_query_key_value: bfloat16 [2, 384, 1152], replicated, may hold values from -0.3125 to 0.3125
- coarse_project: bfloat16 [2, 384, 384], replicated, may hold values from -0.3125 to 0.3125
- coarse_widen: bfloat16 [2, 384, 1536], replicated, may hold values from -0.3125 to 0.3125
- coarse_narrow: bfloat16 [2, 1536, 384], replicated, may hold values from -0.15625 to 0.15625
- expand_weight: bfloat16 [384, 768], replicated, may hold values from -0.3125 to 0.3125
- expand_gain: float32 [192], replicated, may hold values from 0.1 to 1.9
Outputs:
- forecast: bfloat16 [2, 96, 96, 192], P(None, 'lat', ('sec', 'head'))
All inputs are finite; a program needn't handle non-finite values. No bound on the sum of `land_sea` on one device may be relied on, other than what follows from the above.
Results may differ from a plain program's by a relative error of at most 0.019.
Values may be sent and summed in bfloat16 or wider, within the bound.
No kernel may reach another device: no remote copies, remote signals or barrier semaphores. Data moves between devices by JAX's collectives and lax.ppermute only.
A program may use at most 128 MiB of HBM per device.

v0:
```python
import jax
import jax.numpy as jnp
from jax import lax
from jax.sharding import PartitionSpec as P

HF = 6
HC = 12
WIN_LAT = 6
WIN_LON = 12
WIN_TOK = 144


def with_halo(cells, sides, width):
    for axis, dim in sides:
        count = lax.axis_size(axis)
        head = lax.slice_in_dim(cells, 0, width, axis=dim)
        tail = lax.slice_in_dim(cells, cells.shape[dim] - width, cells.shape[dim], axis=dim)
        cells = jnp.concatenate(
            [
                lax.ppermute(tail, axis, [(i, (i + 1) % count) for i in range(count)]),
                cells,
                lax.ppermute(head, axis, [((i + 1) % count, i) for i in range(count)]),
            ],
            axis=dim,
        )
    return cells


def shifted_2(value, axis, steps):
    count = lax.axis_size(axis)
    pairs = [(source, (source + steps) % count) for source in range(count)]
    return lax.ppermute(value, axis, pairs)


def layer_norm(values, norm_gain):
    as_float = values.astype(jnp.float32)
    average = jnp.mean(as_float, axis=-1, keepdims=True)
    centered = as_float - average
    variance = jnp.mean(centered * centered, axis=-1, keepdims=True)
    return centered * lax.rsqrt(variance + 1e-05) * norm_gain


def attend(normed, w_triple, position_bias, region, head_count):
    level_count, row_count, col_count, channels = normed.shape
    head_size = channels // head_count
    lat_windows = row_count // WIN_LAT
    lon_windows = col_count // WIN_LON
    triple = jnp.dot(
        normed.reshape(-1, channels), w_triple, preferred_element_type=jnp.float32
    ).astype(jnp.bfloat16)
    triple = triple.reshape(
        level_count, lat_windows, WIN_LAT, lon_windows, WIN_LON, 3, head_count, head_size
    )
    triple = triple.transpose(5, 1, 3, 6, 0, 2, 4, 7).reshape(
        3, lat_windows, lon_windows, head_count, WIN_TOK, head_size
    )
    scores = jnp.einsum(
        "abhqd,abhkd->abhqk", triple[0], triple[1], preferred_element_type=jnp.float32
    )
    scores = scores * head_size ** (-0.5) + position_bias
    if region is not None:
        token_region = jnp.broadcast_to(
            region.reshape(lat_windows, 1, WIN_LAT, 1), (lat_windows, level_count, WIN_LAT, WIN_LON)
        ).reshape(lat_windows, WIN_TOK)
        same_region = token_region[:, :, None] == token_region[:, None, :]
        scores = jnp.where(same_region[:, None, None], scores, -1e30)
    attention = jax.nn.softmax(scores, axis=-1).astype(jnp.bfloat16)
    context = jnp.einsum(
        "abhqk,abhkd->abhqd", attention, triple[2], preferred_element_type=jnp.float32
    ).astype(jnp.bfloat16)
    context = context.reshape(
        lat_windows, lon_windows, head_count, level_count, WIN_LAT, WIN_LON, head_size
    )
    return context.transpose(3, 0, 4, 1, 5, 2, 6).reshape(
        level_count, row_count, col_count, channels
    )


def finish(stream, context, norm_gains, w_project, w_widen, w_narrow):
    channels = stream.shape[-1]
    flat_stream = stream.reshape(-1, channels)
    projected = jnp.dot(
        context.reshape(-1, channels), w_project, preferred_element_type=jnp.float32
    )
    middle = lax.optimization_barrier(
        (flat_stream.astype(jnp.float32) + projected).astype(jnp.bfloat16)
    )
    normed = layer_norm(middle, norm_gains[1]).astype(jnp.bfloat16)
    hidden = jax.nn.gelu(
        jnp.dot(normed, w_widen, preferred_element_type=jnp.float32), approximate=False
    ).astype(jnp.bfloat16)
    result = (
        middle.astype(jnp.float32) + jnp.dot(hidden, w_narrow, preferred_element_type=jnp.float32)
    ).astype(jnp.bfloat16)
    return lax.optimization_barrier(result).reshape(stream.shape)


def widen_lon(values):
    return with_halo(values, ((("sec", "head"), 2),), WIN_LON // 2)


def local_block(
    stream, shifted, position_bias, norm_gains, w_triple, w_project, w_widen, w_narrow, head_count
):
    if not shifted:
        normed = layer_norm(stream, norm_gains[0]).astype(jnp.bfloat16)
        context = attend(normed, w_triple, position_bias, None, head_count)
        return finish(stream, context, norm_gains, w_project, w_widen, w_narrow)
    half_lat = WIN_LAT // 2
    half_lon = WIN_LON // 2
    row_count = stream.shape[1]
    col_count = stream.shape[2]
    lat_total = lax.axis_size("lat") * row_count
    first_row = lax.axis_index("lat") * row_count
    next_rows = shifted_2(stream[:, :half_lat], "lat", -1)
    rolled = jnp.concatenate([stream[:, half_lat:], next_rows], axis=1)
    global_row = first_row + half_lat + jnp.arange(row_count, dtype=jnp.int32)
    region = (global_row >= lat_total).astype(jnp.int32)
    normed = layer_norm(widen_lon(rolled), norm_gains[0]).astype(jnp.bfloat16)
    context = attend(normed, w_triple, position_bias, region, head_count)
    context = context[:, :, half_lon : half_lon + col_count]
    result = finish(rolled, context, norm_gains, w_project, w_widen, w_narrow)
    behind = shifted_2(result[:, row_count - half_lat :], "lat", 1)
    return jnp.concatenate([behind, result[:, : row_count - half_lat]], axis=1)


def merge_patches(stream, norm_gain, weight_matrix):
    level_count, row_count, col_count, channels = stream.shape
    grouped = stream.reshape(level_count, row_count // 2, 2, col_count // 2, 2, channels)
    grouped = grouped.transpose(0, 1, 3, 2, 4, 5).reshape(-1, 4 * channels)
    normed = layer_norm(grouped, norm_gain).astype(jnp.bfloat16)
    merged = jnp.dot(normed, weight_matrix, preferred_element_type=jnp.float32).astype(jnp.bfloat16)
    merged = lax.optimization_barrier(merged)
    return merged.reshape(level_count, row_count // 2, col_count // 2, -1)


def expand_patches(coarse, weight_matrix, norm_gain, skip_stream):
    level_count, row_count, col_count, channels = coarse.shape
    widened = jnp.dot(
        coarse.reshape(-1, channels), weight_matrix, preferred_element_type=jnp.float32
    )
    fine_channels = weight_matrix.shape[1] // 4
    shuffled = widened.reshape(level_count, row_count, col_count, 2, 2, fine_channels)
    shuffled = shuffled.transpose(0, 1, 3, 2, 4, 5).reshape(
        level_count, 2 * row_count, 2 * col_count, fine_channels
    )
    return (skip_stream.astype(jnp.float32) + layer_norm(shuffled, norm_gain)).astype(jnp.bfloat16)


def on_device(
    fields,
    land_sea,
    land_embed,
    bias_index,
    fine_bias,
    fine_gains,
    fine_query_key_value,
    fine_project,
    fine_widen,
    fine_narrow,
    merge_gain,
    merge_weight,
    coarse_bias,
    coarse_gains,
    coarse_query_key_value,
    coarse_project,
    coarse_widen,
    coarse_narrow,
    expand_weight,
    expand_gain,
):
    stream = (
        fields.astype(jnp.float32) + land_sea.astype(jnp.float32)[None, :, :, None] * land_embed
    )
    stream = lax.optimization_barrier(stream.astype(jnp.bfloat16))
    for block_number in range(2):
        position_bias = jnp.take(fine_bias[block_number], bias_index, axis=1)
        stream = local_block(
            stream,
            block_number == 1,
            position_bias,
            fine_gains[block_number],
            fine_query_key_value[block_number],
            fine_project[block_number],
            fine_widen[block_number],
            fine_narrow[block_number],
            HF,
        )
    coarse = merge_patches(stream, merge_gain, merge_weight)
    for block_number in range(2):
        position_bias = jnp.take(coarse_bias[block_number], bias_index, axis=1)
        coarse = local_block(
            coarse,
            block_number == 1,
            position_bias,
            coarse_gains[block_number],
            coarse_query_key_value[block_number],
            coarse_project[block_number],
            coarse_widen[block_number],
            coarse_narrow[block_number],
            HC,
        )
    return expand_patches(coarse, expand_weight, expand_gain, stream)


def solution(mesh):
    placed = (
        P(None, "lat", ("sec", "head"), None),
        P("lat", ("sec", "head")),
        P(),
        P(),
        P(),
        P(),
        P(),
        P(),
        P(),
        P(),
        P(),
        P(),
        P(),
        P(),
        P(),
        P(),
        P(),
        P(),
        P(),
        P(),
    )
    return jax.shard_map(
        on_device,
        mesh=mesh,
        in_specs=placed,
        out_specs=P(None, "lat", ("sec", "head"), None),
        check_vma=False,
    )
```

profile of v0, /device:TPU:0, one launch (start us, length us, event | category | flops | bytes accessed | tf_op | source)
XLA Modules:
  0.0 377.6 jit_solution(449550823186298793)
XLA Ops:
  0.0 1.0 compare_select_fusion
  1.0 1.6 compare_and_fusion
  3.3 0.8 broadcast_multiply_fusion
  4.1 1.0 add_convert_fusion
  6.8 3.9 %reshape.622 = bf16[2,2,6,2,12,3,6,32]{7,6,5,4,3,2,1,0:T(8,128)(2,1)} reshape(bf16[576,576]{1,0:T(8,128)(2,1)S(1)} %convolution_convert_fusion.3) | data formatting | bytes 1327104 | tf_op jit(solution)/shard_map/reshape | solution.py:51
  10.7 4.0 %fusion.497 = (bf16[1,2,2,6,2,6,12,32]{7,3,0,6,2,5,1,4:T(8,128)(2,1)}, bf16[1,2,2,6,2,6,12,32]{7,3,0,6,2,5,1,4:T(8,128)(2,1)S(1)}, bf16[1,2,2,6,2,6,12,32]{7,3,0,6,2,5,1,4:T(8,128)(2,1)S(1)}) fusion(bf16[3,2,2,6,2,6,12,32]{7,3,0,6,2,5,1,4:T(8,128)(2,1)} %bitcast.172), kind=kLoop, calls=%fused_computation.578 | loop fusion | bytes 1327104 | tf_op jit(solution)/shard_map/slice | solution.py:69
  14.7 1.7 copy.175
  16.4 1.6 copy.176
  19.5 38.7 %gather_fusion = f32[20736,6]{1,0:T(8,128)} fusion(f32[6,3312]{0,1:T(8,128)S(1)} %bitcast.167, s32[21504]{0:T(1024)S(1)} %pad_clamp_fusion), kind=kCustom, calls=%fused_computation.clone | custom fusion | bytes 1078272 | tf_op jit(solution)/shard_map/jit(_take)/gather | solution.py:177
  58.1 11.6 %copy.181 = f32[144,144,6]{0,1,2:T(8,128)S(1)} copy(f32[144,144,6]{2,1,0:T(8,128)} %bitcast.174) | data formatting | bytes 995328 | tf_op jit(solution)/shard_map/jit(_take)/gather | solution.py:177
  69.8 1.4 copy.263
  71.2 38.7 %gather_fusion.1 = f32[20736,6]{1,0:T(8,128)} fusion(f32[6,3312]{0,1:T(8,128)S(1)} %bitcast.168, s32[21504]{0:T(1024)S(1)} %pad_clamp_fusion), kind=kCustom, calls=%fused_computation.2.clone | custom fusion | bytes 1078272 | tf_op jit(solution)/shard_map/jit(_take)/gather | solution.py:177
  109.8 12.2 %copy.196 = f32[144,144,6]{0,1,2:T(8,128)} copy(f32[144,144,6]{2,1,0:T(8,128)} %bitcast.175) | data formatting | bytes 995328 | tf_op jit(solution)/shard_map/jit(_take)/gather | solution.py:177
  124.8 1.1 select_bitcast_fusion.1
  126.0 1.4 fusion.504
  127.8 1.0 copy.185
  130.6 5.5 %fusion.55 = bf16[576,192]{0,1:T(8,128)(2,1)S(1)} fusion(bf16[576,192]{0,1:T(8,128)(2,1)S(1)} %fusion.53, bf16[2,768,192]{1,2,0:T(8,128)(2,1)S(1)} %copy-done.32, bf16[2,192,768]{2,1,0:T(8,128)(2,1)} %param.32, f32[192]{0:T(256)S(1)} %bitcast.207, f32[576]{0:T(1024)S(1)} %add_rsqrt_fusion.6, f32[576]{0:T(1024)S(1)} %broadcast_multiply_fusion.7), kind=kOutput, calls=%fused_computation.98 | convolution fusion | flops 369377280 | bytes 1311744 | tf_op jit(solution)/shard_map/dot_general | solution.py:93
  136.3 6.1 %collective-permute-start = (bf16[2,3,24,192]{3,2,1,0:T(8,128)(2,1)S(1)}, bf16[2,3,24,192]{3,2,1,0:T(8,128)(2,1)S(1)}, u32[]{:S(2)}, u32[]{:S(2)}) collective-permute-start(bf16[2,3,24,192]{3,2,1,0:T(8,128)(2,1)S(1)} %slice.260), channel_id=1, source_target_pairs={{0,14},{2,0},{4,2},{6,4},{8,6},{10,8},{12,10},{14,12},{1,15},{3,1}... | collective-permute-start | bytes 165896 | tf_op jit(solution)/shard_map/ppermute | solution.py:32
  143.4 38.7 %gather_fusion.3 = f32[20736,12]{1,0:T(8,128)} fusion(f32[12,3312]{0,1:T(8,128)S(1)} %bitcast.166, s32[21504]{0:T(1024)S(1)} %pad_clamp_fusion), kind=kCustom, calls=%fused_computation.3.clone | custom fusion | bytes 2073600 | tf_op jit(solution)/shard_map/jit(_take)/gather | solution.py:191
  182.1 11.6 %copy.225 = f32[144,144,12]{0,1,2:T(8,128)S(1)} copy(f32[144,144,12]{2,1,0:T(8,128)} %bitcast.171) | data formatting | bytes 1990656 | tf_op jit(solution)/shard_map/jit(_take)/gather | solution.py:191
  193.7 1.4 select_bitcast_fusion
  196.4 1.5 collective-permute-start.1
  198.5 3.2 collective-permute-done.1
  201.7 2.1 collective-permute-done.2
  205.2 1.5 convolution_convert_fusion.2
  206.7 12.8 %copy.189 = bf16[864,576]{1,0:T(8,128)(2,1)S(1)} copy(bf16[864,576]{0,1:T(8,128)(2,1)} %convolution_convert_fusion.2) | data formatting | bytes 1990656 | tf_op jit(solution)/shard_map/convert_element_type | solution.py:50
  219.5 5.5 %reshape.625 = bf16[2,2,6,3,12,3,6,32]{7,6,5,4,3,2,1,0:T(8,128)(2,1)} reshape(bf16[864,576]{1,0:T(8,128)(2,1)S(1)} %copy.189) | data formatting | bytes 1990656 | tf_op jit(solution)/shard_map/reshape | solution.py:51
  225.0 3.6 fusion.495
  228.6 1.4 copy.190
  230.0 1.4 copy.191
  231.4 1.4 copy.197
  232.8 0.9 fusion.41
  233.9 1.8 fusion.505
  236.4 2.8 copy.200
  239.2 1.9 copy.201
  241.1 1.9 reshape.627
  243.1 1.2 slice.268
  245.3 5.4 %fusion.54 = bf16[576,192]{0,1:T(8,128)(2,1)S(1)} fusion(bf16[576,192]{0,1:T(8,128)(2,1)S(1)} %add_convert_fusion.1, bf16[2,768,192]{1,2,0:T(8,128)(2,1)S(1)} %copy-done.33, bf16[2,192,768]{2,1,0:T(8,128)(2,1)} %param.32, f32[192]{0:T(256)S(1)} %bitcast.206, f32[576]{0:T(1024)S(1)} %add_rsqrt_fusion.5, f32[576]{0:T(1024)S(1)} %broadcast_multiply_fusion.6), kind=kOutput, calls=%fused_computation.97 | convolution fusion | flops 369377280 | bytes 1311744 | tf_op jit(solution)/shard_map/dot_general | solution.py:93
  251.6 39.1 %gather_fusion.2 = f32[20736,12]{1,0:T(8,128)} fusion(f32[12,3312]{0,1:T(8,128)S(1)} %bitcast.165, s32[21504]{0:T(1024)S(1)} %pad_clamp_fusion), kind=kCustom, calls=%fused_computation.1.clone | custom fusion | bytes 2073600 | tf_op jit(solution)/shard_map/jit(_take)/gather | solution.py:191
  290.6 11.6 %copy.213 = f32[144,144,12]{0,1,2:T(8,128)S(1)} copy(f32[144,144,12]{2,1,0:T(8,128)} %bitcast.170) | data formatting | bytes 1990656 | tf_op jit(solution)/shard_map/jit(_take)/gather | solution.py:191
  303.6 1.0 maximum_convert_fusion
  307.0 1.0 convolution_convert_fusion.5
  308.4 1.6 convolution_convert_fusion.1
  310.0 2.3 reshape.630
  312.3 1.8 fusion.498
  314.6 1.2 copy-done.1
  316.2 2.6 convolution_convert_fusion.4
  320.5 4.1 %fusion.80 = bf16[144,384]{1,0:T(8,128)(2,1)S(1)} fusion(bf16[2,1536,384]{2,1,0:T(8,128)(2,1)} %param.41, bf16[2,384,1536]{2,1,0:T(8,128)(2,1)} %param.40, bf16[144,384]{1,0:T(8,128)(2,1)S(1)} %fusion.76, f32[384]{0:T(512)S(1)} %copy-done.28, f32[144]{0:T(256)S(1)} %add_rsqrt_fusion.8, f32[144]{0:T(256)S(1)} %broadcast_multiply_fusion.9), kind=kOutput, calls=%fused_computation.119 | convolution fusion | flops 354557952 | bytes 2695168 | tf_op jit(solution)/shard_map/dot_general | solution.py:93
  324.7 4.7 %collective-permute-start.4 = (bf16[2,3,12,384]{3,2,1,0:T(8,128)(2,1)S(1)}, bf16[2,3,12,384]{3,2,1,0:T(8,128)(2,1)S(1)}, u32[]{:S(2)}, u32[]{:S(2)}) collective-permute-start(bf16[2,3,12,384]{3,2,1,0:T(8,128)(2,1)S(1)} %get-tuple-element.34), channel_id=1, source_target_pairs={{0,14},{2,0},{4,2},{6,4},{8,6},{10,8},{12,10},{14,12},{1,15},{3,1}... | collective-permute-start | bytes 165896 | tf_op jit(solution)/shard_map/ppermute | solution.py:32
  329.6 1.9 collective-permute-done.4
  331.6 1.9 collective-permute-start.6
  333.5 1.8 collective-permute-done.5
  335.3 1.6 collective-permute-done.6
  337.5 1.7 convolution_convert_fusion
  339.2 3.9 %reshape.636 = bf16[2,1,6,2,12,3,12,32]{7,6,5,4,3,2,0,1:T(8,128)(2,1)} reshape(bf16[288,1152]{1,0:T(8,128)(2,1)S(1)} %convolution_convert_fusion) | data formatting | bytes 1327104 | tf_op jit(solution)/shard_map/reshape | solution.py:51
  343.1 2.8 fusion.496
  345.9 1.8 copy.219
  347.7 1.8 copy.220
  349.6 1.9 copy.226
  351.4 4.7 %fusion.507 = (f32[2,12,144]{2,1,0:T(8,128)S(1)}, f32[2,12,144,144]{2,3,1,0:T(8,128)}) fusion(f32[12,144,144]{1,2,0:T(8,128)S(1)} %copy-done.8, pred[144,144]{0,1:T(8,128)(4,1)S(1)} %broadcast_compare_fusion.1, bf16[2,12,144,32]{3,0,2,1:T(2,128)(2,1)} %bitcast.200, bf16[2,12,144,32]{3,0,2,1:T(2,128)(2,1)} %bitcast.199), kind=kOutput, calls=%fused_computation.588 | convolution fusion | flops 34338960 | bytes 3462912 | tf_op jit(solution)/shard_map/sub | solution.py:67
  356.1 2.8 fusion.47
  361.5 4.2 %fusion.77 = bf16[144,384]{1,0:T(8,128)(2,1)S(1)} fusion(bf16[2,1536,384]{2,1,0:T(8,128)(2,1)} %param.41, bf16[2,384,1536]{2,1,0:T(8,128)(2,1)} %param.40, bf16[144,384]{1,0:T(8,128)(2,1)S(1)} %add_convert_fusion.2, f32[384]{0:T(512)S(1)} %copy-done.27, f32[144]{0:T(256)S(1)} %add_rsqrt_fusion.7, f32[144]{0:T(256)S(1)} %broadcast_multiply_fusion.8), kind=kOutput, calls=%fused_computation.118 | convolution fusion | flops 354557952 | bytes 2695168 | tf_op jit(solution)/shard_map/dot_general | solution.py:93
  366.2 7.3 %collective-permute-done.7 = bf16[2,3,12,384]{3,2,1,0:T(8,128)(2,1)S(1)} collective-permute-done((bf16[2,3,12,384]{3,2,1,0:T(8,128)(2,1)S(1)}, bf16[2,3,12,384]{3,2,1,0:T(8,128)(2,1)S(1)}, u32[]{:S(2)}, u32[]{:S(2)}) %collective-permute-start.7) | collective-permute-done | bytes 55328 | tf_op jit(solution)/shard_map/ppermute | solution.py:32
  375.6 1.8 fusion.189
  (190 shorter events, 28.4 us)
Async XLA Ops:
  0.0 307.0 %copy-start = (bf16[768,384]{1,0:T(8,128)(2,1)S(1)}, bf16[768,384]{1,0:T(8,128)(2,1)}, u32[]{:S(2)}) copy-start(bf16[768,384]{1,0:T(8,128)(2,1)} %param.35) | copy-start | bytes 1769476
  0.0 5.6 %copy-start.26 = (f32[2,2,192]{2,1,0:T(2,128)S(1)}, f32[2,2,192]{2,1,0:T(2,128)}, u32[]{:S(2)}) copy-start(f32[2,2,192]{2,1,0:T(2,128)} %param.29) | copy-start | bytes 9220
  0.0 6.4 %copy-start.16 = (bf16[2,192,576]{2,1,0:T(8,128)(2,1)S(1)}, bf16[2,192,576]{2,1,0:T(8,128)(2,1)}, u32[]{:S(2)}) copy-start(bf16[2,192,576]{2,1,0:T(8,128)(2,1)} %param.30) | copy-start | bytes 1327108
  14.7 3.4 copy-start.21
  109.8 12.2 %copy-start.22 = (pred[144,144]{1,0:T(8,128)(4,1)S(1)}, pred[144,144]{1,0:T(8,128)(4,1)}, u32[]{:S(2)}) copy-start(pred[144,144]{1,0:T(8,128)(4,1)} %compare_and_fusion) | copy-start | bytes 62212
  109.8 12.4 %copy-start.2 = (bf16[1,2,2,6,2,6,12,32]{7,3,0,6,2,5,1,4:T(8,128)(2,1)S(1)}, bf16[1,2,2,6,2,6,12,32]{7,3,0,6,2,5,1,4:T(8,128)(2,1)}, u32[]{:S(2)}) copy-start(bf16[1,2,2,6,2,6,12,32]{7,3,0,6,2,5,1,4:T(8,128)(2,1)} %get-tuple-element.17) | copy-start | bytes 663556
  122.2 2.1 copy-start.13
  122.2 1.2 copy-start.4
  122.2 1.4 copy-start.5
  123.7 1.2 copy-start.3
  128.8 1.3 copy-start.19
  129.2 1.3 copy-start.30
  129.2 1.3 copy-start.32
  130.6 12.0 %copy-start.18 = (f32[2,12,3312]{2,0,1:T(2,128)S(1)}, f32[2,12,3312]{2,0,1:T(2,128)}, u32[]{:S(2)}) copy-start(f32[2,12,3312]{2,0,1:T(2,128)} %param.36) | copy-start | bytes 953860
  136.3 59.5 %collective-permute-start = (bf16[2,3,24,192]{3,2,1,0:T(8,128)(2,1)S(1)}, bf16[2,3,24,192]{3,2,1,0:T(8,128)(2,1)S(1)}, u32[]{:S(2)}, u32[]{:S(2)}) collective-permute-start(bf16[2,3,24,192]{3,2,1,0:T(8,128)(2,1)S(1)} %slice.260), channel_id=1, source_target_pairs={{0,14},{2,0},{4,2},{6,4},{8,6},{10,8},{12,10},{14,12},{1,15},{3,1}... | collective-permute-start | bytes 165896 | tf_op jit(solution)/shard_map/ppermute | solution.py:32
  182.1 11.6 %copy-start.14 = (pred[144,144]{0,1:T(8,128)(4,1)S(1)}, pred[144,144]{0,1:T(8,128)(4,1)}, u32[]{:S(2)}) copy-start(pred[144,144]{0,1:T(8,128)(4,1)} %copy-done.13) | copy-start | bytes 62212
  193.7 1.4 copy-start.25
  196.4 5.3 %collective-permute-start.1 = (bf16[2,12,6,192]{3,2,1,0:T(8,128)(2,1)}, bf16[2,12,6,192]{3,2,1,0:T(8,128)(2,1)S(1)}, u32[]{:S(2)}, u32[]{:S(2)}) collective-permute-start(bf16[2,12,6,192]{3,2,1,0:T(8,128)(2,1)} %get-tuple-element.25), channel_id=1, source_target_pairs={{0,1},{1,16},{16,17},{17,0},{2,3},{3,18},{18,19},{19,2},{4,5},{5,2... | collective-permute-start | bytes 165896 | tf_op jit(solution)/shard_map/ppermute | solution.py:20
  197.9 5.9 %collective-permute-start.2 = (bf16[2,12,6,192]{3,2,1,0:T(8,128)(2,1)S(1)}, bf16[2,12,6,192]{3,2,1,0:T(8,128)(2,1)S(1)}, u32[]{:S(2)}, u32[]{:S(2)}) collective-permute-start(bf16[2,12,6,192]{3,2,1,0:T(8,128)(2,1)S(1)} %get-tuple-element.26), channel_id=1, source_target_pairs={{1,0},{16,1},{17,16},{0,17},{3,2},{18,3},{19,18},{2,19},{5,4},{20,... | collective-permute-start | bytes 165896 | tf_op jit(solution)/shard_map/ppermute | solution.py:22
  198.5 6.6 %copy-start.17 = (bf16[2,192,576]{2,1,0:T(8,128)(2,1)S(1)}, bf16[2,192,576]{2,1,0:T(8,128)(2,1)}, u32[]{:S(2)}) copy-start(bf16[2,192,576]{2,1,0:T(8,128)(2,1)} %param.30) | copy-start | bytes 1327108
  232.8 1.2 copy-start.9
  241.1 3.2 copy-start.20
  243.1 1.8 copy-start.29
  244.3 1.1 copy-start.33
  250.9 52.0 %collective-permute-start.3 = (bf16[2,3,24,192]{3,2,1,0:T(8,128)(2,1)S(1)}, bf16[2,3,24,192]{3,2,1,0:T(8,128)(2,1)}, u32[]{:S(2)}, u32[]{:S(2)}) collective-permute-start(bf16[2,3,24,192]{3,2,1,0:T(8,128)(2,1)S(1)} %slice.269), channel_id=1, source_target_pairs={{0,2},{2,4},{4,6},{6,8},{8,10},{10,12},{12,14},{14,0},{1,3},{3,5},... | collective-permute-start | bytes 165896 | tf_op jit(solution)/shard_map/ppermute | solution.py:32
  302.9 0.7 copy-start.6
  312.3 1.8 copy-start.15
  314.6 1.2 copy-start.1
  318.8 1.1 copy-start.10
  319.0 1.4 copy-start.28
  320.5 9.0 %copy-start.23 = (s32[144]{0:T(256)S(1)}, s32[144]{0:T(256)}, u32[]{:S(2)}) copy-start(s32[144]{0:T(256)} %eq.44) | copy-start | bytes 1732
  324.7 12.7 %copy-start.24 = (f32[384]{0:T(512)S(1)}, f32[384]{0:T(512)}, u32[]{:S(2)}) copy-start(f32[384]{0:T(512)} %get-tuple-element.10) | copy-start | bytes 4612
  324.7 6.7 %collective-permute-start.4 = (bf16[2,3,12,384]{3,2,1,0:T(8,128)(2,1)S(1)}, bf16[2,3,12,384]{3,2,1,0:T(8,128)(2,1)S(1)}, u32[]{:S(2)}, u32[]{:S(2)}) collective-permute-start(bf16[2,3,12,384]{3,2,1,0:T(8,128)(2,1)S(1)} %get-tuple-element.34), channel_id=1, source_target_pairs={{0,14},{2,0},{4,2},{6,4},{8,6},{10,8},{12,10},{14,12},{1,15},{3,1}... | collective-permute-start | bytes 165896 | tf_op jit(solution)/shard_map/ppermute | solution.py:32
  331.5 3.8 %collective-permute-start.5 = (bf16[2,6,6,384]{3,2,1,0:T(8,128)(2,1)S(1)}, bf16[2,6,6,384]{3,2,1,0:T(8,128)(2,1)S(1)}, u32[]{:S(2)}, u32[]{:S(2)}) collective-permute-start(bf16[2,6,6,384]{3,2,1,0:T(8,128)(2,1)S(1)} %get-tuple-element.31), channel_id=1, source_target_pairs={{0,1},{1,16},{16,17},{17,0},{2,3},{3,18},{18,19},{19,2},{4,5},{5,2... | collective-permute-start | bytes 165896 | tf_op jit(solution)/shard_map/ppermute | solution.py:20
  331.6 5.3 %collective-permute-start.6 = (bf16[2,6,6,384]{3,2,1,0:T(8,128)(2,1)S(1)}, bf16[2,6,6,384]{3,2,1,0:T(8,128)(2,1)S(1)}, u32[]{:S(2)}, u32[]{:S(2)}) collective-permute-start(bf16[2,6,6,384]{3,2,1,0:T(8,128)(2,1)S(1)} %get-tuple-element.32), channel_id=1, source_target_pairs={{1,0},{16,1},{17,16},{0,17},{3,2},{18,3},{19,18},{2,19},{5,4},{20,... | collective-permute-start | bytes 165896 | tf_op jit(solution)/shard_map/ppermute | solution.py:22
  347.7 3.7 copy-start.8
  359.6 1.3 copy-start.11
  360.0 1.5 copy-start.27
  361.5 4.4 %copy-start.12 = (bf16[384,768]{1,0:T(8,128)(2,1)S(1)}, bf16[384,768]{1,0:T(8,128)(2,1)}, u32[]{:S(2)}) copy-start(bf16[384,768]{1,0:T(8,128)(2,1)} %param.42) | copy-start | bytes 1769476
  365.8 7.7 %collective-permute-start.7 = (bf16[2,3,12,384]{3,2,1,0:T(8,128)(2,1)S(1)}, bf16[2,3,12,384]{3,2,1,0:T(8,128)(2,1)S(1)}, u32[]{:S(2)}, u32[]{:S(2)}) collective-permute-start(bf16[2,3,12,384]{3,2,1,0:T(8,128)(2,1)S(1)} %get-tuple-element.29), channel_id=1, source_target_pairs={{0,2},{2,4},{4,6},{6,8},{8,10},{10,12},{12,14},{14,0},{1,3},{3,5},... | collective-permute-start | bytes 165896 | tf_op jit(solution)/shard_map/ppermute | solution.py:32
  373.9 1.7 copy-start.7
  373.9 1.7 copy-start.31
where the time goes:
time: 381 us; the launch traced here: 378 us
  local copies, waits for them, and re-layouts  283 us (74%)
  matrix products  40.2 us (11%)
  other arithmetic  20.2 us (5%)
  waiting for transfers between devices  17.9 us (5%)
  starting transfers between devices  14.6 us (4%)
    gather x4, local copies, waits for them, and re-layouts, on_device(): position_bias = jnp.take(fine_bias[block_number], bias_index, axis=1)  101 us
    gather x4, local copies, waits for them, and re-layouts, on_device(): position_bias = jnp.take(coarse_bias[block_number], bias_index, axis=1)  101 us
    dot_general x4, matrix products, finish(): jnp.dot(hidden, w_narrow, preferred_element_type=jnp.float32)  19.2 us
    slice x7, local copies, waits for them, and re-layouts, attend(): triple[2]  16.1 us
    reshape x4, local copies, waits for them, and re-layouts, attend(): triple.reshape(level_count, lat_windows, WIN_LAT, lon_windows, WIN_LON, 3...  15.7 us
    convert_element_type x1, local copies, waits for them, and re-layouts, attend(): triple = jnp.dot(normed.reshape(-1, channels), w_triple, preferred_elemen...  12.8 us
    ppermute x4, starting transfers between devices, shifted_2(): return lax.ppermute(value, axis, pairs)  10.9 us
    ppermute x4, waiting for transfers between devices, shifted_2(): return lax.ppermute(value, axis, pairs)  9.16 us
  transfers between devices with their start and end apart: 8, of which 6 were waited for; matrix products, arithmetic and copies ran while one was open for 28% of the time, Pallas kernels for 0%

commit v1 on v0

v1 whole, which is shorter than its diff:
```python
import functools

import jax
import jax.numpy as jnp
import numpy as np
from jax import lax
from jax.experimental import pallas as pl
from jax.experimental.pallas import tpu as pltpu
from jax.sharding import PartitionSpec as P

HF = 6
HC = 12
HEAD = 32
WIN_LAT = 6
WIN_LON = 12
WIN_TOK = 144
HALF_LAT = WIN_LAT // 2
HALF_LON = WIN_LON // 2
LEVELS = 2
QUAD = LEVELS * HALF_LAT * HALF_LON
QP = 40
WP = 4 * QP
LO_COUNT = 13
LOG2E = 1.4426950408889634
MASKED = -1e30
LON = ("sec", "head")
F32 = jnp.float32
BF16 = jnp.bfloat16


def quad_sources(row_count, col_count):
    slots = []
    for a in range(row_count // HALF_LAT):
        for b in range(col_count // HALF_LON):
            for s in range(QP):
                if s >= QUAD:
                    slots.append(None)
                    continue
                level, rest = divmod(s, HALF_LAT * HALF_LON)
                r, c = divmod(rest, HALF_LON)
                slots.append((level, a * HALF_LAT + r, b * HALF_LON + c))
    return slots


def one_hot(sources, width):
    table = np.zeros((len(sources), width), np.float32)
    for slot, source in enumerate(sources):
        if source is not None:
            table[slot, source] = 1.0
    return jnp.asarray(table.astype(jnp.bfloat16))


def fine_tables(rows, cols):
    slots = quad_sources(rows, cols)
    order = one_hot(
        [None if s is None else (s[0] * rows + s[1]) * cols + s[2] for s in slots],
        LEVELS * rows * cols,
    )
    of_row = one_hot([None if s is None else s[1] for s in slots], rows)
    of_col = one_hot([None if s is None else s[2] for s in slots], cols)
    return order, of_row, of_col


def merge_table(rows, cols):
    place = {s: n for n, s in enumerate(quad_sources(rows, cols)) if s is not None}
    sources = []
    for p in range(2):
        for q in range(2):
            for s in quad_sources(rows // 2, cols // 2):
                sources.append(
                    None if s is None else place[(s[0], 2 * s[1] + p, 2 * s[2] + q)]
                )
    return one_hot(sources, len(place) // QUAD * QP)


def expand_table(rows, cols):
    coarse = quad_sources(rows // 2, cols // 2)
    place = {s: n for n, s in enumerate(coarse) if s is not None}
    sources = []
    for level in range(LEVELS):
        for r in range(rows):
            for c in range(cols):
                part = (r % 2) * 2 + c % 2
                sources.append(part * len(coarse) + place[(level, r // 2, c // 2)])
    return one_hot(sources, 4 * len(coarse))


def dot(a, b):
    return jnp.dot(a, b, preferred_element_type=F32)


def dot_t(a, b):
    return lax.dot_general(a, b, (((1,), (1,)), ((), ())), preferred_element_type=F32)


def norm(x, gain):
    mean = jnp.mean(x, axis=-1, keepdims=True)
    centered = x - mean
    variance = jnp.mean(centered * centered, axis=-1, keepdims=True)
    return centered * lax.rsqrt(variance + 1e-05) * gain


def attend(q, k, v, bias_ref, first, heads, key_mask):
    n = q.shape[0]
    channels = q.shape[1]
    scale = HEAD**-0.5 * LOG2E
    outs = []
    for tile in range(0, channels, 128):
        width = min(128, channels - tile)
        count = width // HEAD
        qt = q[:, tile : tile + width]
        lane = lax.broadcasted_iota(jnp.int32, (n, width), 1) // HEAD
        masks = [lane == h for h in range(count)]
        stack = jnp.concatenate([jnp.where(m, qt, jnp.zeros_like(qt)) for m in masks], axis=0)
        scores = dot_t(stack, k[:, tile : tile + width])
        probs = []
        for h in range(count):
            head = tile // HEAD + h
            s = scores[h * n : (h + 1) * n] * scale + bias_ref[pl.ds(head * WP + first, n), :]
            if key_mask is not None:
                s = s + key_mask
            s = s - jnp.max(s, axis=-1, keepdims=True)
            probs.append(jnp.exp2(s).astype(BF16))
        probs = jnp.concatenate(probs, axis=0)
        vt = v[:, tile : tile + width]
        mixed = dot(probs, jnp.concatenate([vt, jnp.ones((WP, width), BF16)], axis=1))
        top = mixed[:n, :width]
        total = mixed[:n, width:]
        for h in range(1, count):
            top = jnp.where(masks[h], mixed[h * n : (h + 1) * n, :width], top)
            total = jnp.where(masks[h], mixed[h * n : (h + 1) * n, width:], total)
        outs.append(top / total)
    return outs[0] if len(outs) == 1 else jnp.concatenate(outs, axis=1)


def gelu(x):
    return 0.5 * x * (1.0 + lax.erf(x * np.float32(0.5**0.5)))


def finish(x, context, gain, w_project, w_widen, w_narrow):
    middle = (x + dot(context, w_project)).astype(BF16).astype(F32)
    second = norm(middle, gain).astype(BF16)
    hidden = gelu(dot(second, w_widen)).astype(BF16)
    return (middle + dot(hidden, w_narrow)).astype(BF16)


def bias_kernel(index_ref, spread_ref, table_ref, out_ref, table, index, *, heads, head_rows):
    spread = spread_ref[...]
    plain = index_ref[...]
    high = (plain >> 4).astype(F32).astype(BF16)
    low = (plain & 15).astype(F32).astype(BF16)

    def moved(part):
        return dot_t(dot(spread, part).astype(BF16), spread).astype(jnp.int32)

    spot = lax.broadcasted_iota(jnp.int32, (WP, WP), 1) % QP
    bias_len = table_ref.shape[-1]
    index[...] = jnp.where(spot < QUAD, moved(high) * 16 + moved(low), bias_len)

    wide = jnp.full((head_rows, LO_COUNT * 256), MASKED, F32)
    table[...] = wide
    table[:heads, :bias_len] = table_ref[...] * LOG2E
    values = table[...]
    big = values.astype(BF16)
    small = (values - big.astype(F32)).astype(BF16)
    left = jnp.concatenate(
        [p[:, i * 256 : (i + 1) * 256] for p in (big, small) for i in range(LO_COUNT)], axis=0
    )
    half = LO_COUNT * head_rows
    ladder = lax.broadcasted_iota(jnp.int32, (256, WP), 0).astype(F32).astype(BF16)

    def one(row, carry):
        entry = index[pl.ds(row, 1), :]
        near = (entry & 255).astype(F32).astype(BF16)
        picks = jnp.where(ladder == near, jnp.ones((), BF16), jnp.zeros((), BF16))
        both = dot(left, picks)
        far = entry >> 8
        total = jnp.zeros((head_rows, WP), F32)
        for i in range(LO_COUNT):
            at = i * head_rows
            total = jnp.where(
                far == i,
                both[at : at + head_rows] + both[half + at : half + at + head_rows],
                total,
            )
        for h in range(heads):
            out_ref[pl.ds(h * WP + row, 1), :] = total[h : h + 1]
        return carry

    lax.fori_loop(0, WP, one, 0, unroll=4)


def bias_of(tables, block, index, spread):
    heads = tables.shape[1]
    head_rows = -(-heads // 8) * 8
    flops = 2 * WP * 256 * WP * LO_COUNT * head_rows * 2
    return pl.pallas_call(
        functools.partial(bias_kernel, heads=heads, head_rows=head_rows),
        out_shape=jax.ShapeDtypeStruct((heads * WP, WP), F32),
        grid=(1,),
        in_specs=[
            pl.BlockSpec(memory_space=pltpu.VMEM),
            pl.BlockSpec(memory_space=pltpu.VMEM),
            pl.BlockSpec((None,) + tables.shape[1:], lambda _: (block, 0, 0)),
        ],
        out_specs=pl.BlockSpec(memory_space=pltpu.VMEM),
        scratch_shapes=[
            pltpu.VMEM((head_rows, LO_COUNT * 256), F32),
            pltpu.VMEM((WP, WP), jnp.int32),
        ],
        cost_estimate=pl.CostEstimate(flops=4 * flops, bytes_accessed=1 << 20, transcendentals=0),
        name="bias_table",
    )(index, spread, tables)


def first_kernel(
    fields_ref, land_ref, embed_ref, order_ref, of_row_ref, of_col_ref, bias_ref,
    gains_ref, w_triple_ref, w_project_ref, w_widen_ref, w_narrow_ref, out_ref, start_ref,
):
    channels = fields_ref.shape[1]
    land = land_ref[...].astype(F32).astype(BF16)
    on_row = dot(of_row_ref[...], land)
    on_land = jnp.sum(on_row * of_col_ref[...].astype(F32), axis=-1, keepdims=True)
    start = dot(order_ref[...], fields_ref[...]) + on_land * embed_ref[...]
    start_ref[...] = start.astype(BF16).astype(F32)
    rows = out_ref.shape[0]
    windows_down = 2
    pairs = rows // (QP * 4) // windows_down
    for a in range(windows_down):
        for b in range(pairs):
            top = (2 * a * 2 * pairs + 2 * b) * QP
            below = ((2 * a + 1) * 2 * pairs + 2 * b) * QP
            x = jnp.concatenate(
                [start_ref[top : top + 2 * QP], start_ref[below : below + 2 * QP]], axis=0
            )
            normed = norm(x, gains_ref[0:1]).astype(BF16)
            triple = dot(normed, w_triple_ref[...]).astype(BF16)
            context = attend(
                triple[:, :channels],
                triple[:, channels : 2 * channels],
                triple[:, 2 * channels :],
                bias_ref, 0, channels // HEAD, None,
            ).astype(BF16)
            done = finish(
                x, context, gains_ref[1:2], w_project_ref[...], w_widen_ref[...], w_narrow_ref[...]
            )
            out_ref[top : top + 2 * QP] = done[: 2 * QP]
            out_ref[below : below + 2 * QP] = done[2 * QP :]


def shifted_block(
    own_ref, north_ref, south_ref, west_ref, east_ref, edge_ref, bias_ref, gains_ref,
    w_triple_ref, w_project_ref, w_widen_ref, w_narrow_ref, query, key, value, context,
):
    channels = own_ref.shape[1]
    heads = channels // HEAD
    across = north_ref.shape[0] // QP
    down = own_ref.shape[0] // QP // across
    line = (across + 2) * QP
    inner = across * QP
    for i in range(down + 2):
        if i == 0:
            middle = north_ref[...]
        elif i == down + 1:
            middle = south_ref[...]
        else:
            middle = own_ref[(i - 1) * inner : i * inner]
        x = jnp.concatenate(
            [
                west_ref[i * QP : (i + 1) * QP].astype(F32),
                middle.astype(F32),
                east_ref[i * QP : (i + 1) * QP].astype(F32),
            ],
            axis=0,
        )
        normed = norm(x, gains_ref[0:1]).astype(BF16)
        triple = dot(normed, w_triple_ref[...])
        if 0 < i < down + 1:
            query[(i - 1) * line : i * line] = triple[:, :channels]
        key[i * line : (i + 1) * line] = triple[:, channels : 2 * channels].astype(BF16)
        value[i * line : (i + 1) * line] = triple[:, 2 * channels :].astype(BF16)
    lane = lax.broadcasted_iota(jnp.int32, (1, WP), 1)
    on_top = edge_ref[0]
    on_bottom = edge_ref[1]
    for wa in range(down // 2 + 1):
        mask = None
        if wa == 0:
            mask = jnp.where(lane < 2 * QP, on_top, 0.0)
        elif wa == down // 2:
            mask = jnp.where(lane < 2 * QP, 0.0, on_bottom)
        for wb in range(across // 2 + 1):
            at = [(2 * wa + r) * line + 2 * wb * QP for r in range(2)]
            k = jnp.concatenate([key[s : s + 2 * QP] for s in at], axis=0)
            v = jnp.concatenate([value[s : s + 2 * QP] for s in at], axis=0)
            rows = [r for r in range(2) if 0 < 2 * wa + r < down + 1]
            cols = [c for c in range(2) if 0 < 2 * wb + c < across + 1]
            size = len(cols) * QP
            qs = [
                query[
                    (2 * wa + r - 1) * line + (2 * wb + cols[0]) * QP :
                    (2 * wa + r - 1) * line + (2 * wb + cols[0]) * QP + size
                ]
                for r in rows
            ]
            if len(cols) == 2:
                groups = [(rows, jnp.concatenate(qs, axis=0) if len(qs) == 2 else qs[0])]
            else:
                groups = [([r], part) for r, part in zip(rows, qs)]
            for group, q in groups:
                out = attend(
                    q.astype(BF16), k, v, bias_ref, (2 * group[0] + cols[0]) * QP, heads, mask
                )
                for n, r in enumerate(group):
                    to = ((2 * wa + r - 1) * across + 2 * wb + cols[0] - 1) * QP
                    context[to : to + size] = out[n * size : (n + 1) * size]
    outs = []
    for at in range(0, own_ref.shape[0], WP):
        outs.append(
            finish(
                own_ref[at : at + WP].astype(F32),
                context[at : at + WP].astype(BF16),
                gains_ref[1:2],
                w_project_ref[...], w_widen_ref[...], w_narrow_ref[...],
            )
        )
    return outs


def middle_kernel(
    own_ref, north_ref, south_ref, west_ref, east_ref, edge_ref, bias_ref, gains_ref,
    w_triple_ref, w_project_ref, w_widen_ref, w_narrow_ref,
    merge_order_ref, merge_gain_ref, merge_weight_ref,
    coarse_bias_ref, coarse_gains_ref, c_triple_ref, c_project_ref, c_widen_ref, c_narrow_ref,
    parts_ref, coarse_ref, query, key, value, context,
):
    outs = shifted_block(
        own_ref, north_ref, south_ref, west_ref, east_ref, edge_ref, bias_ref, gains_ref,
        w_triple_ref, w_project_ref, w_widen_ref, w_narrow_ref, query, key, value, context,
    )
    channels = own_ref.shape[1]
    skip = jnp.concatenate(outs, axis=0)
    grouped = dot(merge_order_ref[...], skip)
    parts_ref[...] = grouped.astype(BF16)
    parts = [grouped[i * WP : (i + 1) * WP] for i in range(4)]
    width = 4 * channels
    mean = sum(jnp.sum(p, axis=-1, keepdims=True) for p in parts) / width
    parts = [p - mean for p in parts]
    variance = sum(jnp.sum(p * p, axis=-1, keepdims=True) for p in parts) / width
    factor = lax.rsqrt(variance + 1e-05)
    coarse = jnp.zeros((WP, merge_weight_ref.shape[1]), F32)
    for i, p in enumerate(parts):
        merged = (p * factor * merge_gain_ref[i : i + 1]).astype(BF16)
        coarse = coarse + dot(merged, merge_weight_ref[i * channels : (i + 1) * channels])
    x = coarse.astype(BF16).astype(F32)
    wide = x.shape[1]
    normed = norm(x, coarse_gains_ref[0:1]).astype(BF16)
    triple = dot(normed, c_triple_ref[...]).astype(BF16)
    mixed = attend(
        triple[:, :wide], triple[:, wide : 2 * wide], triple[:, 2 * wide :],
        coarse_bias_ref, 0, wide // HEAD, None,
    ).astype(BF16)
    coarse_ref[...] = finish(
        x, mixed, coarse_gains_ref[1:2], c_project_ref[...], c_widen_ref[...], c_narrow_ref[...]
    )


def last_kernel(
    own_ref, north_ref, south_ref, west_ref, east_ref, edge_ref, bias_ref, gains_ref,
    w_triple_ref, w_project_ref, w_widen_ref, w_narrow_ref,
    parts_ref, expand_weight_ref, expand_gain_ref, expand_order_ref,
    out_ref, query, key, value, context,
):
    (deep,) = shifted_block(
        own_ref, north_ref, south_ref, west_ref, east_ref, edge_ref, bias_ref, gains_ref,
        w_triple_ref, w_project_ref, w_widen_ref, w_narrow_ref, query, key, value, context,
    )
    channels = parts_ref.shape[1]
    widened = dot(deep, expand_weight_ref[...])
    outs = []
    for i in range(4):
        shuffled = widened[:, i * channels : (i + 1) * channels]
        skip = parts_ref[i * WP : (i + 1) * WP].astype(F32)
        outs.append((skip + norm(shuffled, expand_gain_ref[...])).astype(BF16))
    out_ref[...] = dot(expand_order_ref[...], jnp.concatenate(outs, axis=0)).astype(BF16)


WHOLE = pl.BlockSpec(memory_space=pltpu.VMEM)


def block_spec(array, block):
    return pl.BlockSpec((None,) + array.shape[1:], lambda _: (block,) + (0,) * (array.ndim - 1))


def halo(own):
    rows, cols, _, channels = own.shape
    lat = lax.axis_size("lat")
    lon = lax.axis_size(LON)
    down = [(i, (i + 1) % lat) for i in range(lat)]
    up = [((i + 1) % lat, i) for i in range(lat)]
    east = [(i, (i + 1) % lon) for i in range(lon)]
    west = [((i + 1) % lon, i) for i in range(lon)]
    north = lax.ppermute(own[rows - 1], "lat", down)
    south = lax.ppermute(own[0], "lat", up)

    def side(c):
        return jnp.concatenate([north[c : c + 1], own[:, c], south[c : c + 1]], axis=0)

    from_west = lax.ppermute(side(cols - 1), LON, east)
    from_east = lax.ppermute(side(0), LON, west)
    return [v.reshape(-1, channels) for v in (own, north, south, from_west, from_east)]


def shifted_scratch(rows, cols, channels):
    line = (cols + 2) * QP
    return [
        pltpu.VMEM((rows * line, channels), F32),
        pltpu.VMEM(((rows + 2) * line, channels), BF16),
        pltpu.VMEM(((rows + 2) * line, channels), BF16),
        pltpu.VMEM((rows * cols * QP, channels), F32),
    ]


def on_device(
    fields, land_sea, land_embed, bias_index, fine_bias, fine_gains, fine_query_key_value,
    fine_project, fine_widen, fine_narrow, merge_gain, merge_weight, coarse_bias, coarse_gains,
    coarse_query_key_value, coarse_project, coarse_widen, coarse_narrow, expand_weight, expand_gain,
):
    _, rows, cols, channels = fields.shape
    quad_rows, quad_cols = rows // HALF_LAT, cols // HALF_LON
    tokens = quad_rows * quad_cols * QP
    wide = merge_weight.shape[1]
    spread = one_hot(
        [None if s is None else (s[0] * WIN_LAT + s[1]) * WIN_LON + s[2]
         for s in quad_sources(WIN_LAT, WIN_LON)],
        WIN_TOK,
    )
    order, of_row, of_col = fine_tables(rows, cols)
    fine = [bias_of(fine_bias, n, bias_index, spread) for n in range(2)]
    deep = [bias_of(coarse_bias, n, bias_index, spread) for n in range(2)]
    fine_weights = (fine_gains, fine_query_key_value, fine_project, fine_widen, fine_narrow)
    coarse_weights = (
        coarse_gains, coarse_query_key_value, coarse_project, coarse_widen, coarse_narrow
    )
    params = pltpu.CompilerParams(vmem_limit_bytes=48 << 20)

    first = pl.pallas_call(
        first_kernel,
        out_shape=jax.ShapeDtypeStruct((tokens, channels), BF16),
        grid=(1,),
        in_specs=[WHOLE] * 7 + [block_spec(w, 0) for w in fine_weights],
        out_specs=WHOLE,
        scratch_shapes=[pltpu.VMEM((tokens, channels), F32)],
        compiler_params=params,
        name="fine_plain",
    )(
        fields.reshape(-1, channels), land_sea, land_embed[None], order, of_row, of_col, fine[0],
        *fine_weights,
    )

    place = lax.axis_index("lat")
    edge = jnp.stack(
        [
            jnp.where(place == 0, MASKED, 0.0),
            jnp.where(place == lax.axis_size("lat") - 1, MASKED, 0.0),
        ]
    ).astype(F32)
    smem = pl.BlockSpec(memory_space=pltpu.SMEM)

    parts, coarse = pl.pallas_call(
        middle_kernel,
        out_shape=[
            jax.ShapeDtypeStruct((tokens, channels), BF16),
            jax.ShapeDtypeStruct((tokens // 4, wide), BF16),
        ],
        grid=(1,),
        in_specs=[WHOLE] * 5 + [smem, WHOLE] + [block_spec(w, 1) for w in fine_weights]
        + [WHOLE] * 4 + [block_spec(w, 0) for w in coarse_weights],
        out_specs=[WHOLE] * 2,
        scratch_shapes=shifted_scratch(quad_rows, quad_cols, channels),
        compiler_params=params,
        name="fine_shifted_coarse_plain",
    )(
        *halo(first.reshape(quad_rows, quad_cols, QP, channels)), edge, fine[1], *fine_weights,
        merge_table(rows, cols), merge_gain.reshape(4, channels), merge_weight,
        deep[0], *coarse_weights,
    )

    out = pl.pallas_call(
        last_kernel,
        out_shape=jax.ShapeDtypeStruct((LEVELS * rows * cols, channels), BF16),
        grid=(1,),
        in_specs=[WHOLE] * 5 + [smem, WHOLE] + [block_spec(w, 1) for w in coarse_weights]
        + [WHOLE] * 4,
        out_specs=WHOLE,
        scratch_shapes=shifted_scratch(quad_rows // 2, quad_cols // 2, wide),
        compiler_params=params,
        name="coarse_shifted_expand",
    )(
        *halo(coarse.reshape(quad_rows // 2, quad_cols // 2, QP, wide)), edge, deep[1],
        *coarse_weights, parts, expand_weight, expand_gain[None], expand_table(rows, cols),
    )
    return out.reshape(fields.shape)


def solution(mesh):
    grid = P(None, "lat", LON, None)
    return jax.shard_map(
        on_device,
        mesh=mesh,
        in_specs=(grid, P("lat", LON)) + (P(),) * 18,
        out_specs=grid,
        check_vma=False,
    )
```

time: 381 us -> 130 us (0.34)
  local copies, waits for them, and re-layouts: 283 us -> 13.1 us
  Pallas kernels: 0 us -> 93.5 us
  matrix products: 40.2 us -> 0 us
  other arithmetic: 20.2 us -> 0.18 us
  waiting for transfers between devices: 17.9 us -> 6.85 us
    gather x8 -> x0, local copies, waits for them, and re-layouts: 202 us -> none  [the longest x4 101 us: on_device(): position_bias = jnp.take(fine_bias[block_number], bias_index, axis=1)]
    pallas_call x0 -> x7, Pallas kernels: none -> 93.5 us  [the longest x4 67.1 us: bias_of(): pl.pallas_call(functools.partial(bias_kernel, heads=heads, head_rows=head...]
    dot_general x21 -> x0, matrix products: 35.5 us -> none  [the longest x4 19.2 us: finish(): jnp.dot(hidden, w_narrow, preferred_element_type=jnp.float32)]
    slice x26 -> x6, local copies, waits for them, and re-layouts: 29.3 us -> 0.69 us  [the longest x2 0.66 us: halo(): south = lax.ppermute(own[0], 'lat', up)]
    convert_element_type x12 -> x0, local copies, waits for them, and re-layouts: 19.3 us -> none  [the longest x1 12.8 us: attend(): triple = jnp.dot(normed.reshape(-1, channels), w_triple, preferred_elemen...]
    reshape x10 -> x1, local copies, waits for them, and re-layouts: 18.6 us -> 0.08 us  [on_device(): merge_gain.reshape(4, channels)]
    ppermute x8, waiting for transfers between devices: 17.9 us -> 6.85 us  [the longest x2 3.49 us: halo(): from_east = lax.ppermute(side(0), LON, west)]
    convert_element_type x13 -> x0, other arithmetic: 5.46 us -> none  [the longest x1 1.83 us: expand_patches(): (skip_stream.astype(jnp.float32) + layer_norm(shuffled, norm_gain)).astyp...]
  transfers between devices with their start and end apart: 8 -> 8, of which waited for: 6 -> 3; matrix products, arithmetic and copies ran while one was open for 28% -> 1% of each run, Pallas kernels for 0% -> 41%
where the time goes in v1:
time: 130 us
  Pallas kernels  93.5 us (72%)
  starting transfers between devices  15.7 us (12%)
  local copies, waits for them, and re-layouts  13.1 us (10%)
  waiting for transfers between devices  6.85 us (5%)
    pallas_call x4, Pallas kernels, bias_of(): pl.pallas_call(functools.partial(bias_kernel, heads=heads, head_rows=head...  67.1 us
    unnamed x53, local copies, waits for them, and re-layouts  12.3 us
    pallas_call x1, Pallas kernels, on_device(): pl.pallas_call(middle_kernel, out_shape=[jax.ShapeDtypeStruct((tokens, ch...  12.2 us
    ppermute x2, starting transfers between devices, halo(): south = lax.ppermute(own[0], 'lat', up)  7.91 us
    pallas_call x1, Pallas kernels, on_device(): pl.pallas_call(last_kernel, out_shape=jax.ShapeDtypeStruct((LEVELS * rows...  7.57 us
    pallas_call x1, Pallas kernels, on_device(): pl.pallas_call(first_kernel, out_shape=jax.ShapeDtypeStruct((tokens, chan...  6.64 us
    ppermute x2, waiting for transfers between devices, halo(): from_east = lax.ppermute(side(0), LON, west)  3.49 us
    ppermute x2, starting transfers between devices, halo(): from_west = lax.ppermute(side(cols - 1), LON, east)  3.28 us
  transfers between devices with their start and end apart: 8, of which 3 were waited for; matrix products, arithmetic and copies ran while one was open for 1% of the time, Pallas kernels for 41%

profile of v1, /device:TPU:0, one launch (start us, length us, event | category | flops | bytes accessed | tf_op | source)
XLA Modules:
  0.0 129.7 jit_solution(18217474419594699710)
XLA Ops:
  0.0 1.6 %copy.27.table_ref = f32[2,6,3312]{2,1,0:T(8,128)} copy(f32[2,6,3312]{2,0,1:T(2,128)} %param.30) | data formatting | bytes 317952 | tf_op args[4]
  1.6 1.3 %copy.28.w_narrow_ref = bf16[2,768,192]{2,1,0:T(8,128)(2,1)S(1)} copy(bf16[2,768,192]{1,2,0:T(8,128)(2,1)} %param.35) | data formatting | bytes 1179648 | tf_op args[9]
  3.0 0.0 copy-start.1
  3.0 0.0 copy-start.3
  3.0 0.0 copy-start.7
  3.0 0.0 copy-start.11
  3.0 0.0 copy-start.16
  3.0 0.0 copy-start.17
  3.0 0.0 copy-start.19
  3.0 0.0 copy-start.20
  3.1 0.0 copy-start.21
  3.1 14.3 %bias_table.4.bias_ref = f32[960,160]{1,0:T(8,128)} custom-call(s32[144,144]{1,0:T(8,128)} %index_ref.7, bf16[160,144]{1,0:T(8,128)(2,1)} %constant.26.clone.spread_ref, f32[2,6,3312]{2,1,0:T(8,128)} %copy.27.table_ref), custom_call_target="tpu_custom_call" | custom-call | flops 10905190400 | bytes 1048576 | tf_op jit(solution)/shard_map/bias_table/pallas_call | solution.py:197
  17.3 0.0 copy-done.1
  17.3 0.0 copy-done.3
  17.3 0.0 copy-done.7
  17.3 0.0 copy-done.11
  17.4 0.0 copy-done.16
  17.4 0.0 copy-done.17
  17.4 0.0 copy-done.19
  17.4 0.0 copy-done.20
  17.4 0.0 copy-done.21
  17.4 0.0 copy-start.4
  17.4 1.2 copy-done.4
  18.6 1.1 copy-done.5
  19.8 6.6 %fine_plain.1.own_ref = bf16[640,192]{1,0:T(8,128)(2,1)S(1)} custom-call(bf16[576,192]{1,0:T(8,128)(2,1)S(1)} %bitcast.38, s32[12,24]{1,0:T(8,128)S(1)} %copy-done.20, f32[1,192]{1,0:T(1,128)S(1)} %bitcast.47, bf16[640,576]{1,0:T(8,128)(2,1)S(1)} %copy-done.5, bf16[640,12]{1,0:T(8,128)(2,1)S(1)} %copy-done.16, bf16[640,24]{1,0:T(8,128)(2,1)S(1)} %copy-done.17, ...), custom_call_target="tpu_custom_call" | custom-call | tf_op jit(solution)/shard_map/fine_plain/pallas_call | solution.py:446
  26.4 0.6 fusion
  27.1 3.0 %collective-permute-start = (bf16[4,40,192]{2,1,0:T(8,128)(2,1)}, bf16[4,40,192]{2,1,0:T(8,128)(2,1)S(1)}, u32[]{:S(2)}, u32[]{:S(2)}) collective-permute-start(bf16[4,40,192]{2,1,0:T(8,128)(2,1)} %bitcast.2), channel_id=1, source_target_pairs={{0,2},{2,4},{4,6},{6,8},{8,10},{10,12},{12,14},{14,0},{1,3},{3,5},... | collective-permute-start | bytes 184328 | tf_op jit(solution)/shard_map/ppermute | solution.py:402
  30.0 3.2 %collective-permute-start.1 = (bf16[4,40,192]{2,1,0:T(8,128)(2,1)S(1)}, bf16[4,40,192]{2,1,0:T(8,128)(2,1)S(1)}, u32[]{:S(2)}, u32[]{:S(2)}) collective-permute-start(bf16[4,40,192]{2,1,0:T(8,128)(2,1)S(1)} %bitcast.49), channel_id=1, source_target_pairs={{2,0},{4,2},{6,4},{8,6},{10,8},{12,10},{14,12},{0,14},{3,1},{5,3},... | collective-permute-start | bytes 184328 | tf_op jit(solution)/shard_map/ppermute | solution.py:403
  33.2 14.1 %bias_table.5.bias_ref = f32[960,160]{1,0:T(8,128)} custom-call(s32[144,144]{1,0:T(8,128)} %index_ref.7, bf16[160,144]{1,0:T(8,128)(2,1)} %constant.26.clone.spread_ref, f32[2,6,3312]{2,1,0:T(8,128)} %copy.27.table_ref), custom_call_target="tpu_custom_call" | custom-call | flops 10905190400 | bytes 1048576 | tf_op jit(solution)/shard_map/bias_table/pallas_call | solution.py:197
  47.4 0.0 copy-done.23
  47.4 0.8 copy.32.table_ref
  48.2 19.4 %bias_table.6.coarse_bias_ref = f32[1920,160]{1,0:T(8,128)} custom-call(s32[144,144]{1,0:T(8,128)} %index_ref.7, bf16[160,144]{1,0:T(8,128)(2,1)} %constant.26.clone.spread_ref, f32[2,12,3312]{2,1,0:T(8,128)} %copy.32.table_ref), custom_call_target="tpu_custom_call" | custom-call | flops 21810380800 | bytes 1048576 | tf_op jit(solution)/shard_map/bias_table/pallas_call | solution.py:197
  67.6 0.0 copy-done.24
  67.6 0.1 reshape.53.merge_gain_ref
  67.7 0.0 collective-permute-done
  67.7 0.0 collective-permute-done.1
  67.7 0.7 collective-permute-start.3
  68.5 1.6 %collective-permute-start.2 = (bf16[6,40,192]{2,1,0:T(8,128)(2,1)S(1)}, bf16[6,40,192]{2,1,0:T(8,128)(2,1)S(1)}, u32[]{:S(2)}, u32[]{:S(2)}) collective-permute-start(bf16[6,40,192]{2,1,0:T(8,128)(2,1)S(1)} %pad_maximum_fusion), channel_id=1, source_target_pairs={{0,1},{1,16},{16,17},{17,0},{2,3},{3,18},{18,19},{19,2},{4,5},{5,2... | collective-permute-start | bytes 276488 | tf_op jit(solution)/shard_map/ppermute | solution.py:408
  70.1 0.1 pad_maximum_fusion.4.edge_ref
  70.2 3.5 %collective-permute-done.3 = bf16[6,40,192]{2,1,0:T(8,128)(2,1)S(1)} collective-permute-done((bf16[6,40,192]{2,1,0:T(8,128)(2,1)S(1)}, bf16[6,40,192]{2,1,0:T(8,128)(2,1)S(1)}, u32[]{:S(2)}, u32[]{:S(2)}) %collective-permute-start.3) | collective-permute-done | bytes 92192 | tf_op jit(solution)/shard_map/ppermute | solution.py:409
  73.6 0.8 collective-permute-done.2
  74.5 0.0 copy-start.6
  74.5 1.1 copy-done.6
  75.6 1.1 copy-done.10
  76.7 0.9 copy-done.13
  77.6 0.9 copy-done.15
  78.4 12.2 %fine_shifted_coarse_plain.1 = (bf16[640,192]{1,0:T(8,128)(2,1)S(1)}, bf16[160,384]{1,0:T(8,128)(2,1)S(1)}) custom-call(bf16[640,192]{1,0:T(8,128)(2,1)S(1)} %fine_plain.1.own_ref, bf16[160,192]{1,0:T(8,128)(2,1)S(1)} %bitcast.41, bf16[160,192]{1,0:T(8,128)(2,1)S(1)} %bitcast.42, bf16[240,192]{1,0:T(8,128)(2,1)S(1)} %bitcast.46, ...), custom_call_target="tpu_custom_call" | custom-call | tf_op jit(solution)/shard_map/fine_shifted_coarse_plain/pallas_call | solution.py:469
  90.6 0.1 collective-permute-start.4
  90.7 4.7 %collective-permute-start.5 = (bf16[2,40,384]{2,1,0:T(8,128)(2,1)S(1)}, bf16[2,40,384]{2,1,0:T(8,128)(2,1)S(1)}, u32[]{:S(2)}, u32[]{:S(2)}) collective-permute-start(bf16[2,40,384]{2,1,0:T(8,128)(2,1)S(1)} %bitcast.50), channel_id=1, source_target_pairs={{2,0},{4,2},{6,4},{8,6},{10,8},{12,10},{14,12},{0,14},{3,1},{5,3},... | collective-permute-start | bytes 184328 | tf_op jit(solution)/shard_map/ppermute | solution.py:403
  95.4 2.6 %collective-permute-done.4 = bf16[2,40,384]{2,1,0:T(8,128)(2,1)S(1)} collective-permute-done((bf16[2,40,384]{2,1,0:T(8,128)(2,1)S(1)}, bf16[2,40,384]{2,1,0:T(8,128)(2,1)S(1)}, u32[]{:S(2)}, u32[]{:S(2)}) %collective-permute-start.4) | collective-permute-done | bytes 61472 | tf_op jit(solution)/shard_map/ppermute | solution.py:402
  98.0 0.0 collective-permute-done.5
  98.0 0.8 collective-permute-start.7
  98.9 0.0 copy-start
  98.9 0.0 copy-start.22
  98.9 1.7 %collective-permute-start.6 = (bf16[4,40,384]{2,1,0:T(8,128)(2,1)S(1)}, bf16[4,40,384]{2,1,0:T(8,128)(2,1)S(1)}, u32[]{:S(2)}, u32[]{:S(2)}) collective-permute-start(bf16[4,40,384]{2,1,0:T(8,128)(2,1)S(1)} %pad_maximum_fusion.2), channel_id=1, source_target_pairs={{0,1},{1,16},{16,17},{17,0},{2,3},{3,18},{18,19},{19,2},{4,5},{5,2... | collective-permute-start | bytes 368648 | tf_op jit(solution)/shard_map/ppermute | solution.py:408
  100.6 19.3 %bias_table.7.bias_ref = f32[1920,160]{1,0:T(8,128)} custom-call(s32[144,144]{1,0:T(8,128)} %index_ref.7, bf16[160,144]{1,0:T(8,128)(2,1)} %constant.26.clone.spread_ref, f32[2,12,3312]{2,1,0:T(8,128)} %copy.32.table_ref), custom_call_target="tpu_custom_call" | custom-call | flops 21810380800 | bytes 1048576 | tf_op jit(solution)/shard_map/bias_table/pallas_call | solution.py:197
  119.9 0.0 collective-permute-done.7
  119.9 0.0 collective-permute-done.6
  119.9 0.0 copy-done
  119.9 0.0 copy-done.22
  119.9 0.0 copy-start.8
  119.9 1.1 copy-done.8
  121.0 1.1 copy-done.9
  122.1 7.6 %coarse_shifted_expand.1 = bf16[576,192]{1,0:T(8,128)(2,1)} custom-call(bf16[160,384]{1,0:T(8,128)(2,1)S(1)} %get-tuple-element.7.own_ref, bf16[80,384]{1,0:T(8,128)(2,1)S(1)} %bitcast.39, bf16[80,384]{1,0:T(8,128)(2,1)S(1)} %bitcast.40, bf16[160,384]{1,0:T(8,128)(2,1)S(1)} %bitcast.44, bf16[160,384]{1,0:T(8,128)(2,1)S(1)} %bitcast.43, ...), custom_call_target="tpu_custom_call" | custom-call | tf_op jit(solution)/shard_map/coarse_shifted_expand/pallas_call | solution.py:488
  (26 shorter events, 0.2 us)
Async XLA Ops:
  3.0 14.4 %copy-start.1 = (bf16[2,192,768]{2,1,0:T(8,128)(2,1)S(1)}, bf16[2,192,768]{2,1,0:T(8,128)(2,1)}, u32[]{:S(2)}) copy-start(bf16[2,192,768]{2,1,0:T(8,128)(2,1)} %w_widen_ref.4) | copy-start | bytes 1769476
  3.0 14.4 %copy-start.3 = (bf16[2,192,576]{2,1,0:T(8,128)(2,1)S(1)}, bf16[2,192,576]{2,1,0:T(8,128)(2,1)}, u32[]{:S(2)}) copy-start(bf16[2,192,576]{2,1,0:T(8,128)(2,1)} %w_triple_ref.4) | copy-start | bytes 1327108
  3.0 14.4 %copy-start.7 = (bf16[2,192,192]{2,1,0:T(8,128)(2,1)S(1)}, bf16[2,192,192]{2,1,0:T(8,128)(2,1)}, u32[]{:S(2)}) copy-start(bf16[2,192,192]{2,1,0:T(8,128)(2,1)} %w_project_ref.4) | copy-start | bytes 442372
  3.0 14.3 %copy-start.11 = (bf16[2,12,24,192]{3,2,1,0:T(8,128)(2,1)S(1)}, bf16[2,12,24,192]{3,2,1,0:T(8,128)(2,1)}, u32[]{:S(2)}) copy-start(bf16[2,12,24,192]{3,2,1,0:T(8,128)(2,1)} %param.26) | copy-start | bytes 663556
  3.0 14.3 %copy-start.16 = (bf16[640,12]{1,0:T(8,128)(2,1)S(1)}, bf16[640,12]{1,0:T(8,128)(2,1)}, u32[]{:S(2)}) copy-start(bf16[640,12]{1,0:T(8,128)(2,1)} %constant.28.clone.of_row_ref) | copy-start | bytes 46084
  3.0 14.3 %copy-start.17 = (bf16[640,24]{1,0:T(8,128)(2,1)S(1)}, bf16[640,24]{1,0:T(8,128)(2,1)}, u32[]{:S(2)}) copy-start(bf16[640,24]{1,0:T(8,128)(2,1)} %constant.29.clone.of_col_ref) | copy-start | bytes 92164
  3.0 14.3 %copy-start.19 = (f32[2,2,192]{2,1,0:T(2,128)S(1)}, f32[2,2,192]{2,1,0:T(2,128)}, u32[]{:S(2)}) copy-start(f32[2,2,192]{2,1,0:T(2,128)} %gains_ref.4) | copy-start | bytes 9220
  3.0 14.3 %copy-start.20 = (s32[12,24]{1,0:T(8,128)S(1)}, s32[12,24]{1,0:T(8,128)}, u32[]{:S(2)}) copy-start(s32[12,24]{1,0:T(8,128)} %land_ref.1) | copy-start | bytes 3460
  3.1 14.3 %copy-start.21 = (f32[192]{0:T(256)S(1)}, f32[192]{0:T(256)}, u32[]{:S(2)}) copy-start(f32[192]{0:T(256)} %param.28) | copy-start | bytes 2308
  17.4 1.2 copy-start.4
  18.6 1.1 copy-start.5
  27.1 40.6 %collective-permute-start = (bf16[4,40,192]{2,1,0:T(8,128)(2,1)}, bf16[4,40,192]{2,1,0:T(8,128)(2,1)S(1)}, u32[]{:S(2)}, u32[]{:S(2)}) collective-permute-start(bf16[4,40,192]{2,1,0:T(8,128)(2,1)} %bitcast.2), channel_id=1, source_target_pairs={{0,2},{2,4},{4,6},{6,8},{8,10},{10,12},{12,14},{14,0},{1,3},{3,5},... | collective-permute-start | bytes 184328 | tf_op jit(solution)/shard_map/ppermute | solution.py:402
  30.0 17.3 %copy-start.23 = (f32[2,12,3312]{2,0,1:T(2,128)S(1)}, f32[2,12,3312]{2,0,1:T(2,128)}, u32[]{:S(2)}) copy-start(f32[2,12,3312]{2,0,1:T(2,128)} %param.38) | copy-start | bytes 953860
  30.0 37.7 %collective-permute-start.1 = (bf16[4,40,192]{2,1,0:T(8,128)(2,1)S(1)}, bf16[4,40,192]{2,1,0:T(8,128)(2,1)S(1)}, u32[]{:S(2)}, u32[]{:S(2)}) collective-permute-start(bf16[4,40,192]{2,1,0:T(8,128)(2,1)S(1)} %bitcast.49), channel_id=1, source_target_pairs={{2,0},{4,2},{6,4},{8,6},{10,8},{12,10},{14,12},{0,14},{3,1},{5,3},... | collective-permute-start | bytes 184328 | tf_op jit(solution)/shard_map/ppermute | solution.py:403
  48.2 19.4 %copy-start.24 = (f32[768]{0:T(1024)S(1)}, f32[768]{0:T(1024)}, u32[]{:S(2)}) copy-start(f32[768]{0:T(1024)} %param.36) | copy-start | bytes 9220
  48.2 26.3 %copy-start.2 = (bf16[2,384,384]{2,1,0:T(8,128)(2,1)S(1)}, bf16[2,384,384]{2,1,0:T(8,128)(2,1)}, u32[]{:S(2)}) copy-start(bf16[2,384,384]{2,1,0:T(8,128)(2,1)} %w_project_ref.5) | copy-start | bytes 1769476
  48.2 26.3 %copy-start.18 = (f32[2,2,384]{2,1,0:T(2,128)S(1)}, f32[2,2,384]{2,1,0:T(2,128)}, u32[]{:S(2)}) copy-start(f32[2,2,384]{2,1,0:T(2,128)} %gains_ref.5) | copy-start | bytes 18436
  67.7 6.8 %copy-start.12 = (bf16[4,40,192]{2,1,0:T(8,128)(2,1)}, bf16[4,40,192]{2,1,0:T(8,128)(2,1)S(1)}, u32[]{:S(2)}) copy-start(bf16[4,40,192]{2,1,0:T(8,128)(2,1)S(1)} %collective-permute-done) | copy-start | bytes 184324
  67.7 6.8 %copy-start.14 = (bf16[4,40,192]{2,1,0:T(8,128)(2,1)}, bf16[4,40,192]{2,1,0:T(8,128)(2,1)S(1)}, u32[]{:S(2)}) copy-start(bf16[4,40,192]{2,1,0:T(8,128)(2,1)S(1)} %collective-permute-done.1) | copy-start | bytes 184324
  67.7 5.9 %collective-permute-start.3 = (bf16[6,40,192]{2,1,0:T(8,128)(2,1)S(1)}, bf16[6,40,192]{2,1,0:T(8,128)(2,1)S(1)}, u32[]{:S(2)}, u32[]{:S(2)}) collective-permute-start(bf16[6,40,192]{2,1,0:T(8,128)(2,1)S(1)} %pad_maximum_fusion.1), channel_id=1, source_target_pairs={{1,0},{16,1},{17,16},{0,17},{3,2},{18,3},{19,18},{2,19},{5,4},{20,... | collective-permute-start | bytes 276488 | tf_op jit(solution)/shard_map/ppermute | solution.py:409
  68.5 6.0 %collective-permute-start.2 = (bf16[6,40,192]{2,1,0:T(8,128)(2,1)S(1)}, bf16[6,40,192]{2,1,0:T(8,128)(2,1)S(1)}, u32[]{:S(2)}, u32[]{:S(2)}) collective-permute-start(bf16[6,40,192]{2,1,0:T(8,128)(2,1)S(1)} %pad_maximum_fusion), channel_id=1, source_target_pairs={{0,1},{1,16},{16,17},{17,0},{2,3},{3,18},{18,19},{19,2},{4,5},{5,2... | collective-permute-start | bytes 276488 | tf_op jit(solution)/shard_map/ppermute | solution.py:408
  74.5 1.1 copy-start.6
  75.6 1.1 copy-start.10
  76.7 0.9 copy-start.13
  77.6 0.9 copy-start.15
  90.6 7.3 %collective-permute-start.4 = (bf16[2,40,384]{2,1,0:T(8,128)(2,1)S(1)}, bf16[2,40,384]{2,1,0:T(8,128)(2,1)S(1)}, u32[]{:S(2)}, u32[]{:S(2)}) collective-permute-start(bf16[2,40,384]{2,1,0:T(8,128)(2,1)S(1)} %bitcast.51), channel_id=1, source_target_pairs={{0,2},{2,4},{4,6},{6,8},{8,10},{10,12},{12,14},{14,0},{1,3},{3,5},... | collective-permute-start | bytes 184328 | tf_op jit(solution)/shard_map/ppermute | solution.py:402
  90.7 7.3 %collective-permute-start.5 = (bf16[2,40,384]{2,1,0:T(8,128)(2,1)S(1)}, bf16[2,40,384]{2,1,0:T(8,128)(2,1)S(1)}, u32[]{:S(2)}, u32[]{:S(2)}) collective-permute-start(bf16[2,40,384]{2,1,0:T(8,128)(2,1)S(1)} %bitcast.50), channel_id=1, source_target_pairs={{2,0},{4,2},{6,4},{8,6},{10,8},{12,10},{14,12},{0,14},{3,1},{5,3},... | collective-permute-start | bytes 184328 | tf_op jit(solution)/shard_map/ppermute | solution.py:403
  98.0 21.8 %collective-permute-start.7 = (bf16[4,40,384]{2,1,0:T(8,128)(2,1)S(1)}, bf16[4,40,384]{2,1,0:T(8,128)(2,1)S(1)}, u32[]{:S(2)}, u32[]{:S(2)}) collective-permute-start(bf16[4,40,384]{2,1,0:T(8,128)(2,1)S(1)} %pad_maximum_fusion.3), channel_id=1, source_target_pairs={{1,0},{16,1},{17,16},{0,17},{3,2},{18,3},{19,18},{2,19},{5,4},{20,... | collective-permute-start | bytes 368648 | tf_op jit(solution)/shard_map/ppermute | solution.py:409
  98.9 21.0 %copy-start = (bf16[2,384,1152]{2,1,0:T(8,128)(2,1)S(1)}, bf16[2,384,1152]{2,1,0:T(8,128)(2,1)}, u32[]{:S(2)}) copy-start(bf16[2,384,1152]{2,1,0:T(8,128)(2,1)} %w_triple_ref.5) | copy-start | bytes 5308420
  98.9 21.0 %copy-start.22 = (f32[192]{0:T(256)S(1)}, f32[192]{0:T(256)}, u32[]{:S(2)}) copy-start(f32[192]{0:T(256)} %param.45) | copy-start | bytes 2308
  98.9 21.0 %collective-permute-start.6 = (bf16[4,40,384]{2,1,0:T(8,128)(2,1)S(1)}, bf16[4,40,384]{2,1,0:T(8,128)(2,1)S(1)}, u32[]{:S(2)}, u32[]{:S(2)}) collective-permute-start(bf16[4,40,384]{2,1,0:T(8,128)(2,1)S(1)} %pad_maximum_fusion.2), channel_id=1, source_target_pairs={{0,1},{1,16},{16,17},{17,0},{2,3},{3,18},{18,19},{19,2},{4,5},{5,2... | collective-permute-start | bytes 368648 | tf_op jit(solution)/shard_map/ppermute | solution.py:408
  119.9 1.1 copy-start.8
  121.0 1.1 copy-start.9

commit v2 on v1

v2 whole, which is shorter than its diff:
```python
import functools

import jax
import jax.numpy as jnp
import numpy as np
from jax import lax
from jax.experimental import pallas as pl
from jax.experimental.pallas import tpu as pltpu
from jax.sharding import PartitionSpec as P

HF = 6
HC = 12
HEAD = 32
WIN_LAT = 6
WIN_LON = 12
WIN_TOK = 144
HALF_LAT = WIN_LAT // 2
HALF_LON = WIN_LON // 2
LEVELS = 2
QUAD = LEVELS * HALF_LAT * HALF_LON
QP = 40
WP = 4 * QP
LO_COUNT = 13
LOG2E = 1.4426950408889634
MASKED = -1e30
LON = ("sec", "head")
F32 = jnp.float32
BF16 = jnp.bfloat16


def quad_sources(row_count, col_count):
    slots = []
    for a in range(row_count // HALF_LAT):
        for b in range(col_count // HALF_LON):
            for s in range(QP):
                if s >= QUAD:
                    slots.append(None)
                    continue
                level, rest = divmod(s, HALF_LAT * HALF_LON)
                r, c = divmod(rest, HALF_LON)
                slots.append((level, a * HALF_LAT + r, b * HALF_LON + c))
    return slots


def one_hot(sources, width):
    table = np.zeros((len(sources), width), np.float32)
    for slot, source in enumerate(sources):
        if source is not None:
            table[slot, source] = 1.0
    return jnp.asarray(table.astype(jnp.bfloat16))


def fine_tables(rows, cols):
    slots = quad_sources(rows, cols)
    order = one_hot(
        [None if s is None else (s[0] * rows + s[1]) * cols + s[2] for s in slots],
        LEVELS * rows * cols,
    )
    of_row = one_hot([None if s is None else s[1] for s in slots], rows)
    of_col = one_hot([None if s is None else s[2] for s in slots], cols)
    return order, of_row, of_col


def merge_table(rows, cols):
    place = {s: n for n, s in enumerate(quad_sources(rows, cols)) if s is not None}
    sources = []
    for p in range(2):
        for q in range(2):
            for s in quad_sources(rows // 2, cols // 2):
                sources.append(
                    None if s is None else place[(s[0], 2 * s[1] + p, 2 * s[2] + q)]
                )
    return one_hot(sources, len(place) // QUAD * QP)


def expand_table(rows, cols):
    coarse = quad_sources(rows // 2, cols // 2)
    place = {s: n for n, s in enumerate(coarse) if s is not None}
    sources = []
    for level in range(LEVELS):
        for r in range(rows):
            for c in range(cols):
                part = (r % 2) * 2 + c % 2
                sources.append(part * len(coarse) + place[(level, r // 2, c // 2)])
    return one_hot(sources, 4 * len(coarse))


def dot(a, b):
    return jnp.dot(a, b, preferred_element_type=F32)


def dot_t(a, b):
    return lax.dot_general(a, b, (((1,), (1,)), ((), ())), preferred_element_type=F32)


def norm(x, gain):
    mean = jnp.mean(x, axis=-1, keepdims=True)
    centered = x - mean
    variance = jnp.mean(centered * centered, axis=-1, keepdims=True)
    return centered * lax.rsqrt(variance + 1e-05) * gain


def attend(q, k, v, bias_ref, first, key_mask):
    n = q.shape[0]
    channels = q.shape[1]
    scale = HEAD**-0.5 * LOG2E
    outs = []
    for tile in range(0, channels, 128):
        width = min(128, channels - tile)
        count = width // HEAD
        qt = q[:, tile : tile + width]
        lane = lax.broadcasted_iota(jnp.int32, (n, width), 1) // HEAD
        masks = [lane == h for h in range(count)]
        stack = jnp.concatenate([jnp.where(m, qt, jnp.zeros_like(qt)) for m in masks], axis=0)
        scores = dot_t(stack, k[:, tile : tile + width])
        probs = []
        for h in range(count):
            head = tile // HEAD + h
            bias = jnp.concatenate(
                [
                    bias_ref[0, head, first : first + n, :],
                    bias_ref[1, head, first : first + n, : WP - 128],
                ],
                axis=1,
            )
            s = scores[h * n : (h + 1) * n] * scale + bias
            if key_mask is not None:
                s = s + key_mask
            s = s - jnp.max(s, axis=-1, keepdims=True)
            probs.append(jnp.exp2(s).astype(BF16))
        probs = jnp.concatenate(probs, axis=0)
        vt = v[:, tile : tile + width]
        mixed = dot(probs, jnp.concatenate([vt, jnp.ones((WP, width), BF16)], axis=1))
        top = mixed[:n, :width]
        total = mixed[:n, width:]
        for h in range(1, count):
            top = jnp.where(masks[h], mixed[h * n : (h + 1) * n, :width], top)
            total = jnp.where(masks[h], mixed[h * n : (h + 1) * n, width:], total)
        outs.append(top / total)
    return outs[0] if len(outs) == 1 else jnp.concatenate(outs, axis=1)


def gelu(x):
    return 0.5 * x * (1.0 + lax.erf(x * np.float32(0.5**0.5)))


def finish(x, context, gain, w_project, w_widen, w_narrow):
    middle = (x + dot(context, w_project)).astype(BF16).astype(F32)
    second = norm(middle, gain).astype(BF16)
    hidden = gelu(dot(second, w_widen)).astype(BF16)
    return (middle + dot(hidden, w_narrow)).astype(BF16)


def padded(heads):
    return -(-heads // 8) * 8


def bias_kernel(index_ref, spread_ref, *refs, picks):
    table_refs = refs[:-4]
    out_ref, table, index, left = refs[-4:]
    rows = table.shape[0]
    bias_len = table_refs[0].shape[-1]

    @pl.when(pl.program_id(0) == 0)
    def _():
        spread = spread_ref[...]
        plain = index_ref[...]
        high = (plain >> 4).astype(F32).astype(BF16)
        low = (plain & 15).astype(F32).astype(BF16)

        def moved(part):
            return dot_t(dot(spread, part).astype(BF16), spread).astype(jnp.int32)

        spot = lax.broadcasted_iota(jnp.int32, (WP, WP), 1) % QP
        index[...] = jnp.where(spot < QUAD, moved(high) * 16 + moved(low), bias_len)
        table[...] = jnp.full(table.shape, MASKED, F32)
        at = 0
        for table_ref, block in zip(table_refs, picks):
            heads = table_ref.shape[0]
            for h in range(heads):
                table[at + h : at + h + 1, :bias_len] = (
                    table_ref[h, block : block + 1, :] * LOG2E
                )
            at += padded(heads)
        values = table[...]
        big = values.astype(BF16)
        small = (values - big.astype(F32)).astype(BF16)
        for n, part in enumerate((big, small)):
            left[:, n * 256 : (n + 1) * 256] = jnp.concatenate(
                [part[:, i * 256 : (i + 1) * 256] for i in range(LO_COUNT)], axis=0
            )

    ladder = lax.broadcasted_iota(jnp.int32, (256, 256), 0).astype(F32).astype(BF16)
    lane = lax.broadcasted_iota(jnp.int32, (8, 256), 1) // 32
    sublane = lax.broadcasted_iota(jnp.int32, (8, 256), 0)
    span = out_ref.shape[1] // rows
    for group in range(span // 8):
        first = pl.multiple_of(pl.program_id(0) * span + group * 8, 8)
        entries = index[pl.ds(first, 8), :]
        rest = jnp.concatenate([entries[:, 128:]] * 8, axis=1)
        rest = jnp.sum(jnp.where(lane == sublane, rest, 0).astype(F32), axis=0, keepdims=True)
        pieces = [
            jnp.concatenate([entries[j : j + 1, :128], entries[j + 1 : j + 2, :128]], axis=1)
            for j in range(0, 8, 2)
        ] + [rest.astype(jnp.int32)]
        for t, entry in enumerate(pieces):
            near = (entry & 255).astype(F32).astype(BF16)
            far = entry >> 8
            chosen = jnp.where(ladder == near, jnp.ones((), BF16), jnp.zeros((), BF16))
            found = dot(left[...], jnp.concatenate([chosen, chosen], axis=0))
            total = found[:rows]
            for i in range(1, LO_COUNT):
                total = jnp.where(far == i, found[i * rows : (i + 1) * rows], total)
            for h in range(0, rows, 8):
                part = total[h : h + 8]
                at = h * span + group * 8
                if t < 4:
                    for j in range(2):
                        out_ref[0, pl.ds(at + 2 * t + j, 8, stride=span), :] = (
                            part[:, j * 128 : (j + 1) * 128]
                        )
                else:
                    for j in range(8):
                        moved_part = part[:, j // 4 * 128 : (j // 4 + 1) * 128]
                        if j % 4:
                            moved_part = pltpu.roll(moved_part, 128 - 32 * (j % 4), 1)
                        out_ref[1, pl.ds(at + j, 8, stride=span), :] = moved_part


def bias_of(picks, index, spread, span=32):
    tables = [t.transpose(1, 0, 2) for t, _ in picks]
    rows = sum(padded(t.shape[0]) for t in tables)
    flops = 2 * WP * 256 * WP * LO_COUNT * rows * 4
    steps = WP // span
    whole = pl.BlockSpec(memory_space=pltpu.VMEM)
    out = pl.pallas_call(
        functools.partial(bias_kernel, picks=tuple(b for _, b in picks)),
        out_shape=jax.ShapeDtypeStruct((2, steps * rows * span, 128), F32),
        grid=(steps,),
        in_specs=[whole] * (2 + len(tables)),
        out_specs=pl.BlockSpec((2, rows * span, 128), lambda i: (0, i, 0)),
        scratch_shapes=[
            pltpu.VMEM((rows, LO_COUNT * 256), F32),
            pltpu.VMEM((WP, WP), jnp.int32),
            pltpu.VMEM((rows * LO_COUNT, 512), BF16),
        ],
        compiler_params=pltpu.CompilerParams(vmem_limit_bytes=16 << 20),
        cost_estimate=pl.CostEstimate(flops=2 * flops, bytes_accessed=1 << 20, transcendentals=0),
        name="bias_table",
    )(index, spread, *tables)
    return out.reshape(2, steps, rows, span, 128)


def bias_copies(source_ref, bias, first, sems, at):
    steps, span, heads = source_ref.shape[1], source_ref.shape[3], bias.shape[1]
    return [
        pltpu.make_async_copy(
            source_ref.at[half, step, pl.ds(first, heads)],
            bias.at[half, :, pl.ds(step * span, span)],
            sems.at[at + half * steps + step],
        )
        for half in range(2)
        for step in range(steps)
    ]


class Fetched:
    def __init__(self, copies):
        self.copies = copies
        for group in copies:
            for copy in group:
                copy.start()

    def wait(self, *numbers):
        for n in numbers:
            for copy in self.copies[n]:
                copy.wait()


def first_kernel(
    fields_ref, land_ref, embed_ref, order_hbm, of_row_ref, of_col_ref, bias_hbm,
    gains_ref, triple_hbm, project_hbm, widen_hbm, narrow_hbm,
    out_ref, top_ref, bottom_ref,
    start_ref, order, bias, w_triple, w_project, w_widen, w_narrow, sems, bias_sems,
):
    channels = fields_ref.shape[1]
    fetched = Fetched(
        [[pltpu.make_async_copy(order_hbm, order, sems.at[0])],
         bias_copies(bias_hbm, bias, 0, bias_sems, 0)]
        + [
            [pltpu.make_async_copy(source.at[0], target, sems.at[1 + n])]
            for n, (source, target) in enumerate(
                [(triple_hbm, w_triple), (project_hbm, w_project),
                 (widen_hbm, w_widen), (narrow_hbm, w_narrow)]
            )
        ]
    )
    land = land_ref[...].astype(F32).astype(BF16)
    on_row = dot(of_row_ref[...], land)
    on_land = jnp.sum(on_row * of_col_ref[...].astype(F32), axis=-1, keepdims=True)
    fetched.wait(0)
    start = dot(order[...], fields_ref[...]) + on_land * embed_ref[...]
    start_ref[...] = start.astype(BF16).astype(F32)
    fetched.wait(1, 2, 3, 4, 5)
    rows = out_ref.shape[0]
    inner = top_ref.shape[0]
    down = rows // inner // 2
    for a in range(down):
        for b in range(inner // QP // 2):
            top = 2 * a * inner + 2 * b * QP
            below = top + inner
            x = jnp.concatenate(
                [start_ref[top : top + 2 * QP], start_ref[below : below + 2 * QP]], axis=0
            )
            normed = norm(x, gains_ref[0, 0:1]).astype(BF16)
            triple = dot(normed, w_triple[...]).astype(BF16)
            context = attend(
                triple[:, :channels],
                triple[:, channels : 2 * channels],
                triple[:, 2 * channels :],
                bias, 0, None,
            ).astype(BF16)
            done = finish(
                x, context, gains_ref[0, 1:2], w_project[...], w_widen[...], w_narrow[...]
            )
            out_ref[top : top + 2 * QP] = done[: 2 * QP]
            out_ref[below : below + 2 * QP] = done[2 * QP :]
    top_ref[...] = out_ref[:inner]
    bottom_ref[...] = out_ref[rows - inner :]


def shifted_block(
    own_ref, north_ref, south_ref, west_ref, east_ref, gains_ref, fetched,
    bias, w_triple, w_project, w_widen, w_narrow, query, key, value, context,
):
    channels = own_ref.shape[1]
    fetched.wait(1)
    across = north_ref.shape[0] // QP
    down = own_ref.shape[0] // QP // across
    line = (across + 2) * QP
    inner = across * QP
    for i in range(down + 2):
        if i == 0:
            middle = north_ref[...]
        elif i == down + 1:
            middle = south_ref[...]
        else:
            middle = own_ref[(i - 1) * inner : i * inner]
        x = jnp.concatenate(
            [
                west_ref[i * QP : (i + 1) * QP].astype(F32),
                middle.astype(F32),
                east_ref[i * QP : (i + 1) * QP].astype(F32),
            ],
            axis=0,
        )
        normed = norm(x, gains_ref[1, 0:1]).astype(BF16)
        triple = dot(normed, w_triple[...])
        if 0 < i < down + 1:
            query[(i - 1) * line : i * line] = triple[:, :channels]
        key[i * line : (i + 1) * line] = triple[:, channels : 2 * channels].astype(BF16)
        value[i * line : (i + 1) * line] = triple[:, 2 * channels :].astype(BF16)
    lane = lax.broadcasted_iota(jnp.int32, (1, WP), 1)
    place = lax.axis_index("lat")
    on_top = jnp.where(place == 0, MASKED, 0.0).astype(F32)
    on_bottom = jnp.where(place == lax.axis_size("lat") - 1, MASKED, 0.0).astype(F32)
    fetched.wait(0)
    for wa in range(down // 2 + 1):
        mask = None
        if wa == 0:
            mask = jnp.where(lane < 2 * QP, on_top, 0.0)
        elif wa == down // 2:
            mask = jnp.where(lane < 2 * QP, 0.0, on_bottom)
        for wb in range(across // 2 + 1):
            at = [(2 * wa + r) * line + 2 * wb * QP for r in range(2)]
            k = jnp.concatenate([key[s : s + 2 * QP] for s in at], axis=0)
            v = jnp.concatenate([value[s : s + 2 * QP] for s in at], axis=0)
            rows = [r for r in range(2) if 0 < 2 * wa + r < down + 1]
            cols = [c for c in range(2) if 0 < 2 * wb + c < across + 1]
            size = len(cols) * QP
            qs = [
                query[
                    (2 * wa + r - 1) * line + (2 * wb + cols[0]) * QP :
                    (2 * wa + r - 1) * line + (2 * wb + cols[0]) * QP + size
                ]
                for r in rows
            ]
            if len(cols) == 2:
                groups = [(rows, jnp.concatenate(qs, axis=0) if len(qs) == 2 else qs[0])]
            else:
                groups = [([r], part) for r, part in zip(rows, qs)]
            for group, q in groups:
                out = attend(
                    q.astype(BF16), k, v, bias, (2 * group[0] + cols[0]) * QP, mask
                )
                for n, r in enumerate(group):
                    to = ((2 * wa + r - 1) * across + 2 * wb + cols[0] - 1) * QP
                    context[to : to + size] = out[n * size : (n + 1) * size]
    fetched.wait(2, 3, 4)
    outs = []
    for at in range(0, own_ref.shape[0], WP):
        outs.append(
            finish(
                own_ref[at : at + WP].astype(F32),
                context[at : at + WP].astype(BF16),
                gains_ref[1, 1:2],
                w_project[...], w_widen[...], w_narrow[...],
            )
        )
    return outs


def block_copies(pairs, block, sems, at):
    return [
        [pltpu.make_async_copy(source.at[block], target, sems.at[at + n])]
        for n, (source, target) in enumerate(pairs)
    ]


def middle_kernel(
    own_ref, north_ref, south_ref, west_ref, east_ref, gains_ref, merge_gain_ref,
    coarse_gains_ref, bias_hbm, triple_hbm, project_hbm, widen_hbm, narrow_hbm,
    merge_order_hbm, merge_weight_hbm, c_triple_hbm, c_project_hbm, c_widen_hbm, c_narrow_hbm,
    parts_ref, coarse_ref, top_ref, bottom_ref,
    query, key, value, context, bias, c_bias, w_triple, w_project, w_widen, w_narrow,
    merge_order, merge_weight, c_triple, c_project, c_widen, c_narrow, sems, bias_sems,
):
    steps = bias_hbm.shape[1]
    heads = bias.shape[1]
    fetched = Fetched(
        [bias_copies(bias_hbm, bias, 0, bias_sems, 0)]
        + block_copies(
            [(triple_hbm, w_triple), (project_hbm, w_project),
             (widen_hbm, w_widen), (narrow_hbm, w_narrow)], 1, sems, 0,
        )
        + [
            [pltpu.make_async_copy(merge_order_hbm, merge_order, sems.at[4])],
            [pltpu.make_async_copy(merge_weight_hbm, merge_weight, sems.at[5])],
            bias_copies(bias_hbm, c_bias, padded(heads), bias_sems, 2 * steps),
        ]
        + block_copies(
            [(c_triple_hbm, c_triple), (c_project_hbm, c_project),
             (c_widen_hbm, c_widen), (c_narrow_hbm, c_narrow)], 0, sems, 6,
        )
    )
    outs = shifted_block(
        own_ref, north_ref, south_ref, west_ref, east_ref, gains_ref, fetched,
        bias, w_triple, w_project, w_widen, w_narrow, query, key, value, context,
    )
    channels = own_ref.shape[1]
    skip = jnp.concatenate(outs, axis=0)
    fetched.wait(*range(5, 12))
    grouped = dot(merge_order[...], skip)
    parts_ref[...] = grouped.astype(BF16)
    parts = [grouped[i * WP : (i + 1) * WP] for i in range(4)]
    width = 4 * channels
    mean = sum(jnp.sum(p, axis=-1, keepdims=True) for p in parts) / width
    parts = [p - mean for p in parts]
    variance = sum(jnp.sum(p * p, axis=-1, keepdims=True) for p in parts) / width
    factor = lax.rsqrt(variance + 1e-05)
    coarse = jnp.zeros((WP, merge_weight.shape[1]), F32)
    for i, p in enumerate(parts):
        merged = (p * factor * merge_gain_ref[i : i + 1]).astype(BF16)
        coarse = coarse + dot(merged, merge_weight[i * channels : (i + 1) * channels])
    x = coarse.astype(BF16).astype(F32)
    wide = x.shape[1]
    normed = norm(x, coarse_gains_ref[0, 0:1]).astype(BF16)
    triple = dot(normed, c_triple[...]).astype(BF16)
    mixed = attend(
        triple[:, :wide], triple[:, wide : 2 * wide], triple[:, 2 * wide :], c_bias, 0, None
    ).astype(BF16)
    done = finish(
        x, mixed, coarse_gains_ref[0, 1:2], c_project[...], c_widen[...], c_narrow[...]
    )
    coarse_ref[...] = done
    inner = top_ref.shape[0]
    top_ref[...] = done[:inner]
    bottom_ref[...] = done[WP - inner :]


def last_kernel(
    own_ref, north_ref, south_ref, west_ref, east_ref, gains_ref, parts_ref, expand_gain_ref,
    bias_hbm, triple_hbm, project_hbm, widen_hbm, narrow_hbm, expand_weight_hbm, expand_order_hbm,
    out_ref,
    query, key, value, context, bias, w_triple, w_project, w_widen, w_narrow,
    expand_weight, expand_order, sems, bias_sems,
):
    fetched = Fetched(
        [bias_copies(bias_hbm, bias, 0, bias_sems, 0)]
        + block_copies(
            [(triple_hbm, w_triple), (project_hbm, w_project),
             (widen_hbm, w_widen), (narrow_hbm, w_narrow)], 1, sems, 0,
        )
        + [
            [pltpu.make_async_copy(expand_weight_hbm, expand_weight, sems.at[4])],
            [pltpu.make_async_copy(expand_order_hbm, expand_order, sems.at[5])],
        ]
    )
    (deep,) = shifted_block(
        own_ref, north_ref, south_ref, west_ref, east_ref, gains_ref, fetched,
        bias, w_triple, w_project, w_widen, w_narrow, query, key, value, context,
    )
    channels = parts_ref.shape[1]
    fetched.wait(5, 6)
    widened = dot(deep, expand_weight[...])
    outs = []
    for i in range(4):
        shuffled = widened[:, i * channels : (i + 1) * channels]
        skip = parts_ref[i * WP : (i + 1) * WP].astype(F32)
        outs.append((skip + norm(shuffled, expand_gain_ref[...])).astype(BF16))
    out_ref[...] = dot(expand_order[...], jnp.concatenate(outs, axis=0)).astype(BF16)


WHOLE = pl.BlockSpec(memory_space=pltpu.VMEM)
APART = pl.BlockSpec(memory_space=pltpu.HBM)


def weight_scratch(weights):
    return [pltpu.VMEM(w.shape[1:], BF16) for w in weights]


def halo(own, top, bottom):
    rows, cols, _, channels = own.shape
    top = top.reshape(own.shape[1:])
    bottom = bottom.reshape(own.shape[1:])
    lat = lax.axis_size("lat")
    lon = lax.axis_size(LON)
    down = [(i, (i + 1) % lat) for i in range(lat)]
    up = [((i + 1) % lat, i) for i in range(lat)]
    east = [(i, (i + 1) % lon) for i in range(lon)]
    west = [((i + 1) % lon, i) for i in range(lon)]
    north = lax.ppermute(bottom, "lat", down)
    south = lax.ppermute(top, "lat", up)

    def side(c):
        return jnp.concatenate([north[c : c + 1], own[:, c], south[c : c + 1]], axis=0)

    from_west = lax.ppermute(side(cols - 1), LON, east)
    from_east = lax.ppermute(side(0), LON, west)
    return [v.reshape(-1, channels) for v in (own, north, south, from_west, from_east)]


def shifted_scratch(rows, cols, channels):
    line = (cols + 2) * QP
    return [
        pltpu.VMEM((rows * line, channels), F32),
        pltpu.VMEM(((rows + 2) * line, channels), BF16),
        pltpu.VMEM(((rows + 2) * line, channels), BF16),
        pltpu.VMEM((rows * cols * QP, channels), F32),
    ]


def on_device(
    fields, land_sea, land_embed, bias_index, fine_bias, fine_gains, fine_query_key_value,
    fine_project, fine_widen, fine_narrow, merge_gain, merge_weight, coarse_bias, coarse_gains,
    coarse_query_key_value, coarse_project, coarse_widen, coarse_narrow, expand_weight, expand_gain,
):
    _, rows, cols, channels = fields.shape
    quad_rows, quad_cols = rows // HALF_LAT, cols // HALF_LON
    tokens = quad_rows * quad_cols * QP
    wide = merge_weight.shape[1]
    spread = one_hot(
        [None if s is None else (s[0] * WIN_LAT + s[1]) * WIN_LON + s[2]
         for s in quad_sources(WIN_LAT, WIN_LON)],
        WIN_TOK,
    )
    order, of_row, of_col = fine_tables(rows, cols)
    bias_first = bias_of([(fine_bias, 0)], bias_index, spread)
    bias_middle = bias_of([(fine_bias, 1), (coarse_bias, 0)], bias_index, spread)
    bias_last = bias_of([(coarse_bias, 1)], bias_index, spread)
    fine_weights = (fine_query_key_value, fine_project, fine_widen, fine_narrow)
    coarse_weights = (coarse_query_key_value, coarse_project, coarse_widen, coarse_narrow)
    steps = bias_first.shape[1]
    dma = pltpu.SemaphoreType.DMA
    fine_scratch = pltpu.VMEM((2, HF, WP, 128), F32)
    coarse_scratch = pltpu.VMEM((2, HC, WP, 128), F32)
    line = quad_cols * QP

    first, top, bottom = pl.pallas_call(
        first_kernel,
        out_shape=[
            jax.ShapeDtypeStruct((tokens, channels), BF16),
            jax.ShapeDtypeStruct((line, channels), BF16),
            jax.ShapeDtypeStruct((line, channels), BF16),
        ],
        in_specs=[WHOLE] * 3 + [APART] + [WHOLE] * 2 + [APART, WHOLE] + [APART] * 4,
        out_specs=[WHOLE] * 3,
        scratch_shapes=[pltpu.VMEM((tokens, channels), F32), pltpu.VMEM(order.shape, BF16)]
        + [fine_scratch] + weight_scratch(fine_weights) + [dma((5,)), dma((2 * steps,))],
        compiler_params=pltpu.CompilerParams(vmem_limit_bytes=20 << 20),
        name="fine_plain",
    )(
        fields.reshape(-1, channels), land_sea, land_embed[None], order, of_row, of_col,
        bias_first, fine_gains, *fine_weights,
    )

    merge_order = merge_table(rows, cols)
    parts, coarse, top, bottom = pl.pallas_call(
        middle_kernel,
        out_shape=[
            jax.ShapeDtypeStruct((tokens, channels), BF16),
            jax.ShapeDtypeStruct((tokens // 4, wide), BF16),
            jax.ShapeDtypeStruct((line // 2, wide), BF16),
            jax.ShapeDtypeStruct((line // 2, wide), BF16),
        ],
        in_specs=[WHOLE] * 8 + [APART] * 11,
        out_specs=[WHOLE] * 4,
        scratch_shapes=shifted_scratch(quad_rows, quad_cols, channels)
        + [fine_scratch, coarse_scratch] + weight_scratch(fine_weights)
        + [pltpu.VMEM(merge_order.shape, BF16), pltpu.VMEM(merge_weight.shape, BF16)]
        + weight_scratch(coarse_weights) + [dma((10,)), dma((4 * steps,))],
        compiler_params=pltpu.CompilerParams(vmem_limit_bytes=32 << 20),
        name="fine_shifted_coarse_plain",
    )(
        *halo(first.reshape(quad_rows, quad_cols, QP, channels), top, bottom),
        fine_gains, merge_gain.reshape(4, channels), coarse_gains, bias_middle, *fine_weights,
        merge_order, merge_weight, *coarse_weights,
    )

    expand_order = expand_table(rows, cols)
    out = pl.pallas_call(
        last_kernel,
        out_shape=jax.ShapeDtypeStruct((LEVELS * rows * cols, channels), BF16),
        in_specs=[WHOLE] * 8 + [APART] * 7,
        out_specs=WHOLE,
        scratch_shapes=shifted_scratch(quad_rows // 2, quad_cols // 2, wide)
        + [coarse_scratch] + weight_scratch(coarse_weights)
        + [pltpu.VMEM(expand_weight.shape, BF16), pltpu.VMEM(expand_order.shape, BF16)]
        + [dma((6,)), dma((2 * steps,))],
        compiler_params=pltpu.CompilerParams(vmem_limit_bytes=28 << 20),
        name="coarse_shifted_expand",
    )(
        *halo(coarse.reshape(quad_rows // 2, quad_cols // 2, QP, wide), top, bottom),
        coarse_gains, parts, expand_gain[None], bias_last, *coarse_weights,
        expand_weight, expand_order,
    )
    return out.reshape(fields.shape)


def solution(mesh):
    grid = P(None, "lat", LON, None)
    return jax.shard_map(
        on_device,
        mesh=mesh,
        in_specs=(grid, P("lat", LON)) + (P(),) * 18,
        out_specs=grid,
        check_vma=False,
    )
```

time: 130 us -> 96.2 us (0.74)
  Pallas kernels: 93.5 us -> 55.3 us
  local copies, waits for them, and re-layouts: 13.1 us -> 17.7 us
  waiting for transfers between devices: 6.85 us -> 5.27 us
    pallas_call x5 -> x4, Pallas kernels: 73.7 us -> 34.6 us  [the longest x3 26.4 us: bias_of(): pl.pallas_call(functools.partial(bias_kernel, picks=tuple((b for _, b in...]
    unnamed x53 -> x75, local copies, waits for them, and re-layouts: 12.3 us -> 17.6 us
    ppermute x2, waiting for transfers between devices: 3.49 us -> 0.01 us  [halo(): from_east = lax.ppermute(side(0), LON, west)]
    ppermute x4, waiting for transfers between devices: 2.56 us -> 5.26 us  [the longest x2 4.65 us: halo(): north = lax.ppermute(bottom, 'lat', down)]
    ppermute x2, starting transfers between devices: 1.49 us -> 0.06 us  [halo(): from_east = lax.ppermute(side(0), LON, west)]
    concatenate x4, other arithmetic: 0.1 us -> 1.42 us  [side(): return jnp.concatenate([north[c:c + 1], own[:, c], south[c:c + 1]], axis=0)]
    pallas_call x1, Pallas kernels: 12.2 us -> 13.5 us  [on_device(): pl.pallas_call(middle_kernel, out_shape=[jax.ShapeDtypeStruct((tokens, ch...]
  transfers between devices with their start and end apart: 8 -> 8, of which waited for: 3 -> 3; matrix products, arithmetic and copies ran while one was open for 1% -> 1% of each run, Pallas kernels for 41% -> 22%
where the time goes in v2:
time: 96.2 us; the launch traced here: 95.6 us
  Pallas kernels  55.3 us (57%)
  local copies, waits for them, and re-layouts  17.7 us (18%)
  starting transfers between devices  15.3 us (16%)
  waiting for transfers between devices  5.27 us (5%)
  other arithmetic  1.42 us (1%)
    pallas_call x3, Pallas kernels, bias_of(): pl.pallas_call(functools.partial(bias_kernel, picks=tuple((b for _, b in...  26.4 us
    unnamed x75, local copies, waits for them, and re-layouts  17.6 us
    pallas_call x1, Pallas kernels, on_device(): pl.pallas_call(middle_kernel, out_shape=[jax.ShapeDtypeStruct((tokens, ch...  13.5 us
    pallas_call x1, Pallas kernels, on_device(): pl.pallas_call(first_kernel, out_shape=[jax.ShapeDtypeStruct((tokens, cha...  8.15 us
    pallas_call x1, Pallas kernels, on_device(): pl.pallas_call(last_kernel, out_shape=jax.ShapeDtypeStruct((LEVELS * rows...  7.28 us
    ppermute x2, starting transfers between devices, halo(): south = lax.ppermute(top, 'lat', up)  7.16 us
    ppermute x2, waiting for transfers between devices, halo(): north = lax.ppermute(bottom, 'lat', down)  4.65 us
    ppermute x2, starting transfers between devices, halo(): from_west = lax.ppermute(side(cols - 1), LON, east)  4.3 us
  transfers between devices with their start and end apart: 8, of which 3 were waited for; matrix products, arithmetic and copies ran while one was open for 1% of the time, Pallas kernels for 22%

profile of v2, /device:TPU:0, one launch (start us, length us, event | category | flops | bytes accessed | tf_op | source)
XLA Modules:
  0.0 95.6 jit_solution(9631447417873470969)
XLA Ops:
  0.0 1.3 %copy.27.narrow_hbm = bf16[2,768,192]{2,1,0:T(8,128)(2,1)S(1)} copy(bf16[2,768,192]{1,2,0:T(8,128)(2,1)} %param.35) | data formatting | bytes 1179648 | tf_op args[9]
  1.3 0.0 copy-start.28
  1.3 0.9 copy-done.28
  2.3 0.9 copy-done.30
  3.2 0.9 copy-done.33
  4.1 0.0 copy-start.18
  4.1 0.0 copy-start.19
  4.1 0.0 copy-start.20
  4.1 0.0 copy-start.22
  4.1 0.0 copy-start.23
  4.1 0.0 copy-start.24
  4.1 5.9 %bias_table.3 = f32[2,1280,128]{2,1,0:T(8,128)S(1)} custom-call(s32[144,144]{1,0:T(8,128)S(1)} %copy-done.30, bf16[160,144]{1,0:T(8,128)(2,1)S(1)} %copy-done.33, f32[6,2,3312]{2,1,0:T(2,128)S(1)} %bitcast.55), custom_call_target="tpu_custom_call" | custom-call | flops 10905190400 | bytes 1048576 | tf_op jit(solution)/shard_map/bias_table/pallas_call | solution.py:236
  10.0 0.0 copy-done.5
  10.0 0.0 copy-done.8
  10.0 0.0 copy-done.10
  10.0 0.0 copy-done.12
  10.1 0.0 copy-done.18
  10.1 0.0 copy-done.19
  10.1 0.0 copy-done.20
  10.1 0.0 copy-start.26
  10.1 0.0 copy-start.29
  10.1 0.0 copy-start.31
  10.1 0.0 copy-start.34
  10.2 8.1 %fine_plain.1 = (bf16[640,192]{1,0:T(8,128)(2,1)S(1)}, bf16[160,192]{1,0:T(8,128)(2,1)S(1)}, bf16[160,192]{1,0:T(8,128)(2,1)S(1)}) custom-call(bf16[576,192]{1,0:T(8,128)(2,1)S(1)} %bitcast.44, s32[12,24]{1,0:T(8,128)S(1)} %copy-done.23, f32[1,192]{1,0:T(1,128)S(1)} %bitcast.51, bf16[640,576]{1,0:T(8,128)(2,1)S(1)} %copy-done.10, ...), custom_call_target="tpu_custom_call" | custom-call | tf_op jit(solution)/shard_map/fine_plain/pallas_call | solution.py:579
  18.3 3.0 %collective-permute-start = (bf16[4,40,192]{2,1,0:T(8,128)(2,1)S(1)}, bf16[4,40,192]{2,1,0:T(8,128)(2,1)S(1)}, u32[]{:S(2)}, u32[]{:S(2)}) collective-permute-start(bf16[4,40,192]{2,1,0:T(8,128)(2,1)S(1)} %bitcast.58), channel_id=1, source_target_pairs={{0,2},{2,4},{4,6},{6,8},{8,10},{10,12},{12,14},{14,0},{1,3},{3,5},... | collective-permute-start | bytes 184328 | tf_op jit(solution)/shard_map/ppermute | solution.py:532
  21.3 3.1 %collective-permute-start.1 = (bf16[4,40,192]{2,1,0:T(8,128)(2,1)S(1)}, bf16[4,40,192]{2,1,0:T(8,128)(2,1)S(1)}, u32[]{:S(2)}, u32[]{:S(2)}) collective-permute-start(bf16[4,40,192]{2,1,0:T(8,128)(2,1)S(1)} %bitcast.57), channel_id=1, source_target_pairs={{2,0},{4,2},{6,4},{8,6},{10,8},{12,10},{14,12},{0,14},{3,1},{5,3},... | collective-permute-start | bytes 184328 | tf_op jit(solution)/shard_map/ppermute | solution.py:533
  24.5 2.5 %collective-permute-done = bf16[4,40,192]{2,1,0:T(8,128)(2,1)S(1)} collective-permute-done((bf16[4,40,192]{2,1,0:T(8,128)(2,1)S(1)}, bf16[4,40,192]{2,1,0:T(8,128)(2,1)S(1)}, u32[]{:S(2)}, u32[]{:S(2)}) %collective-permute-start) | collective-permute-done | bytes 61472 | tf_op jit(solution)/shard_map/ppermute | solution.py:532
  26.9 0.6 collective-permute-done.1
  27.5 0.7 pad_maximum_fusion.1
  28.2 0.0 collective-permute-start.3
  28.2 0.7 pad_maximum_fusion
  28.9 2.0 %collective-permute-start.2 = (bf16[6,40,192]{2,1,0:T(8,128)(2,1)}, bf16[6,40,192]{2,1,0:T(8,128)(2,1)}, u32[]{:S(2)}, u32[]{:S(2)}) collective-permute-start(bf16[6,40,192]{2,1,0:T(8,128)(2,1)} %pad_maximum_fusion), channel_id=1, source_target_pairs={{0,1},{1,16},{16,17},{17,0},{2,3},{3,18},{18,19},{19,2},{4,5},{5,2... | collective-permute-start | bytes 276488 | tf_op jit(solution)/shard_map/ppermute | solution.py:538
  31.0 0.0 copy-start.36
  31.0 0.0 copy-start
  31.0 0.0 copy-start.21
  31.0 12.2 %bias_table.4 = f32[2,3840,128]{2,1,0:T(8,128)S(1)} custom-call(s32[144,144]{1,0:T(8,128)S(1)} %copy-done.31, bf16[160,144]{1,0:T(8,128)(2,1)S(1)} %copy-done.34, f32[6,2,3312]{2,1,0:T(2,128)S(1)} %bitcast.56, f32[12,2,3312]{2,1,0:T(2,128)S(1)} %bitcast.53), custom_call_target="tpu_custom_call" | custom-call | flops 32715571200 | bytes 1048576 | tf_op jit(solution)/shard_map/bias_table/pallas_call | solution.py:236
  43.3 1.9 %copy-done.3 = f32[2,3840,128]{2,1,0:T(8,128)} copy-done((f32[2,3840,128]{2,1,0:T(8,128)}, f32[2,3840,128]{2,1,0:T(8,128)S(1)}, u32[]{:S(2)}) %copy-start.3) | copy-done | bytes 3932184
  45.1 0.1 reshape.69.merge_gain_ref
  45.2 0.0 collective-permute-done.3
  45.2 0.0 collective-permute-done.2
  45.2 0.0 copy-start.1
  45.3 1.7 %copy-done.1 = bf16[2,1536,384]{2,1,0:T(8,128)(2,1)S(1)} copy-done((bf16[2,1536,384]{2,1,0:T(8,128)(2,1)S(1)}, bf16[2,1536,384]{2,1,0:T(8,128)(2,1)}, u32[]{:S(2)}) %copy-start.1) | copy-done | bytes 2359320
  46.9 1.5 %copy-done.2 = bf16[2,384,1152]{2,1,0:T(8,128)(2,1)S(1)} copy-done((bf16[2,384,1152]{2,1,0:T(8,128)(2,1)S(1)}, bf16[2,384,1152]{2,1,0:T(8,128)(2,1)}, u32[]{:S(2)}) %copy-start.2) | copy-done | bytes 1769496
  48.4 2.1 %copy-done.4 = f32[2,3840,128]{2,1,0:T(8,128)S(1)} copy-done((f32[2,3840,128]{2,1,0:T(8,128)S(1)}, f32[2,3840,128]{2,1,0:T(8,128)}, u32[]{:S(2)}) %copy-start.4) | copy-done | bytes 3932184
  50.5 1.1 %copy-done.6 = bf16[2,192,768]{2,1,0:T(8,128)(2,1)S(1)} copy-done((bf16[2,192,768]{2,1,0:T(8,128)(2,1)S(1)}, bf16[2,192,768]{2,1,0:T(8,128)(2,1)}, u32[]{:S(2)}) %copy-start.6) | copy-done | bytes 589848
  51.6 1.1 %copy-done.7 = bf16[2,384,384]{2,1,0:T(8,128)(2,1)S(1)} copy-done((bf16[2,384,384]{2,1,0:T(8,128)(2,1)S(1)}, bf16[2,384,384]{2,1,0:T(8,128)(2,1)}, u32[]{:S(2)}) %copy-start.7) | copy-done | bytes 589848
  52.6 1.0 %copy-done.9 = bf16[2,192,576]{2,1,0:T(8,128)(2,1)S(1)} copy-done((bf16[2,192,576]{2,1,0:T(8,128)(2,1)S(1)}, bf16[2,192,576]{2,1,0:T(8,128)(2,1)}, u32[]{:S(2)}) %copy-start.9) | copy-done | bytes 442392
  53.7 1.1 %copy-done.11 = bf16[640,640]{1,0:T(8,128)(2,1)S(1)} copy-done((bf16[640,640]{1,0:T(8,128)(2,1)S(1)}, bf16[640,640]{1,0:T(8,128)(2,1)}, u32[]{:S(2)}) %copy-start.11) | copy-done | bytes 819224
  54.8 1.0 %copy-done.15 = bf16[640,192]{1,0:T(8,128)(2,1)S(1)} copy-done((bf16[640,192]{1,0:T(8,128)(2,1)S(1)}, bf16[640,192]{1,0:T(8,128)(2,1)}, u32[]{:S(2)}) %copy-start.15) | copy-done | bytes 245784
  55.8 1.1 %copy-done.16 = bf16[768,384]{1,0:T(8,128)(2,1)S(1)} copy-done((bf16[768,384]{1,0:T(8,128)(2,1)S(1)}, bf16[768,384]{1,0:T(8,128)(2,1)}, u32[]{:S(2)}) %copy-start.16) | copy-done | bytes 589848
  56.8 13.5 %fine_shifted_coarse_plain.1 = (bf16[640,192]{1,0:T(8,128)(2,1)S(1)}, bf16[160,384]{1,0:T(8,128)(2,1)S(1)}, bf16[80,384]{1,0:T(8,128)(2,1)S(1)}, bf16[80,384]{1,0:T(8,128)(2,1)S(1)}) custom-call(bf16[640,192]{1,0:T(8,128)(2,1)S(1)} %copy-done.15, bf16[160,192]{1,0:T(8,128)(2,1)S(1)} %bitcast.47, bf16[160,192]{1,0:T(8,128)(2,1)S(1)} %bitcast.48, ...), custom_call_target="tpu_custom_call" | custom-call | tf_op jit(solution)/shard_map/fine_shifted_coarse_plain/pallas_call | solution.py:598
  70.3 0.7 collective-permute-start.4
  71.1 4.1 %collective-permute-start.5 = (bf16[2,40,384]{2,1,0:T(8,128)(2,1)S(1)}, bf16[2,40,384]{2,1,0:T(8,128)(2,1)S(1)}, u32[]{:S(2)}, u32[]{:S(2)}) collective-permute-start(bf16[2,40,384]{2,1,0:T(8,128)(2,1)S(1)} %bitcast.59), channel_id=1, source_target_pairs={{2,0},{4,2},{6,4},{8,6},{10,8},{12,10},{14,12},{0,14},{3,1},{5,3},... | collective-permute-start | bytes 184328 | tf_op jit(solution)/shard_map/ppermute | solution.py:533
  75.1 2.2 %collective-permute-done.4 = bf16[2,40,384]{2,1,0:T(8,128)(2,1)S(1)} collective-permute-done((bf16[2,40,384]{2,1,0:T(8,128)(2,1)S(1)}, bf16[2,40,384]{2,1,0:T(8,128)(2,1)S(1)}, u32[]{:S(2)}, u32[]{:S(2)}) %collective-permute-start.4) | collective-permute-done | bytes 61472 | tf_op jit(solution)/shard_map/ppermute | solution.py:532
  77.3 0.0 collective-permute-done.5
  77.4 0.1 collective-permute-start.7
  77.5 0.0 copy-start.13
  77.5 0.0 copy-start.17
  77.5 0.0 copy-start.25
  77.5 2.3 %collective-permute-start.6 = (bf16[4,40,384]{2,1,0:T(8,128)(2,1)S(1)}, bf16[4,40,384]{2,1,0:T(8,128)(2,1)S(1)}, u32[]{:S(2)}, u32[]{:S(2)}) collective-permute-start(bf16[4,40,384]{2,1,0:T(8,128)(2,1)S(1)} %pad_maximum_fusion.2), channel_id=1, source_target_pairs={{0,1},{1,16},{16,17},{17,0},{2,3},{3,18},{18,19},{19,2},{4,5},{5,2... | collective-permute-start | bytes 368648 | tf_op jit(solution)/shard_map/ppermute | solution.py:538
  79.8 8.3 %bias_table.5 = f32[2,2560,128]{2,1,0:T(8,128)S(1)} custom-call(s32[144,144]{1,0:T(8,128)S(1)} %copy-done.32, bf16[160,144]{1,0:T(8,128)(2,1)S(1)} %copy-done.35, f32[12,2,3312]{2,1,0:T(2,128)S(1)} %bitcast.54), custom_call_target="tpu_custom_call" | custom-call | flops 21810380800 | bytes 1048576 | tf_op jit(solution)/shard_map/bias_table/pallas_call | solution.py:236
  88.1 0.0 collective-permute-done.7
  88.1 0.0 collective-permute-done.6
  88.2 7.3 %coarse_shifted_expand.1 = bf16[576,192]{1,0:T(8,128)(2,1)} custom-call(bf16[160,384]{1,0:T(8,128)(2,1)S(1)} %get-tuple-element.15.own_ref, bf16[80,384]{1,0:T(8,128)(2,1)S(1)} %bitcast.45, bf16[80,384]{1,0:T(8,128)(2,1)S(1)} %bitcast.46, bf16[160,384]{1,0:T(8,128)(2,1)S(1)} %bitcast.50, bf16[160,384]{1,0:T(8,128)(2,1)S(1)} %bitcast.49, ...), custom_call_target="tpu_custom_call" | custom-call | tf_op jit(solution)/shard_map/coarse_shifted_expand/pallas_call | solution.py:621
  (44 shorter events, 0.2 us)
Async XLA Ops:
  1.3 0.9 copy-start.28
  2.3 0.9 copy-start.30
  3.2 0.9 copy-start.33
  4.1 6.0 %copy-start.5 = (bf16[2,192,768]{2,1,0:T(8,128)(2,1)S(1)}, bf16[2,192,768]{2,1,0:T(8,128)(2,1)}, u32[]{:S(2)}) copy-start(bf16[2,192,768]{2,1,0:T(8,128)(2,1)} %widen_hbm.4) | copy-start | bytes 1769476
  4.1 6.0 %copy-start.8 = (bf16[2,192,576]{2,1,0:T(8,128)(2,1)S(1)}, bf16[2,192,576]{2,1,0:T(8,128)(2,1)}, u32[]{:S(2)}) copy-start(bf16[2,192,576]{2,1,0:T(8,128)(2,1)} %triple_hbm.4) | copy-start | bytes 1327108
  4.1 6.0 %copy-start.10 = (bf16[640,576]{1,0:T(8,128)(2,1)S(1)}, bf16[640,576]{1,0:T(8,128)(2,1)}, u32[]{:S(2)}) copy-start(bf16[640,576]{1,0:T(8,128)(2,1)} %constant.13.clone.order_hbm) | copy-start | bytes 2211844
  4.1 6.0 %copy-start.12 = (bf16[2,192,192]{2,1,0:T(8,128)(2,1)S(1)}, bf16[2,192,192]{2,1,0:T(8,128)(2,1)}, u32[]{:S(2)}) copy-start(bf16[2,192,192]{2,1,0:T(8,128)(2,1)} %project_hbm.4) | copy-start | bytes 442372
  4.1 6.0 %copy-start.18 = (bf16[2,12,24,192]{3,2,1,0:T(8,128)(2,1)S(1)}, bf16[2,12,24,192]{3,2,1,0:T(8,128)(2,1)}, u32[]{:S(2)}) copy-start(bf16[2,12,24,192]{3,2,1,0:T(8,128)(2,1)} %param.26) | copy-start | bytes 663556
  4.1 6.0 %copy-start.19 = (bf16[640,12]{1,0:T(8,128)(2,1)S(1)}, bf16[640,12]{1,0:T(8,128)(2,1)}, u32[]{:S(2)}) copy-start(bf16[640,12]{1,0:T(8,128)(2,1)} %constant.14.clone.of_row_ref) | copy-start | bytes 46084
  4.1 6.0 %copy-start.20 = (bf16[640,24]{1,0:T(8,128)(2,1)S(1)}, bf16[640,24]{1,0:T(8,128)(2,1)}, u32[]{:S(2)}) copy-start(bf16[640,24]{1,0:T(8,128)(2,1)} %constant.15.clone.of_col_ref) | copy-start | bytes 92164
  4.1 6.0 %copy-start.22 = (f32[2,2,192]{2,1,0:T(2,128)S(1)}, f32[2,2,192]{2,1,0:T(2,128)}, u32[]{:S(2)}) copy-start(f32[2,2,192]{2,1,0:T(2,128)} %gains_ref.4) | copy-start | bytes 9220
  4.1 6.0 %copy-start.23 = (s32[12,24]{1,0:T(8,128)S(1)}, s32[12,24]{1,0:T(8,128)}, u32[]{:S(2)}) copy-start(s32[12,24]{1,0:T(8,128)} %land_ref.1) | copy-start | bytes 3460
  4.1 6.0 %copy-start.24 = (f32[192]{0:T(256)S(1)}, f32[192]{0:T(256)}, u32[]{:S(2)}) copy-start(f32[192]{0:T(256)} %param.28) | copy-start | bytes 2308
  10.1 20.8 %copy-start.26 = (f32[2,12,3312]{2,0,1:T(2,128)S(1)}, f32[2,12,3312]{2,0,1:T(2,128)}, u32[]{:S(2)}) copy-start(f32[2,12,3312]{2,0,1:T(2,128)} %param.38) | copy-start | bytes 953860
  10.1 20.8 %copy-start.29 = (f32[2,6,3312]{2,0,1:T(2,128)S(1)}, f32[2,6,3312]{2,0,1:T(2,128)}, u32[]{:S(2)}) copy-start(f32[2,6,3312]{2,0,1:T(2,128)} %param.30) | copy-start | bytes 476932
  10.1 20.8 %copy-start.31 = (s32[144,144]{1,0:T(8,128)S(1)}, s32[144,144]{1,0:T(8,128)}, u32[]{:S(2)}) copy-start(s32[144,144]{1,0:T(8,128)} %index_ref.5) | copy-start | bytes 248836
  10.1 20.8 %copy-start.34 = (bf16[160,144]{1,0:T(8,128)(2,1)S(1)}, bf16[160,144]{1,0:T(8,128)(2,1)}, u32[]{:S(2)}) copy-start(bf16[160,144]{1,0:T(8,128)(2,1)} %constant.12.clone.spread_ref) | copy-start | bytes 138244
  18.3 12.6 %copy-start.14 = (bf16[640,192]{1,0:T(8,128)(2,1)}, bf16[640,192]{1,0:T(8,128)(2,1)S(1)}, u32[]{:S(2)}) copy-start(bf16[640,192]{1,0:T(8,128)(2,1)S(1)} %get-tuple-element.12.own_ref) | copy-start | bytes 737284
  18.3 8.6 %collective-permute-start = (bf16[4,40,192]{2,1,0:T(8,128)(2,1)S(1)}, bf16[4,40,192]{2,1,0:T(8,128)(2,1)S(1)}, u32[]{:S(2)}, u32[]{:S(2)}) collective-permute-start(bf16[4,40,192]{2,1,0:T(8,128)(2,1)S(1)} %bitcast.58), channel_id=1, source_target_pairs={{0,2},{2,4},{4,6},{6,8},{8,10},{10,12},{12,14},{14,0},{1,3},{3,5},... | collective-permute-start | bytes 184328 | tf_op jit(solution)/shard_map/ppermute | solution.py:532
  21.3 6.2 %collective-permute-start.1 = (bf16[4,40,192]{2,1,0:T(8,128)(2,1)S(1)}, bf16[4,40,192]{2,1,0:T(8,128)(2,1)S(1)}, u32[]{:S(2)}, u32[]{:S(2)}) collective-permute-start(bf16[4,40,192]{2,1,0:T(8,128)(2,1)S(1)} %bitcast.57), channel_id=1, source_target_pairs={{2,0},{4,2},{6,4},{8,6},{10,8},{12,10},{14,12},{0,14},{3,1},{5,3},... | collective-permute-start | bytes 184328 | tf_op jit(solution)/shard_map/ppermute | solution.py:533
  28.2 17.0 %collective-permute-start.3 = (bf16[6,40,192]{2,1,0:T(8,128)(2,1)}, bf16[6,40,192]{2,1,0:T(8,128)(2,1)}, u32[]{:S(2)}, u32[]{:S(2)}) collective-permute-start(bf16[6,40,192]{2,1,0:T(8,128)(2,1)} %pad_maximum_fusion.1), channel_id=1, source_target_pairs={{1,0},{16,1},{17,16},{0,17},{3,2},{18,3},{19,18},{2,19},{5,4},{20,... | collective-permute-start | bytes 276488 | tf_op jit(solution)/shard_map/ppermute | solution.py:539
  28.9 16.3 %collective-permute-start.2 = (bf16[6,40,192]{2,1,0:T(8,128)(2,1)}, bf16[6,40,192]{2,1,0:T(8,128)(2,1)}, u32[]{:S(2)}, u32[]{:S(2)}) collective-permute-start(bf16[6,40,192]{2,1,0:T(8,128)(2,1)} %pad_maximum_fusion), channel_id=1, source_target_pairs={{0,1},{1,16},{16,17},{17,0},{2,3},{3,18},{18,19},{19,2},{4,5},{5,2... | collective-permute-start | bytes 276488 | tf_op jit(solution)/shard_map/ppermute | solution.py:538
  31.0 14.2 %copy-start.36 = (f32[768]{0:T(1024)S(1)}, f32[768]{0:T(1024)}, u32[]{:S(2)}) copy-start(f32[768]{0:T(1024)} %param.36) | copy-start | bytes 9220
  31.0 14.2 %copy-start = (bf16[2,384,1536]{2,1,0:T(8,128)(2,1)S(1)}, bf16[2,384,1536]{2,1,0:T(8,128)(2,1)}, u32[]{:S(2)}) copy-start(bf16[2,384,1536]{2,1,0:T(8,128)(2,1)} %widen_hbm.5) | copy-start | bytes 7077892
  31.0 14.2 %copy-start.21 = (f32[2,2,384]{2,1,0:T(2,128)S(1)}, f32[2,2,384]{2,1,0:T(2,128)}, u32[]{:S(2)}) copy-start(f32[2,2,384]{2,1,0:T(2,128)} %gains_ref.5) | copy-start | bytes 18436
  43.3 1.9 %copy-start.3 = (f32[2,3840,128]{2,1,0:T(8,128)}, f32[2,3840,128]{2,1,0:T(8,128)S(1)}, u32[]{:S(2)}) copy-start(f32[2,3840,128]{2,1,0:T(8,128)S(1)} %bias_table.4) | copy-start | bytes 11796484
  45.2 1.7 %copy-start.1 = (bf16[2,1536,384]{2,1,0:T(8,128)(2,1)S(1)}, bf16[2,1536,384]{2,1,0:T(8,128)(2,1)}, u32[]{:S(2)}) copy-start(bf16[2,1536,384]{2,1,0:T(8,128)(2,1)} %narrow_hbm.3) | copy-start | bytes 7077892
  46.9 1.5 %copy-start.2 = (bf16[2,384,1152]{2,1,0:T(8,128)(2,1)S(1)}, bf16[2,384,1152]{2,1,0:T(8,128)(2,1)}, u32[]{:S(2)}) copy-start(bf16[2,384,1152]{2,1,0:T(8,128)(2,1)} %triple_hbm.5) | copy-start | bytes 5308420
  48.4 2.1 %copy-start.4 = (f32[2,3840,128]{2,1,0:T(8,128)S(1)}, f32[2,3840,128]{2,1,0:T(8,128)}, u32[]{:S(2)}) copy-start(f32[2,3840,128]{2,1,0:T(8,128)} %copy-done.3) | copy-start | bytes 11796484
  50.5 1.1 %copy-start.6 = (bf16[2,192,768]{2,1,0:T(8,128)(2,1)S(1)}, bf16[2,192,768]{2,1,0:T(8,128)(2,1)}, u32[]{:S(2)}) copy-start(bf16[2,192,768]{2,1,0:T(8,128)(2,1)} %widen_hbm.4) | copy-start | bytes 1769476
  51.6 1.1 %copy-start.7 = (bf16[2,384,384]{2,1,0:T(8,128)(2,1)S(1)}, bf16[2,384,384]{2,1,0:T(8,128)(2,1)}, u32[]{:S(2)}) copy-start(bf16[2,384,384]{2,1,0:T(8,128)(2,1)} %project_hbm.5) | copy-start | bytes 1769476
  52.6 1.0 %copy-start.9 = (bf16[2,192,576]{2,1,0:T(8,128)(2,1)S(1)}, bf16[2,192,576]{2,1,0:T(8,128)(2,1)}, u32[]{:S(2)}) copy-start(bf16[2,192,576]{2,1,0:T(8,128)(2,1)} %triple_hbm.4) | copy-start | bytes 1327108
  53.7 1.1 %copy-start.11 = (bf16[640,640]{1,0:T(8,128)(2,1)S(1)}, bf16[640,640]{1,0:T(8,128)(2,1)}, u32[]{:S(2)}) copy-start(bf16[640,640]{1,0:T(8,128)(2,1)} %constant.16.clone.merge_order_hbm) | copy-start | bytes 2457604
  54.8 1.0 %copy-start.15 = (bf16[640,192]{1,0:T(8,128)(2,1)S(1)}, bf16[640,192]{1,0:T(8,128)(2,1)}, u32[]{:S(2)}) copy-start(bf16[640,192]{1,0:T(8,128)(2,1)} %copy-done.14) | copy-start | bytes 737284
  55.8 1.1 %copy-start.16 = (bf16[768,384]{1,0:T(8,128)(2,1)S(1)}, bf16[768,384]{1,0:T(8,128)(2,1)}, u32[]{:S(2)}) copy-start(bf16[768,384]{1,0:T(8,128)(2,1)} %merge_weight_hbm.1) | copy-start | bytes 1769476
  56.8 22.9 %copy-start.27 = (f32[2,12,3312]{2,0,1:T(2,128)S(1)}, f32[2,12,3312]{2,0,1:T(2,128)}, u32[]{:S(2)}) copy-start(f32[2,12,3312]{2,0,1:T(2,128)} %param.38) | copy-start | bytes 953860
  56.8 22.9 %copy-start.32 = (s32[144,144]{1,0:T(8,128)S(1)}, s32[144,144]{1,0:T(8,128)}, u32[]{:S(2)}) copy-start(s32[144,144]{1,0:T(8,128)} %index_ref.5) | copy-start | bytes 248836
  56.8 22.9 %copy-start.35 = (bf16[160,144]{1,0:T(8,128)(2,1)S(1)}, bf16[160,144]{1,0:T(8,128)(2,1)}, u32[]{:S(2)}) copy-start(bf16[160,144]{1,0:T(8,128)(2,1)} %constant.12.clone.spread_ref) | copy-start | bytes 138244
  70.3 7.0 %collective-permute-start.4 = (bf16[2,40,384]{2,1,0:T(8,128)(2,1)S(1)}, bf16[2,40,384]{2,1,0:T(8,128)(2,1)S(1)}, u32[]{:S(2)}, u32[]{:S(2)}) collective-permute-start(bf16[2,40,384]{2,1,0:T(8,128)(2,1)S(1)} %bitcast.60), channel_id=1, source_target_pairs={{0,2},{2,4},{4,6},{6,8},{8,10},{10,12},{12,14},{14,0},{1,3},{3,5},... | collective-permute-start | bytes 184328 | tf_op jit(solution)/shard_map/ppermute | solution.py:532
  71.1 6.3 %collective-permute-start.5 = (bf16[2,40,384]{2,1,0:T(8,128)(2,1)S(1)}, bf16[2,40,384]{2,1,0:T(8,128)(2,1)S(1)}, u32[]{:S(2)}, u32[]{:S(2)}) collective-permute-start(bf16[2,40,384]{2,1,0:T(8,128)(2,1)S(1)} %bitcast.59), channel_id=1, source_target_pairs={{2,0},{4,2},{6,4},{8,6},{10,8},{12,10},{14,12},{0,14},{3,1},{5,3},... | collective-permute-start | bytes 184328 | tf_op jit(solution)/shard_map/ppermute | solution.py:533
  77.4 10.7 %collective-permute-start.7 = (bf16[4,40,384]{2,1,0:T(8,128)(2,1)S(1)}, bf16[4,40,384]{2,1,0:T(8,128)(2,1)S(1)}, u32[]{:S(2)}, u32[]{:S(2)}) collective-permute-start(bf16[4,40,384]{2,1,0:T(8,128)(2,1)S(1)} %pad_maximum_fusion.3), channel_id=1, source_target_pairs={{1,0},{16,1},{17,16},{0,17},{3,2},{18,3},{19,18},{2,19},{5,4},{20,... | collective-permute-start | bytes 368648 | tf_op jit(solution)/shard_map/ppermute | solution.py:539
  77.5 10.7 %copy-start.13 = (bf16[576,640]{1,0:T(8,128)(2,1)S(1)}, bf16[576,640]{1,0:T(8,128)(2,1)}, u32[]{:S(2)}) copy-start(bf16[576,640]{1,0:T(8,128)(2,1)} %constant.17.clone.expand_order_hbm) | copy-start | bytes 2211844
  77.5 10.7 %copy-start.17 = (bf16[384,768]{1,0:T(8,128)(2,1)S(1)}, bf16[384,768]{1,0:T(8,128)(2,1)}, u32[]{:S(2)}) copy-start(bf16[384,768]{1,0:T(8,128)(2,1)} %expand_weight_hbm.1) | copy-start | bytes 1769476
  77.5 10.7 %copy-start.25 = (f32[192]{0:T(256)S(1)}, f32[192]{0:T(256)}, u32[]{:S(2)}) copy-start(f32[192]{0:T(256)} %param.45) | copy-start | bytes 2308
  77.5 10.6 %collective-permute-start.6 = (bf16[4,40,384]{2,1,0:T(8,128)(2,1)S(1)}, bf16[4,40,384]{2,1,0:T(8,128)(2,1)S(1)}, u32[]{:S(2)}, u32[]{:S(2)}) collective-permute-start(bf16[4,40,384]{2,1,0:T(8,128)(2,1)S(1)} %pad_maximum_fusion.2), channel_id=1, source_target_pairs={{0,1},{1,16},{16,17},{17,0},{2,3},{3,18},{18,19},{19,2},{4,5},{5,2... | collective-permute-start | bytes 368648 | tf_op jit(solution)/shard_map/ppermute | solution.py:538

commit v3 on v2

--- a/solution.py
+++ b/solution.py
@@ -23,6 +23,7 @@
 LO_COUNT = 13
 LOG2E = 1.4426950408889634
 MASKED = -1e30
+VMEM_LIMIT = 60 << 20
 LON = ("sec", "head")
 F32 = jnp.float32
 BF16 = jnp.bfloat16
@@ -50,11 +51,15 @@
     return jnp.asarray(table.astype(jnp.bfloat16))
 
 
+def target_row(targets):
+    return jnp.asarray(np.array([-1 if t is None else t for t in targets], np.int32)[None])
+
+
 def fine_tables(rows, cols):
     slots = quad_sources(rows, cols)
-    order = one_hot(
-        [None if s is None else (s[0] * rows + s[1]) * cols + s[2] for s in slots],
-        LEVELS * rows * cols,
+    place = {s: n for n, s in enumerate(slots) if s is not None}
+    order = target_row(
+        [place[(level, r, c)] for level in range(LEVELS) for r in range(rows) for c in range(cols)]
     )
     of_row = one_hot([None if s is None else s[1] for s in slots], rows)
     of_col = one_hot([None if s is None else s[2] for s in slots], cols)
@@ -62,27 +67,35 @@
 
 
 def merge_table(rows, cols):
-    place = {s: n for n, s in enumerate(quad_sources(rows, cols)) if s is not None}
-    sources = []
-    for p in range(2):
-        for q in range(2):
-            for s in quad_sources(rows // 2, cols // 2):
-                sources.append(
-                    None if s is None else place[(s[0], 2 * s[1] + p, 2 * s[2] + q)]
-                )
-    return one_hot(sources, len(place) // QUAD * QP)
-
-
-def expand_table(rows, cols):
     coarse = quad_sources(rows // 2, cols // 2)
     place = {s: n for n, s in enumerate(coarse) if s is not None}
-    sources = []
-    for level in range(LEVELS):
-        for r in range(rows):
-            for c in range(cols):
-                part = (r % 2) * 2 + c % 2
-                sources.append(part * len(coarse) + place[(level, r // 2, c // 2)])
-    return one_hot(sources, 4 * len(coarse))
+    return target_row(
+        [
+            None
+            if s is None
+            else ((s[1] % 2) * 2 + s[2] % 2) * len(coarse) + place[(s[0], s[1] // 2, s[2] // 2)]
+            for s in quad_sources(rows, cols)
+        ]
+    )
+
+
+def expand_table(rows, cols):
+    return target_row(
+        [
+            None
+            if s is None
+            else (s[0] * rows + 2 * s[1] + p) * cols + 2 * s[2] + q
+            for p in range(2)
+            for q in range(2)
+            for s in quad_sources(rows // 2, cols // 2)
+        ]
+    )
+
+
+def sent_to(target_ref, count):
+    width = target_ref.shape[1]
+    slot = lax.broadcasted_iota(jnp.int32, (count, width), 0)
+    return jnp.where(slot == target_ref[...], 1.0, 0.0).astype(BF16)
 
 
 def dot(a, b):
@@ -148,7 +161,8 @@
     middle = (x + dot(context, w_project)).astype(BF16).astype(F32)
     second = norm(middle, gain).astype(BF16)
     hidden = gelu(dot(second, w_widen)).astype(BF16)
-    return (middle + dot(hidden, w_narrow)).astype(BF16)
+    narrow = dot if w_narrow.shape[0] > w_narrow.shape[1] else dot_t
+    return (middle + narrow(hidden, w_narrow)).astype(BF16)
 
 
 def padded(heads):
@@ -244,7 +258,7 @@
             pltpu.VMEM((WP, WP), jnp.int32),
             pltpu.VMEM((rows * LO_COUNT, 512), BF16),
         ],
-        compiler_params=pltpu.CompilerParams(vmem_limit_bytes=16 << 20),
+        compiler_params=pltpu.CompilerParams(vmem_limit_bytes=VMEM_LIMIT),
         cost_estimate=pl.CostEstimate(flops=2 * flops, bytes_accessed=1 << 20, transcendentals=0),
         name="bias_table",
     )(index, spread, *tables)
@@ -278,55 +292,52 @@
 
 
 def first_kernel(
-    fields_ref, land_ref, embed_ref, order_hbm, of_row_ref, of_col_ref, bias_hbm,
-    gains_ref, triple_hbm, project_hbm, widen_hbm, narrow_hbm,
+    fields_ref, land_ref, embed_ref, order_ref, of_row_ref, of_col_ref, gains_ref,
+    bias_hbm, triple_hbm, project_hbm, widen_hbm, narrow_hbm,
     out_ref, top_ref, bottom_ref,
-    start_ref, order, bias, w_triple, w_project, w_widen, w_narrow, sems, bias_sems,
+    context, bias, w_triple, w_project, w_widen, w_narrow, sems, bias_sems,
 ):
     channels = fields_ref.shape[1]
     fetched = Fetched(
-        [[pltpu.make_async_copy(order_hbm, order, sems.at[0])],
-         bias_copies(bias_hbm, bias, 0, bias_sems, 0)]
-        + [
-            [pltpu.make_async_copy(source.at[0], target, sems.at[1 + n])]
-            for n, (source, target) in enumerate(
-                [(triple_hbm, w_triple), (project_hbm, w_project),
-                 (widen_hbm, w_widen), (narrow_hbm, w_narrow)]
-            )
-        ]
+        block_copies(
+            [(triple_hbm, w_triple), (project_hbm, w_project),
+             (widen_hbm, w_widen), (narrow_hbm, w_narrow)], 0, sems, 0,
+        )
+        + [bias_copies(bias_hbm, bias, 0, bias_sems, 0)]
     )
     land = land_ref[...].astype(F32).astype(BF16)
     on_row = dot(of_row_ref[...], land)
     on_land = jnp.sum(on_row * of_col_ref[...].astype(F32), axis=-1, keepdims=True)
+    rows = out_ref.shape[0]
+    start = dot(sent_to(order_ref, rows), fields_ref[...]) + on_land * embed_ref[...]
+    x = start.astype(BF16).astype(F32)
+    normed = norm(x, gains_ref[0, 0:1]).astype(BF16)
     fetched.wait(0)
-    start = dot(order[...], fields_ref[...]) + on_land * embed_ref[...]
-    start_ref[...] = start.astype(BF16).astype(F32)
-    fetched.wait(1, 2, 3, 4, 5)
-    rows = out_ref.shape[0]
+    triple = dot(normed, w_triple[...]).astype(BF16)
+    fetched.wait(4)
     inner = top_ref.shape[0]
-    down = rows // inner // 2
-    for a in range(down):
+    for a in range(rows // inner // 2):
         for b in range(inner // QP // 2):
             top = 2 * a * inner + 2 * b * QP
             below = top + inner
-            x = jnp.concatenate(
-                [start_ref[top : top + 2 * QP], start_ref[below : below + 2 * QP]], axis=0
+            window = jnp.concatenate(
+                [triple[top : top + 2 * QP], triple[below : below + 2 * QP]], axis=0
             )
-            normed = norm(x, gains_ref[0, 0:1]).astype(BF16)
-            triple = dot(normed, w_triple[...]).astype(BF16)
-            context = attend(
-                triple[:, :channels],
-                triple[:, channels : 2 * channels],
-                triple[:, 2 * channels :],
+            mixed = attend(
+                window[:, :channels],
+                window[:, channels : 2 * channels],
+                window[:, 2 * channels :],
                 bias, 0, None,
             ).astype(BF16)
-            done = finish(
-                x, context, gains_ref[0, 1:2], w_project[...], w_widen[...], w_narrow[...]
-            )
-            out_ref[top : top + 2 * QP] = done[: 2 * QP]
-            out_ref[below : below + 2 * QP] = done[2 * QP :]
-    top_ref[...] = out_ref[:inner]
-    bottom_ref[...] = out_ref[rows - inner :]
+            context[top : top + 2 * QP] = mixed[: 2 * QP]
+            context[below : below + 2 * QP] = mixed[2 * QP :]
+    fetched.wait(1, 2, 3)
+    done = finish(
+        x, context[...], gains_ref[0, 1:2], w_project[...], w_widen[...], w_narrow[...]
+    )
+    out_ref[...] = done
+    top_ref[...] = done[:inner]
+    bottom_ref[...] = done[rows - inner :]
 
 
 def shifted_block(
@@ -334,11 +345,11 @@
     bias, w_triple, w_project, w_widen, w_narrow, query, key, value, context,
 ):
     channels = own_ref.shape[1]
-    fetched.wait(1)
     across = north_ref.shape[0] // QP
     down = own_ref.shape[0] // QP // across
     line = (across + 2) * QP
     inner = across * QP
+    pieces = []
     for i in range(down + 2):
         if i == 0:
             middle = north_ref[...]
@@ -346,20 +357,17 @@
             middle = south_ref[...]
         else:
             middle = own_ref[(i - 1) * inner : i * inner]
-        x = jnp.concatenate(
-            [
-                west_ref[i * QP : (i + 1) * QP].astype(F32),
-                middle.astype(F32),
-                east_ref[i * QP : (i + 1) * QP].astype(F32),
-            ],
-            axis=0,
-        )
-        normed = norm(x, gains_ref[1, 0:1]).astype(BF16)
-        triple = dot(normed, w_triple[...])
-        if 0 < i < down + 1:
-            query[(i - 1) * line : i * line] = triple[:, :channels]
-        key[i * line : (i + 1) * line] = triple[:, channels : 2 * channels].astype(BF16)
-        value[i * line : (i + 1) * line] = triple[:, 2 * channels :].astype(BF16)
+        pieces += [
+            west_ref[i * QP : (i + 1) * QP].astype(F32),
+            middle.astype(F32),
+            east_ref[i * QP : (i + 1) * QP].astype(F32),
+        ]
+    normed = norm(jnp.concatenate(pieces, axis=0), gains_ref[1, 0:1]).astype(BF16)
+    fetched.wait(1)
+    query[...] = dot(normed[line : (down + 1) * line], w_triple[:, :channels])
+    both = dot(normed, w_triple[:, channels:]).astype(BF16)
+    key[...] = both[:, :channels]
+    value[...] = both[:, channels:]
     lane = lax.broadcasted_iota(jnp.int32, (1, WP), 1)
     place = lax.axis_index("lat")
     on_top = jnp.where(place == 0, MASKED, 0.0).astype(F32)
@@ -397,17 +405,10 @@
                     to = ((2 * wa + r - 1) * across + 2 * wb + cols[0] - 1) * QP
                     context[to : to + size] = out[n * size : (n + 1) * size]
     fetched.wait(2, 3, 4)
-    outs = []
-    for at in range(0, own_ref.shape[0], WP):
-        outs.append(
-            finish(
-                own_ref[at : at + WP].astype(F32),
-                context[at : at + WP].astype(BF16),
-                gains_ref[1, 1:2],
-                w_project[...], w_widen[...], w_narrow[...],
-            )
-        )
-    return outs
+    return finish(
+        own_ref[...].astype(F32), context[...].astype(BF16), gains_ref[1, 1:2],
+        w_project[...], w_widen[...], w_narrow[...],
+    )
 
 
 def block_copies(pairs, block, sems, at):
@@ -419,11 +420,11 @@
 
 def middle_kernel(
     own_ref, north_ref, south_ref, west_ref, east_ref, gains_ref, merge_gain_ref,
-    coarse_gains_ref, bias_hbm, triple_hbm, project_hbm, widen_hbm, narrow_hbm,
-    merge_order_hbm, merge_weight_hbm, c_triple_hbm, c_project_hbm, c_widen_hbm, c_narrow_hbm,
+    coarse_gains_ref, merge_order_ref, bias_hbm, triple_hbm, project_hbm, widen_hbm, narrow_hbm,
+    merge_weight_hbm, c_triple_hbm, c_project_hbm, c_widen_hbm, c_narrow_hbm,
     parts_ref, coarse_ref, top_ref, bottom_ref,
     query, key, value, context, bias, c_bias, w_triple, w_project, w_widen, w_narrow,
-    merge_order, merge_weight, c_triple, c_project, c_widen, c_narrow, sems, bias_sems,
+    merge_weight, c_triple, c_project, c_widen, c_narrow, sems, bias_sems,
 ):
     steps = bias_hbm.shape[1]
     heads = bias.shape[1]
@@ -434,23 +435,20 @@
              (widen_hbm, w_widen), (narrow_hbm, w_narrow)], 1, sems, 0,
         )
         + [
-            [pltpu.make_async_copy(merge_order_hbm, merge_order, sems.at[4])],
-            [pltpu.make_async_copy(merge_weight_hbm, merge_weight, sems.at[5])],
+            [pltpu.make_async_copy(merge_weight_hbm, merge_weight, sems.at[4])],
             bias_copies(bias_hbm, c_bias, padded(heads), bias_sems, 2 * steps),
         ]
         + block_copies(
             [(c_triple_hbm, c_triple), (c_project_hbm, c_project),
-             (c_widen_hbm, c_widen), (c_narrow_hbm, c_narrow)], 0, sems, 6,
+             (c_widen_hbm, c_widen), (c_narrow_hbm, c_narrow)], 0, sems, 5,
         )
     )
-    outs = shifted_block(
+    skip = shifted_block(
         own_ref, north_ref, south_ref, west_ref, east_ref, gains_ref, fetched,
         bias, w_triple, w_project, w_widen, w_narrow, query, key, value, context,
     )
     channels = own_ref.shape[1]
-    skip = jnp.concatenate(outs, axis=0)
-    fetched.wait(*range(5, 12))
-    grouped = dot(merge_order[...], skip)
+    grouped = dot(sent_to(merge_order_ref, skip.shape[0]), skip)
     parts_ref[...] = grouped.astype(BF16)
     parts = [grouped[i * WP : (i + 1) * WP] for i in range(4)]
     width = 4 * channels
@@ -458,6 +456,7 @@
     parts = [p - mean for p in parts]
     variance = sum(jnp.sum(p * p, axis=-1, keepdims=True) for p in parts) / width
     factor = lax.rsqrt(variance + 1e-05)
+    fetched.wait(5)
     coarse = jnp.zeros((WP, merge_weight.shape[1]), F32)
     for i, p in enumerate(parts):
         merged = (p * factor * merge_gain_ref[i : i + 1]).astype(BF16)
@@ -465,10 +464,12 @@
     x = coarse.astype(BF16).astype(F32)
     wide = x.shape[1]
     normed = norm(x, coarse_gains_ref[0, 0:1]).astype(BF16)
+    fetched.wait(6, 7)
     triple = dot(normed, c_triple[...]).astype(BF16)
     mixed = attend(
         triple[:, :wide], triple[:, wide : 2 * wide], triple[:, 2 * wide :], c_bias, 0, None
     ).astype(BF16)
+    fetched.wait(8, 9, 10)
     done = finish(
         x, mixed, coarse_gains_ref[0, 1:2], c_project[...], c_widen[...], c_narrow[...]
     )
@@ -480,10 +481,10 @@
 
 def last_kernel(
     own_ref, north_ref, south_ref, west_ref, east_ref, gains_ref, parts_ref, expand_gain_ref,
-    bias_hbm, triple_hbm, project_hbm, widen_hbm, narrow_hbm, expand_weight_hbm, expand_order_hbm,
+    expand_order_ref, bias_hbm, triple_hbm, project_hbm, widen_hbm, narrow_hbm, expand_weight_hbm,
     out_ref,
     query, key, value, context, bias, w_triple, w_project, w_widen, w_narrow,
-    expand_weight, expand_order, sems, bias_sems,
+    expand_weight, sems, bias_sems,
 ):
     fetched = Fetched(
         [bias_copies(bias_hbm, bias, 0, bias_sems, 0)]
@@ -491,24 +492,22 @@
             [(triple_hbm, w_triple), (project_hbm, w_project),
              (widen_hbm, w_widen), (narrow_hbm, w_narrow)], 1, sems, 0,
         )
-        + [
-            [pltpu.make_async_copy(expand_weight_hbm, expand_weight, sems.at[4])],
-            [pltpu.make_async_copy(expand_order_hbm, expand_order, sems.at[5])],
-        ]
-    )
-    (deep,) = shifted_block(
+        + [[pltpu.make_async_copy(expand_weight_hbm, expand_weight, sems.at[4])]]
+    )
+    deep = shifted_block(
         own_ref, north_ref, south_ref, west_ref, east_ref, gains_ref, fetched,
         bias, w_triple, w_project, w_widen, w_narrow, query, key, value, context,
     )
     channels = parts_ref.shape[1]
-    fetched.wait(5, 6)
+    fetched.wait(5)
     widened = dot(deep, expand_weight[...])
     outs = []
     for i in range(4):
         shuffled = widened[:, i * channels : (i + 1) * channels]
         skip = parts_ref[i * WP : (i + 1) * WP].astype(F32)
         outs.append((skip + norm(shuffled, expand_gain_ref[...])).astype(BF16))
-    out_ref[...] = dot(expand_order[...], jnp.concatenate(outs, axis=0)).astype(BF16)
+    moves = sent_to(expand_order_ref, out_ref.shape[0])
+    out_ref[...] = dot(moves, jnp.concatenate(outs, axis=0)).astype(BF16)
 
 
 WHOLE = pl.BlockSpec(memory_space=pltpu.VMEM)
@@ -568,7 +567,9 @@
     bias_first = bias_of([(fine_bias, 0)], bias_index, spread)
     bias_middle = bias_of([(fine_bias, 1), (coarse_bias, 0)], bias_index, spread)
     bias_last = bias_of([(coarse_bias, 1)], bias_index, spread)
-    fine_weights = (fine_query_key_value, fine_project, fine_widen, fine_narrow)
+    fine_weights = (
+        fine_query_key_value, fine_project, fine_widen, fine_narrow.transpose(0, 2, 1)
+    )
     coarse_weights = (coarse_query_key_value, coarse_project, coarse_widen, coarse_narrow)
     steps = bias_first.shape[1]
     dma = pltpu.SemaphoreType.DMA
@@ -583,18 +584,17 @@
             jax.ShapeDtypeStruct((line, channels), BF16),
             jax.ShapeDtypeStruct((line, channels), BF16),
         ],
-        in_specs=[WHOLE] * 3 + [APART] + [WHOLE] * 2 + [APART, WHOLE] + [APART] * 4,
+        in_specs=[WHOLE] * 7 + [APART] * 5,
         out_specs=[WHOLE] * 3,
-        scratch_shapes=[pltpu.VMEM((tokens, channels), F32), pltpu.VMEM(order.shape, BF16)]
-        + [fine_scratch] + weight_scratch(fine_weights) + [dma((5,)), dma((2 * steps,))],
-        compiler_params=pltpu.CompilerParams(vmem_limit_bytes=20 << 20),
+        scratch_shapes=[pltpu.VMEM((tokens, channels), BF16), fine_scratch]
+        + weight_scratch(fine_weights) + [dma((4,)), dma((2 * steps,))],
+        compiler_params=pltpu.CompilerParams(vmem_limit_bytes=VMEM_LIMIT),
         name="fine_plain",
     )(
         fields.reshape(-1, channels), land_sea, land_embed[None], order, of_row, of_col,
-        bias_first, fine_gains, *fine_weights,
-    )
-
-    merge_order = merge_table(rows, cols)
+        fine_gains, bias_first, *fine_weights,
+    )
+
     parts, coarse, top, bottom = pl.pallas_call(
         middle_kernel,
         out_shape=[
@@ -603,36 +603,35 @@
             jax.ShapeDtypeStruct((line // 2, wide), BF16),
             jax.ShapeDtypeStruct((line // 2, wide), BF16),
         ],
-        in_specs=[WHOLE] * 8 + [APART] * 11,
+        in_specs=[WHOLE] * 9 + [APART] * 10,
         out_specs=[WHOLE] * 4,
         scratch_shapes=shifted_scratch(quad_rows, quad_cols, channels)
         + [fine_scratch, coarse_scratch] + weight_scratch(fine_weights)
-        + [pltpu.VMEM(merge_order.shape, BF16), pltpu.VMEM(merge_weight.shape, BF16)]
-        + weight_scratch(coarse_weights) + [dma((10,)), dma((4 * steps,))],
-        compiler_params=pltpu.CompilerParams(vmem_limit_bytes=32 << 20),
+        + [pltpu.VMEM(merge_weight.shape, BF16)]
+        + weight_scratch(coarse_weights) + [dma((9,)), dma((4 * steps,))],
+        compiler_params=pltpu.CompilerParams(vmem_limit_bytes=VMEM_LIMIT),
         name="fine_shifted_coarse_plain",
     )(
         *halo(first.reshape(quad_rows, quad_cols, QP, channels), top, bottom),
-        fine_gains, merge_gain.reshape(4, channels), coarse_gains, bias_middle, *fine_weights,
-        merge_order, merge_weight, *coarse_weights,
-    )
-
-    expand_order = expand_table(rows, cols)
+        fine_gains, merge_gain.reshape(4, channels), coarse_gains,
+        merge_table(rows, cols), bias_middle, *fine_weights, merge_weight, *coarse_weights,
+    )
+
     out = pl.pallas_call(
         last_kernel,
         out_shape=jax.ShapeDtypeStruct((LEVELS * rows * cols, channels), BF16),
-        in_specs=[WHOLE] * 8 + [APART] * 7,
+        in_specs=[WHOLE] * 9 + [APART] * 6,
         out_specs=WHOLE,
         scratch_shapes=shifted_scratch(quad_rows // 2, quad_cols // 2, wide)
         + [coarse_scratch] + weight_scratch(coarse_weights)
-        + [pltpu.VMEM(expand_weight.shape, BF16), pltpu.VMEM(expand_order.shape, BF16)]
-        + [dma((6,)), dma((2 * steps,))],
-        compiler_params=pltpu.CompilerParams(vmem_limit_bytes=28 << 20),
+        + [pltpu.VMEM(expand_weight.shape, BF16)]
+        + [dma((5,)), dma((2 * steps,))],
+        compiler_params=pltpu.CompilerParams(vmem_limit_bytes=VMEM_LIMIT),
         name="coarse_shifted_expand",
     )(
         *halo(coarse.reshape(quad_rows // 2, quad_cols // 2, QP, wide), top, bottom),
-        coarse_gains, parts, expand_gain[None], bias_last, *coarse_weights,
-        expand_weight, expand_order,
+        coarse_gains, parts, expand_gain[None], expand_table(rows, cols),
+        bias_last, *coarse_weights, expand_weight,
     )
     return out.reshape(fields.shape)
 

time: 96.2 us -> 85.7 us (0.89)
  local copies, waits for them, and re-layouts: 17.7 us -> 3.88 us
  Pallas kernels: 55.3 us -> 61.6 us
  waiting for transfers between devices: 5.27 us -> 3.9 us
  other arithmetic: 1.42 us -> 0.1 us
    unnamed x75 -> x18, local copies, waits for them, and re-layouts: 17.6 us -> 1.37 us
    pallas_call x3, Pallas kernels: 26.4 us -> 31.9 us  [bias_of(): pl.pallas_call(functools.partial(bias_kernel, picks=tuple((b for _, b in...]
    pallas_call x1, Pallas kernels: 7.28 us -> 9.33 us  [on_device(): pl.pallas_call(last_kernel, out_shape=jax.ShapeDtypeStruct((LEVELS * rows...]
    squeeze x2, local copies, waits for them, and re-layouts: 0.02 us -> 1.81 us  [side(): return jnp.concatenate([north[c:c + 1], own[:, c], south[c:c + 1]], axis=0)]
    ppermute x2, waiting for transfers between devices: 4.65 us -> 3.29 us  [halo(): north = lax.ppermute(bottom, 'lat', down)]
    concatenate x4, other arithmetic: 1.42 us -> 0.1 us  [side(): return jnp.concatenate([north[c:c + 1], own[:, c], south[c:c + 1]], axis=0)]
  transfers between devices with their start and end apart: 8 -> 8, of which waited for: 3 -> 3; matrix products, arithmetic and copies ran while one was open for 1% -> 3% of each run, Pallas kernels for 22% -> 29%
where the time goes in v3:
time: 85.7 us; the launch traced here: 85.3 us
  Pallas kernels  61.6 us (72%)
  starting transfers between devices  15.5 us (18%)
  waiting for transfers between devices  3.9 us (5%)
  local copies, waits for them, and re-layouts  3.88 us (5%)
    pallas_call x3, Pallas kernels, bias_of(): pl.pallas_call(functools.partial(bias_kernel, picks=tuple((b for _, b in...  31.9 us
    pallas_call x1, Pallas kernels, on_device(): pl.pallas_call(middle_kernel, out_shape=[jax.ShapeDtypeStruct((tokens, ch...  12.8 us
    pallas_call x1, Pallas kernels, on_device(): pl.pallas_call(last_kernel, out_shape=jax.ShapeDtypeStruct((LEVELS * rows...  9.33 us
    pallas_call x1, Pallas kernels, on_device(): pl.pallas_call(first_kernel, out_shape=[jax.ShapeDtypeStruct((tokens, cha...  7.51 us
    ppermute x2, starting transfers between devices, halo(): south = lax.ppermute(top, 'lat', up)  7.15 us
    ppermute x2, starting transfers between devices, halo(): from_west = lax.ppermute(side(cols - 1), LON, east)  4.52 us
    ppermute x2, starting transfers between devices, halo(): north = lax.ppermute(bottom, 'lat', down)  3.75 us
    ppermute x2, waiting for transfers between devices, halo(): north = lax.ppermute(bottom, 'lat', down)  3.29 us
  transfers between devices with their start and end apart: 8, of which 3 were waited for; matrix products, arithmetic and copies ran while one was open for 3% of the time, Pallas kernels for 29%

profile of v3, /device:TPU:0, one launch (start us, length us, event | category | flops | bytes accessed | tf_op | source)
XLA Modules:
  0.0 85.3 jit_solution(6590505430193914909)
XLA Ops:
  0.0 7.5 %bias_table.3 = f32[2,1280,128]{2,1,0:T(8,128)} custom-call(s32[144,144]{1,0:T(8,128)} %index_ref.5, bf16[160,144]{1,0:T(8,128)(2,1)} %constant.12.clone.spread_ref, f32[6,2,3312]{2,1,0:T(2,128)} %bitcast.60), custom_call_target="tpu_custom_call" | custom-call | flops 10905190400 | bytes 1048576 | tf_op jit(solution)/shard_map/bias_table/pallas_call | solution.py:250
  7.5 7.5 %fine_plain.1 = (bf16[640,192]{1,0:T(8,128)(2,1)}, bf16[160,192]{1,0:T(8,128)(2,1)}, bf16[160,192]{1,0:T(8,128)(2,1)}) custom-call(bf16[576,192]{1,0:T(8,128)(2,1)} %bitcast.47, s32[12,24]{1,0:T(8,128)} %land_ref.1, f32[1,192]{1,0:T(1,128)} %bitcast.56, s32[1,576]{1,0:T(1,128)} %constant.13.clone.order_ref, bf16[640,12]{1,0:T(8,128)(2,1)} %constant.14.clone.of_row_ref, ...), custom_call_target="tpu_custom_call" | custom-call | tf_op jit(solution)/shard_map/fine_plain/pallas_call | solution.py:580
  15.0 3.0 %collective-permute-start = (bf16[4,40,192]{2,1,0:T(8,128)(2,1)}, bf16[4,40,192]{2,1,0:T(8,128)(2,1)S(1)}, u32[]{:S(2)}, u32[]{:S(2)}) collective-permute-start(bf16[4,40,192]{2,1,0:T(8,128)(2,1)} %bitcast.63), channel_id=1, source_target_pairs={{0,2},{2,4},{4,6},{6,8},{8,10},{10,12},{12,14},{14,0},{1,3},{3,5},... | collective-permute-start | bytes 184328 | tf_op jit(solution)/shard_map/ppermute | solution.py:531
  18.0 3.1 %collective-permute-start.1 = (bf16[4,40,192]{2,1,0:T(8,128)(2,1)}, bf16[4,40,192]{2,1,0:T(8,128)(2,1)S(1)}, u32[]{:S(2)}, u32[]{:S(2)}) collective-permute-start(bf16[4,40,192]{2,1,0:T(8,128)(2,1)} %bitcast.62), channel_id=1, source_target_pairs={{2,0},{4,2},{6,4},{8,6},{10,8},{12,10},{14,12},{0,14},{3,1},{5,3},... | collective-permute-start | bytes 184328 | tf_op jit(solution)/shard_map/ppermute | solution.py:532
  21.1 0.9 %slice_bitcast_fusion = (bf16[4,40,192]{2,1,0:T(8,128)(2,1)S(1)}, bf16[4,40,192]{2,1,0:T(8,128)(2,1)S(1)}) fusion(bf16[4,4,40,192]{3,2,1,0:T(8,128)(2,1)} %bitcast.45), kind=kLoop, calls=%fused_computation.4 | loop fusion | bytes 245760 | tf_op jit(solution)/shard_map/squeeze | solution.py:535
  22.0 1.8 %collective-permute-done = bf16[4,40,192]{2,1,0:T(8,128)(2,1)S(1)} collective-permute-done((bf16[4,40,192]{2,1,0:T(8,128)(2,1)}, bf16[4,40,192]{2,1,0:T(8,128)(2,1)S(1)}, u32[]{:S(2)}, u32[]{:S(2)}) %collective-permute-start) | collective-permute-done | bytes 61472 | tf_op jit(solution)/shard_map/ppermute | solution.py:531
  23.8 0.0 copy-start.2
  23.8 0.6 collective-permute-done.1
  24.4 0.0 copy-start.3
  24.4 0.1 collective-permute-start.3
  24.5 2.2 %collective-permute-start.2 = (bf16[6,40,192]{2,1,0:T(8,128)(2,1)S(1)}, bf16[6,40,192]{2,1,0:T(8,128)(2,1)S(1)}, u32[]{:S(2)}, u32[]{:S(2)}) collective-permute-start(bf16[6,40,192]{2,1,0:T(8,128)(2,1)S(1)} %pad_maximum_fusion), channel_id=1, source_target_pairs={{0,1},{1,16},{16,17},{17,0},{2,3},{3,18},{18,19},{19,2},{4,5},{5,2... | collective-permute-start | bytes 276488 | tf_op jit(solution)/shard_map/ppermute | solution.py:537
  26.8 0.0 copy-start.8
  26.8 14.3 %bias_table.4 = f32[2,3840,128]{2,1,0:T(8,128)} custom-call(s32[144,144]{1,0:T(8,128)} %index_ref.5, bf16[160,144]{1,0:T(8,128)(2,1)} %constant.12.clone.spread_ref, f32[6,2,3312]{2,1,0:T(2,128)} %bitcast.61, f32[12,2,3312]{2,1,0:T(2,128)} %bitcast.58), custom_call_target="tpu_custom_call" | custom-call | flops 32715571200 | bytes 1048576 | tf_op jit(solution)/shard_map/bias_table/pallas_call | solution.py:250
  41.1 0.0 copy-done.2
  41.1 0.0 copy-done.3
  41.1 0.0 copy-done.8
  41.1 0.7 reshape.69.merge_gain_ref
  41.8 0.0 collective-permute-done.3
  41.8 0.0 copy-start.4
  41.8 0.0 collective-permute-done.2
  41.8 0.0 copy-start.5
  41.8 0.6 copy-done.4
  42.4 0.0 copy-done.5
  42.5 12.8 %fine_shifted_coarse_plain.1 = (bf16[640,192]{1,0:T(8,128)(2,1)}, bf16[160,384]{1,0:T(8,128)(2,1)}, bf16[80,384]{1,0:T(8,128)(2,1)}, bf16[80,384]{1,0:T(8,128)(2,1)}) custom-call(bf16[640,192]{1,0:T(8,128)(2,1)} %get-tuple-element.12.own_ref, bf16[160,192]{1,0:T(8,128)(2,1)} %bitcast.50, bf16[160,192]{1,0:T(8,128)(2,1)} %bitcast.51, ...), custom_call_target="tpu_custom_call" | custom-call | tf_op jit(solution)/shard_map/fine_shifted_coarse_plain/pallas_call | solution.py:598
  55.3 0.7 collective-permute-start.4
  56.0 4.0 %collective-permute-start.5 = (bf16[2,40,384]{2,1,0:T(8,128)(2,1)}, bf16[2,40,384]{2,1,0:T(8,128)(2,1)S(1)}, u32[]{:S(2)}, u32[]{:S(2)}) collective-permute-start(bf16[2,40,384]{2,1,0:T(8,128)(2,1)} %bitcast.64), channel_id=1, source_target_pairs={{2,0},{4,2},{6,4},{8,6},{10,8},{12,10},{14,12},{0,14},{3,1},{5,3},... | collective-permute-start | bytes 184328 | tf_op jit(solution)/shard_map/ppermute | solution.py:532
  60.0 0.9 %slice_bitcast_fusion.2 = (bf16[2,40,384]{2,1,0:T(8,128)(2,1)S(1)}, bf16[2,40,384]{2,1,0:T(8,128)(2,1)S(1)}) fusion(bf16[2,2,40,384]{3,2,1,0:T(8,128)(2,1)} %bitcast.46), kind=kLoop, calls=%fused_computation.6 | loop fusion | bytes 245760 | tf_op jit(solution)/shard_map/squeeze | solution.py:535
  60.9 1.5 %collective-permute-done.4 = bf16[2,40,384]{2,1,0:T(8,128)(2,1)S(1)} collective-permute-done((bf16[2,40,384]{2,1,0:T(8,128)(2,1)}, bf16[2,40,384]{2,1,0:T(8,128)(2,1)S(1)}, u32[]{:S(2)}, u32[]{:S(2)}) %collective-permute-start.4) | collective-permute-done | bytes 61472 | tf_op jit(solution)/shard_map/ppermute | solution.py:531
  62.5 0.0 copy-start
  62.5 0.0 collective-permute-done.5
  62.5 0.0 copy-start.1
  62.5 0.1 collective-permute-start.7
  62.6 2.3 %collective-permute-start.6 = (bf16[4,40,384]{2,1,0:T(8,128)(2,1)S(1)}, bf16[4,40,384]{2,1,0:T(8,128)(2,1)S(1)}, u32[]{:S(2)}, u32[]{:S(2)}) collective-permute-start(bf16[4,40,384]{2,1,0:T(8,128)(2,1)S(1)} %pad_maximum_fusion.2), channel_id=1, source_target_pairs={{0,1},{1,16},{16,17},{17,0},{2,3},{3,18},{18,19},{19,2},{4,5},{5,2... | collective-permute-start | bytes 368648 | tf_op jit(solution)/shard_map/ppermute | solution.py:537
  64.9 10.2 %bias_table.5 = f32[2,2560,128]{2,1,0:T(8,128)} custom-call(s32[144,144]{1,0:T(8,128)} %index_ref.5, bf16[160,144]{1,0:T(8,128)(2,1)} %constant.12.clone.spread_ref, f32[12,2,3312]{2,1,0:T(2,128)} %bitcast.59), custom_call_target="tpu_custom_call" | custom-call | flops 21810380800 | bytes 1048576 | tf_op jit(solution)/shard_map/bias_table/pallas_call | solution.py:250
  75.1 0.0 copy-done
  75.1 0.0 copy-done.1
  75.1 0.0 collective-permute-done.7
  75.1 0.0 copy-start.6
  75.1 0.0 collective-permute-done.6
  75.1 0.0 copy-start.7
  75.1 0.6 copy-done.6
  75.7 0.1 copy-done.7
  75.8 9.3 %coarse_shifted_expand.1 = bf16[576,192]{1,0:T(8,128)(2,1)} custom-call(bf16[160,384]{1,0:T(8,128)(2,1)} %get-tuple-element.15.own_ref, bf16[80,384]{1,0:T(8,128)(2,1)} %bitcast.48, bf16[80,384]{1,0:T(8,128)(2,1)} %bitcast.49, bf16[160,384]{1,0:T(8,128)(2,1)} %bitcast.55, bf16[160,384]{1,0:T(8,128)(2,1)} %bitcast.54, f32[2,2,384]{2,1,0:T(2,128)} %gains_ref.5, ...), custom_call_target="tpu_custom_call" | custom-call | tf_op jit(solution)/shard_map/coarse_shifted_expand/pallas_call | solution.py:620
  (8 shorter events, 0.1 us)
Async XLA Ops:
  15.0 8.8 %collective-permute-start = (bf16[4,40,192]{2,1,0:T(8,128)(2,1)}, bf16[4,40,192]{2,1,0:T(8,128)(2,1)S(1)}, u32[]{:S(2)}, u32[]{:S(2)}) collective-permute-start(bf16[4,40,192]{2,1,0:T(8,128)(2,1)} %bitcast.63), channel_id=1, source_target_pairs={{0,2},{2,4},{4,6},{6,8},{8,10},{10,12},{12,14},{14,0},{1,3},{3,5},... | collective-permute-start | bytes 184328 | tf_op jit(solution)/shard_map/ppermute | solution.py:531
  18.0 6.4 %collective-permute-start.1 = (bf16[4,40,192]{2,1,0:T(8,128)(2,1)}, bf16[4,40,192]{2,1,0:T(8,128)(2,1)S(1)}, u32[]{:S(2)}, u32[]{:S(2)}) collective-permute-start(bf16[4,40,192]{2,1,0:T(8,128)(2,1)} %bitcast.62), channel_id=1, source_target_pairs={{2,0},{4,2},{6,4},{8,6},{10,8},{12,10},{14,12},{0,14},{3,1},{5,3},... | collective-permute-start | bytes 184328 | tf_op jit(solution)/shard_map/ppermute | solution.py:532
  23.8 17.3 %copy-start.2 = (bf16[4,40,192]{2,1,0:T(8,128)(2,1)}, bf16[4,40,192]{2,1,0:T(8,128)(2,1)S(1)}, u32[]{:S(2)}) copy-start(bf16[4,40,192]{2,1,0:T(8,128)(2,1)S(1)} %collective-permute-done) | copy-start | bytes 184324
  24.4 16.7 %copy-start.3 = (bf16[4,40,192]{2,1,0:T(8,128)(2,1)}, bf16[4,40,192]{2,1,0:T(8,128)(2,1)S(1)}, u32[]{:S(2)}) copy-start(bf16[4,40,192]{2,1,0:T(8,128)(2,1)S(1)} %collective-permute-done.1) | copy-start | bytes 184324
  24.4 17.3 %collective-permute-start.3 = (bf16[6,40,192]{2,1,0:T(8,128)(2,1)S(1)}, bf16[6,40,192]{2,1,0:T(8,128)(2,1)S(1)}, u32[]{:S(2)}, u32[]{:S(2)}) collective-permute-start(bf16[6,40,192]{2,1,0:T(8,128)(2,1)S(1)} %pad_maximum_fusion.1), channel_id=1, source_target_pairs={{1,0},{16,1},{17,16},{0,17},{3,2},{18,3},{19,18},{2,19},{5,4},{20,... | collective-permute-start | bytes 276488 | tf_op jit(solution)/shard_map/ppermute | solution.py:538
  24.5 17.2 %collective-permute-start.2 = (bf16[6,40,192]{2,1,0:T(8,128)(2,1)S(1)}, bf16[6,40,192]{2,1,0:T(8,128)(2,1)S(1)}, u32[]{:S(2)}, u32[]{:S(2)}) collective-permute-start(bf16[6,40,192]{2,1,0:T(8,128)(2,1)S(1)} %pad_maximum_fusion), channel_id=1, source_target_pairs={{0,1},{1,16},{16,17},{17,0},{2,3},{3,18},{18,19},{19,2},{4,5},{5,2... | collective-permute-start | bytes 276488 | tf_op jit(solution)/shard_map/ppermute | solution.py:537
  26.8 14.3 %copy-start.8 = (f32[768]{0:T(1024)S(1)}, f32[768]{0:T(1024)}, u32[]{:S(2)}) copy-start(f32[768]{0:T(1024)} %param.36) | copy-start | bytes 9220
  41.8 0.7 copy-start.4
  41.8 0.7 copy-start.5
  55.3 7.2 %collective-permute-start.4 = (bf16[2,40,384]{2,1,0:T(8,128)(2,1)}, bf16[2,40,384]{2,1,0:T(8,128)(2,1)S(1)}, u32[]{:S(2)}, u32[]{:S(2)}) collective-permute-start(bf16[2,40,384]{2,1,0:T(8,128)(2,1)} %bitcast.65), channel_id=1, source_target_pairs={{0,2},{2,4},{4,6},{6,8},{8,10},{10,12},{12,14},{14,0},{1,3},{3,5},... | collective-permute-start | bytes 184328 | tf_op jit(solution)/shard_map/ppermute | solution.py:531
  56.0 6.5 %collective-permute-start.5 = (bf16[2,40,384]{2,1,0:T(8,128)(2,1)}, bf16[2,40,384]{2,1,0:T(8,128)(2,1)S(1)}, u32[]{:S(2)}, u32[]{:S(2)}) collective-permute-start(bf16[2,40,384]{2,1,0:T(8,128)(2,1)} %bitcast.64), channel_id=1, source_target_pairs={{2,0},{4,2},{6,4},{8,6},{10,8},{12,10},{14,12},{0,14},{3,1},{5,3},... | collective-permute-start | bytes 184328 | tf_op jit(solution)/shard_map/ppermute | solution.py:532
  62.5 12.6 %copy-start = (bf16[2,40,384]{2,1,0:T(8,128)(2,1)}, bf16[2,40,384]{2,1,0:T(8,128)(2,1)S(1)}, u32[]{:S(2)}) copy-start(bf16[2,40,384]{2,1,0:T(8,128)(2,1)S(1)} %collective-permute-done.4) | copy-start | bytes 184324
  62.5 12.6 %copy-start.1 = (bf16[2,40,384]{2,1,0:T(8,128)(2,1)}, bf16[2,40,384]{2,1,0:T(8,128)(2,1)S(1)}, u32[]{:S(2)}) copy-start(bf16[2,40,384]{2,1,0:T(8,128)(2,1)S(1)} %collective-permute-done.5) | copy-start | bytes 184324
  62.5 12.5 %collective-permute-start.7 = (bf16[4,40,384]{2,1,0:T(8,128)(2,1)S(1)}, bf16[4,40,384]{2,1,0:T(8,128)(2,1)S(1)}, u32[]{:S(2)}, u32[]{:S(2)}) collective-permute-start(bf16[4,40,384]{2,1,0:T(8,128)(2,1)S(1)} %pad_maximum_fusion.3), channel_id=1, source_target_pairs={{1,0},{16,1},{17,16},{0,17},{3,2},{18,3},{19,18},{2,19},{5,4},{20,... | collective-permute-start | bytes 368648 | tf_op jit(solution)/shard_map/ppermute | solution.py:538
  62.6 12.5 %collective-permute-start.6 = (bf16[4,40,384]{2,1,0:T(8,128)(2,1)S(1)}, bf16[4,40,384]{2,1,0:T(8,128)(2,1)S(1)}, u32[]{:S(2)}, u32[]{:S(2)}) collective-permute-start(bf16[4,40,384]{2,1,0:T(8,128)(2,1)S(1)} %pad_maximum_fusion.2), channel_id=1, source_target_pairs={{0,1},{1,16},{16,17},{17,0},{2,3},{3,18},{18,19},{19,2},{4,5},{5,2... | collective-permute-start | bytes 368648 | tf_op jit(solution)/shard_map/ppermute | solution.py:537
  75.1 0.6 copy-start.6
  75.1 0.7 copy-start.7

commit v4 on v3

--- a/solution.py
+++ b/solution.py
@@ -23,7 +23,6 @@
 LO_COUNT = 13
 LOG2E = 1.4426950408889634
 MASKED = -1e30
-VMEM_LIMIT = 60 << 20
 LON = ("sec", "head")
 F32 = jnp.float32
 BF16 = jnp.bfloat16
@@ -169,24 +168,27 @@
     return -(-heads // 8) * 8
 
 
-def bias_kernel(index_ref, spread_ref, *refs, picks):
-    table_refs = refs[:-4]
-    out_ref, table, index, left = refs[-4:]
+def bias_kernel(*refs, picks, fresh):
+    if fresh:
+        index_ref, spread_ref, *table_refs, out_ref, index, table, left = refs
+    else:
+        index, *table_refs, out_ref, table, left = refs
     rows = table.shape[0]
     bias_len = table_refs[0].shape[-1]
 
     @pl.when(pl.program_id(0) == 0)
     def _():
-        spread = spread_ref[...]
-        plain = index_ref[...]
-        high = (plain >> 4).astype(F32).astype(BF16)
-        low = (plain & 15).astype(F32).astype(BF16)
-
-        def moved(part):
-            return dot_t(dot(spread, part).astype(BF16), spread).astype(jnp.int32)
-
-        spot = lax.broadcasted_iota(jnp.int32, (WP, WP), 1) % QP
-        index[...] = jnp.where(spot < QUAD, moved(high) * 16 + moved(low), bias_len)
+        if fresh:
+            spread = spread_ref[...]
+            plain = index_ref[...]
+            high = (plain >> 4).astype(F32).astype(BF16)
+            low = (plain & 15).astype(F32).astype(BF16)
+
+            def moved(part):
+                return dot_t(dot(spread, part).astype(BF16), spread).astype(jnp.int32)
+
+            spot = lax.broadcasted_iota(jnp.int32, (WP, WP), 1) % QP
+            index[...] = jnp.where(spot < QUAD, moved(high) * 16 + moved(low), bias_len)
         table[...] = jnp.full(table.shape, MASKED, F32)
         at = 0
         for table_ref, block in zip(table_refs, picks):
@@ -241,28 +243,32 @@
                         out_ref[1, pl.ds(at + j, 8, stride=span), :] = moved_part
 
 
-def bias_of(picks, index, spread, span=32):
+def bias_of(picks, order, vmem, span=32):
     tables = [t.transpose(1, 0, 2) for t, _ in picks]
     rows = sum(padded(t.shape[0]) for t in tables)
     flops = 2 * WP * 256 * WP * LO_COUNT * rows * 4
     steps = WP // span
-    whole = pl.BlockSpec(memory_space=pltpu.VMEM)
+    fresh = len(order) == 2
+    out_shape = [jax.ShapeDtypeStruct((2, steps * rows * span, 128), F32)]
+    out_specs = [pl.BlockSpec((2, rows * span, 128), lambda i: (0, i, 0))]
+    if fresh:
+        out_shape.append(jax.ShapeDtypeStruct((WP, WP), jnp.int32))
+        out_specs.append(pl.BlockSpec((WP, WP), lambda i: (0, 0)))
     out = pl.pallas_call(
-        functools.partial(bias_kernel, picks=tuple(b for _, b in picks)),
-        out_shape=jax.ShapeDtypeStruct((2, steps * rows * span, 128), F32),
+        functools.partial(bias_kernel, picks=tuple(b for _, b in picks), fresh=fresh),
+        out_shape=out_shape,
         grid=(steps,),
-        in_specs=[whole] * (2 + len(tables)),
-        out_specs=pl.BlockSpec((2, rows * span, 128), lambda i: (0, i, 0)),
+        in_specs=[pl.BlockSpec(memory_space=pltpu.VMEM)] * (len(order) + len(tables)),
+        out_specs=out_specs,
         scratch_shapes=[
             pltpu.VMEM((rows, LO_COUNT * 256), F32),
-            pltpu.VMEM((WP, WP), jnp.int32),
             pltpu.VMEM((rows * LO_COUNT, 512), BF16),
         ],
-        compiler_params=pltpu.CompilerParams(vmem_limit_bytes=VMEM_LIMIT),
+        compiler_params=pltpu.CompilerParams(vmem_limit_bytes=vmem << 20),
         cost_estimate=pl.CostEstimate(flops=2 * flops, bytes_accessed=1 << 20, transcendentals=0),
         name="bias_table",
-    )(index, spread, *tables)
-    return out.reshape(2, steps, rows, span, 128)
+    )(*order, *tables)
+    return [out[0].reshape(2, steps, rows, span, 128)] + list(out[1:])
 
 
 def bias_copies(source_ref, bias, first, sems, at):
@@ -281,7 +287,7 @@
 class Fetched:
     def __init__(self, copies):
         self.copies = copies
-        for group in copies:
+        for group in copies[1:2] + copies[:1] + copies[2:]:
             for copy in group:
                 copy.start()
 
@@ -299,11 +305,11 @@
 ):
     channels = fields_ref.shape[1]
     fetched = Fetched(
-        block_copies(
+        [bias_copies(bias_hbm, bias, 0, bias_sems, 0)]
+        + block_copies(
             [(triple_hbm, w_triple), (project_hbm, w_project),
              (widen_hbm, w_widen), (narrow_hbm, w_narrow)], 0, sems, 0,
         )
-        + [bias_copies(bias_hbm, bias, 0, bias_sems, 0)]
     )
     land = land_ref[...].astype(F32).astype(BF16)
     on_row = dot(of_row_ref[...], land)
@@ -312,9 +318,9 @@
     start = dot(sent_to(order_ref, rows), fields_ref[...]) + on_land * embed_ref[...]
     x = start.astype(BF16).astype(F32)
     normed = norm(x, gains_ref[0, 0:1]).astype(BF16)
+    fetched.wait(1)
+    triple = dot(normed, w_triple[...]).astype(BF16)
     fetched.wait(0)
-    triple = dot(normed, w_triple[...]).astype(BF16)
-    fetched.wait(4)
     inner = top_ref.shape[0]
     for a in range(rows // inner // 2):
         for b in range(inner // QP // 2):
@@ -331,7 +337,7 @@
             ).astype(BF16)
             context[top : top + 2 * QP] = mixed[: 2 * QP]
             context[below : below + 2 * QP] = mixed[2 * QP :]
-    fetched.wait(1, 2, 3)
+    fetched.wait(2, 3, 4)
     done = finish(
         x, context[...], gains_ref[0, 1:2], w_project[...], w_widen[...], w_narrow[...]
     )
@@ -456,10 +462,12 @@
     parts = [p - mean for p in parts]
     variance = sum(jnp.sum(p * p, axis=-1, keepdims=True) for p in parts) / width
     factor = lax.rsqrt(variance + 1e-05)
+    merge_gain = merge_gain_ref[...].reshape(1, width)
     fetched.wait(5)
     coarse = jnp.zeros((WP, merge_weight.shape[1]), F32)
     for i, p in enumerate(parts):
-        merged = (p * factor * merge_gain_ref[i : i + 1]).astype(BF16)
+        gain = merge_gain[:, i * channels : (i + 1) * channels]
+        merged = (p * factor * gain).astype(BF16)
         coarse = coarse + dot(merged, merge_weight[i * channels : (i + 1) * channels])
     x = coarse.astype(BF16).astype(F32)
     wide = x.shape[1]
@@ -564,9 +572,9 @@
         WIN_TOK,
     )
     order, of_row, of_col = fine_tables(rows, cols)
-    bias_first = bias_of([(fine_bias, 0)], bias_index, spread)
-    bias_middle = bias_of([(fine_bias, 1), (coarse_bias, 0)], bias_index, spread)
-    bias_last = bias_of([(coarse_bias, 1)], bias_index, spread)
+    bias_first, ordered = bias_of([(fine_bias, 0)], (bias_index, spread), 16)
+    (bias_middle,) = bias_of([(fine_bias, 1), (coarse_bias, 0)], (ordered,), 16)
+    (bias_last,) = bias_of([(coarse_bias, 1)], (ordered,), 16)
     fine_weights = (
         fine_query_key_value, fine_project, fine_widen, fine_narrow.transpose(0, 2, 1)
     )
@@ -588,7 +596,7 @@
         out_specs=[WHOLE] * 3,
         scratch_shapes=[pltpu.VMEM((tokens, channels), BF16), fine_scratch]
         + weight_scratch(fine_weights) + [dma((4,)), dma((2 * steps,))],
-        compiler_params=pltpu.CompilerParams(vmem_limit_bytes=VMEM_LIMIT),
+        compiler_params=pltpu.CompilerParams(vmem_limit_bytes=20 << 20),
         name="fine_plain",
     )(
         fields.reshape(-1, channels), land_sea, land_embed[None], order, of_row, of_col,
@@ -609,11 +617,11 @@
         + [fine_scratch, coarse_scratch] + weight_scratch(fine_weights)
         + [pltpu.VMEM(merge_weight.shape, BF16)]
         + weight_scratch(coarse_weights) + [dma((9,)), dma((4 * steps,))],
-        compiler_params=pltpu.CompilerParams(vmem_limit_bytes=VMEM_LIMIT),
+        compiler_params=pltpu.CompilerParams(vmem_limit_bytes=60 << 20),
         name="fine_shifted_coarse_plain",
     )(
         *halo(first.reshape(quad_rows, quad_cols, QP, channels), top, bottom),
-        fine_gains, merge_gain.reshape(4, channels), coarse_gains,
+        fine_gains, merge_gain, coarse_gains,
         merge_table(rows, cols), bias_middle, *fine_weights, merge_weight, *coarse_weights,
     )
 
@@ -626,7 +634,7 @@
         + [coarse_scratch] + weight_scratch(coarse_weights)
         + [pltpu.VMEM(expand_weight.shape, BF16)]
         + [dma((5,)), dma((2 * steps,))],
-        compiler_params=pltpu.CompilerParams(vmem_limit_bytes=VMEM_LIMIT),
+        compiler_params=pltpu.CompilerParams(vmem_limit_bytes=28 << 20),
         name="coarse_shifted_expand",
     )(
         *halo(coarse.reshape(quad_rows // 2, quad_cols // 2, QP, wide), top, bottom),

time: 85.7 us -> 80 us (0.933)
  Pallas kernels: 61.6 us -> 52.5 us
  local copies, waits for them, and re-layouts: 3.88 us -> 6.3 us
    pallas_call x3, Pallas kernels: 31.9 us -> 25.9 us  [bias_of(): pl.pallas_call(functools.partial(bias_kernel, picks=tuple((b for _, b in...]
    unnamed x18 -> x64, local copies, waits for them, and re-layouts: 1.37 us -> 5.39 us
    pallas_call x1, Pallas kernels: 7.51 us -> 5.85 us  [on_device(): pl.pallas_call(first_kernel, out_shape=[jax.ShapeDtypeStruct((tokens, cha...]
    pallas_call x1, Pallas kernels: 9.33 us -> 7.88 us  [on_device(): pl.pallas_call(last_kernel, out_shape=jax.ShapeDtypeStruct((LEVELS * rows...]
    squeeze x2, local copies, waits for them, and re-layouts: 1.81 us -> 0.88 us  [side(): return jnp.concatenate([north[c:c + 1], own[:, c], south[c:c + 1]], axis=0)]
  transfers between devices with their start and end apart: 8 -> 8, of which waited for: 3 -> 3; matrix products, arithmetic and copies ran while one was open for 3% -> 1% of each run, Pallas kernels for 29% -> 25%
where the time goes in v4:
time: 80 us; the launch traced here: 79.7 us
  Pallas kernels  52.5 us (66%)
  starting transfers between devices  15.6 us (20%)
  local copies, waits for them, and re-layouts  6.3 us (8%)
  waiting for transfers between devices  4.59 us (6%)
    pallas_call x3, Pallas kernels, bias_of(): pl.pallas_call(functools.partial(bias_kernel, picks=tuple((b for _, b in...  25.9 us
    pallas_call x1, Pallas kernels, on_device(): pl.pallas_call(middle_kernel, out_shape=[jax.ShapeDtypeStruct((tokens, ch...  12.9 us
    pallas_call x1, Pallas kernels, on_device(): pl.pallas_call(last_kernel, out_shape=jax.ShapeDtypeStruct((LEVELS * rows...  7.88 us
    ppermute x2, starting transfers between devices, halo(): south = lax.ppermute(top, 'lat', up)  7.18 us
    pallas_call x1, Pallas kernels, on_device(): pl.pallas_call(first_kernel, out_shape=[jax.ShapeDtypeStruct((tokens, cha...  5.85 us
    unnamed x64, local copies, waits for them, and re-layouts  5.39 us
    ppermute x2, starting transfers between devices, halo(): from_west = lax.ppermute(side(cols - 1), LON, east)  4.52 us
    ppermute x2, waiting for transfers between devices, halo(): north = lax.ppermute(bottom, 'lat', down)  3.98 us
  transfers between devices with their start and end apart: 8, of which 3 were waited for; matrix products, arithmetic and copies ran while one was open for 1% of the time, Pallas kernels for 25%

profile of v4, /device:TPU:0, one launch (start us, length us, event | category | flops | bytes accessed | tf_op | source)
XLA Modules:
  0.0 79.7 jit_solution(4188769938709412243)
XLA Ops:
  0.0 0.9 %copy-done.24 = f32[2,6,3312]{2,0,1:T(2,128)S(1)} copy-done((f32[2,6,3312]{2,0,1:T(2,128)S(1)}, f32[2,6,3312]{2,0,1:T(2,128)}, u32[]{:S(2)}) %copy-start.24) | copy-done | bytes 159000
  0.9 0.9 %copy-done.26 = s32[144,144]{1,0:T(8,128)S(1)} copy-done((s32[144,144]{1,0:T(8,128)S(1)}, s32[144,144]{1,0:T(8,128)}, u32[]{:S(2)}) %copy-start.26) | copy-done | bytes 82968
  1.8 0.9 %copy-done.27 = bf16[160,144]{1,0:T(8,128)(2,1)S(1)} copy-done((bf16[160,144]{1,0:T(8,128)(2,1)S(1)}, bf16[160,144]{1,0:T(8,128)(2,1)}, u32[]{:S(2)}) %copy-start.27) | copy-done | bytes 46104
  2.7 0.0 copy-start.13
  2.7 0.0 copy-start.14
  2.7 0.0 copy-start.15
  2.8 0.0 copy-start.17
  2.8 0.0 copy-start.18
  2.8 0.0 copy-start.19
  2.8 0.0 copy-start.21
  2.8 5.8 %bias_table.3 = (f32[2,1280,128]{2,1,0:T(8,128)S(1)}, s32[160,160]{1,0:T(8,128)S(1)}) custom-call(s32[144,144]{1,0:T(8,128)S(1)} %copy-done.26, bf16[160,144]{1,0:T(8,128)(2,1)S(1)} %copy-done.27, f32[6,2,3312]{2,1,0:T(2,128)S(1)} %bitcast.56), custom_call_target="tpu_custom_call" | custom-call | flops 10905190400 | bytes 1048576 | tf_op jit(solution)/shard_map/bias_table/pallas_call | solution.py:257
  8.6 0.0 copy-done.4
  8.6 0.0 copy-done.5
  8.6 0.0 copy-done.7
  8.7 0.0 copy-done.8
  8.7 0.0 copy-done.13
  8.7 0.0 copy-done.14
  8.7 0.0 copy-done.15
  8.7 0.0 copy-done.17
  8.7 0.0 copy-done.18
  8.7 0.0 copy-done.19
  8.7 0.0 copy-done.21
  8.7 0.0 copy-start.23
  8.7 0.0 copy-start.25
  8.8 5.8 %fine_plain.1 = (bf16[640,192]{1,0:T(8,128)(2,1)S(1)}, bf16[160,192]{1,0:T(8,128)(2,1)S(1)}, bf16[160,192]{1,0:T(8,128)(2,1)S(1)}) custom-call(bf16[576,192]{1,0:T(8,128)(2,1)S(1)} %bitcast.47, s32[12,24]{1,0:T(8,128)S(1)} %copy-done.18, f32[1,192]{1,0:T(1,128)S(1)} %bitcast.52, s32[1,576]{1,0:T(1,128)S(1)} %copy-done.19, bf16[640,12]{1,0:T(8,128)(2,1)S(1)} %copy-done.14, ...), custom_call_target="tpu_custom_call" | custom-call | tf_op jit(solution)/shard_map/fine_plain/pallas_call | solution.py:588
  14.6 0.0 copy-start.9
  14.6 3.0 %collective-permute-start = (bf16[4,40,192]{2,1,0:T(8,128)(2,1)S(1)}, bf16[4,40,192]{2,1,0:T(8,128)(2,1)S(1)}, u32[]{:S(2)}, u32[]{:S(2)}) collective-permute-start(bf16[4,40,192]{2,1,0:T(8,128)(2,1)S(1)} %bitcast.59), channel_id=1, source_target_pairs={{0,2},{2,4},{4,6},{6,8},{8,10},{10,12},{12,14},{14,0},{1,3},{3,5},... | collective-permute-start | bytes 184328 | tf_op jit(solution)/shard_map/ppermute | solution.py:539
  17.6 3.1 %collective-permute-start.1 = (bf16[4,40,192]{2,1,0:T(8,128)(2,1)S(1)}, bf16[4,40,192]{2,1,0:T(8,128)(2,1)S(1)}, u32[]{:S(2)}, u32[]{:S(2)}) collective-permute-start(bf16[4,40,192]{2,1,0:T(8,128)(2,1)S(1)} %bitcast.58), channel_id=1, source_target_pairs={{2,0},{4,2},{6,4},{8,6},{10,8},{12,10},{14,12},{0,14},{3,1},{5,3},... | collective-permute-start | bytes 184328 | tf_op jit(solution)/shard_map/ppermute | solution.py:540
  20.8 2.5 %collective-permute-done = bf16[4,40,192]{2,1,0:T(8,128)(2,1)S(1)} collective-permute-done((bf16[4,40,192]{2,1,0:T(8,128)(2,1)S(1)}, bf16[4,40,192]{2,1,0:T(8,128)(2,1)S(1)}, u32[]{:S(2)}, u32[]{:S(2)}) %collective-permute-start) | collective-permute-done | bytes 61472 | tf_op jit(solution)/shard_map/ppermute | solution.py:539
  23.2 0.6 collective-permute-done.1
  23.9 0.1 collective-permute-start.3
  24.0 2.2 %collective-permute-start.2 = (bf16[6,40,192]{2,1,0:T(8,128)(2,1)S(1)}, bf16[6,40,192]{2,1,0:T(8,128)(2,1)S(1)}, u32[]{:S(2)}, u32[]{:S(2)}) collective-permute-start(bf16[6,40,192]{2,1,0:T(8,128)(2,1)S(1)} %pad_maximum_fusion), channel_id=1, source_target_pairs={{0,1},{1,16},{16,17},{17,0},{2,3},{3,18},{18,19},{19,2},{4,5},{5,2... | collective-permute-start | bytes 276488 | tf_op jit(solution)/shard_map/ppermute | solution.py:545
  26.2 0.0 copy-done.23
  26.2 0.0 copy-done.25
  26.2 12.0 %bias_table.4 = f32[2,3840,128]{2,1,0:T(8,128)S(1)} custom-call(s32[160,160]{1,0:T(8,128)S(1)} %get-tuple-element.18.refs_0_, f32[6,2,3312]{2,1,0:T(2,128)S(1)} %bitcast.57, f32[12,2,3312]{2,1,0:T(2,128)S(1)} %bitcast.54), custom_call_target="tpu_custom_call" | custom-call | flops 32715571200 | bytes 1048576 | tf_op jit(solution)/shard_map/bias_table/pallas_call | solution.py:257
  38.2 0.0 copy-done.9
  38.2 0.0 copy-done.28
  38.2 0.0 copy-done.29
  38.3 1.9 %copy-done.3 = f32[2,3840,128]{2,1,0:T(8,128)} copy-done((f32[2,3840,128]{2,1,0:T(8,128)}, f32[2,3840,128]{2,1,0:T(8,128)S(1)}, u32[]{:S(2)}) %copy-start.3) | copy-done | bytes 3932184
  40.1 0.0 collective-permute-done.3
  40.1 0.0 collective-permute-done.2
  40.1 0.0 copy-start.31
  40.2 0.6 copy-done.30
  40.8 0.0 copy-done.31
  40.8 12.9 %fine_shifted_coarse_plain.1 = (bf16[640,192]{1,0:T(8,128)(2,1)}, bf16[160,384]{1,0:T(8,128)(2,1)}, bf16[80,384]{1,0:T(8,128)(2,1)}, bf16[80,384]{1,0:T(8,128)(2,1)}) custom-call(bf16[640,192]{1,0:T(8,128)(2,1)} %copy-done.9, bf16[160,192]{1,0:T(8,128)(2,1)} %bitcast.60, bf16[160,192]{1,0:T(8,128)(2,1)} %bitcast.61, bf16[240,192]{1,0:T(8,128)(2,1)} %bitcast.63, ...), custom_call_target="tpu_custom_call" | custom-call | tf_op jit(solution)/shard_map/fine_shifted_coarse_plain/pallas_call | solution.py:606
  53.7 0.7 collective-permute-start.4
  54.5 4.1 %collective-permute-start.5 = (bf16[2,40,384]{2,1,0:T(8,128)(2,1)}, bf16[2,40,384]{2,1,0:T(8,128)(2,1)S(1)}, u32[]{:S(2)}, u32[]{:S(2)}) collective-permute-start(bf16[2,40,384]{2,1,0:T(8,128)(2,1)} %bitcast.64), channel_id=1, source_target_pairs={{2,0},{4,2},{6,4},{8,6},{10,8},{12,10},{14,12},{0,14},{3,1},{5,3},... | collective-permute-start | bytes 184328 | tf_op jit(solution)/shard_map/ppermute | solution.py:540
  58.5 0.9 %slice_bitcast_fusion.2 = (bf16[2,40,384]{2,1,0:T(8,128)(2,1)S(1)}, bf16[2,40,384]{2,1,0:T(8,128)(2,1)S(1)}) fusion(bf16[2,2,40,384]{3,2,1,0:T(8,128)(2,1)} %bitcast.46), kind=kLoop, calls=%fused_computation.6 | loop fusion | bytes 245760 | tf_op jit(solution)/shard_map/squeeze | solution.py:543
  59.4 1.5 %collective-permute-done.4 = bf16[2,40,384]{2,1,0:T(8,128)(2,1)S(1)} collective-permute-done((bf16[2,40,384]{2,1,0:T(8,128)(2,1)}, bf16[2,40,384]{2,1,0:T(8,128)(2,1)S(1)}, u32[]{:S(2)}, u32[]{:S(2)}) %collective-permute-start.4) | collective-permute-done | bytes 61472 | tf_op jit(solution)/shard_map/ppermute | solution.py:539
  60.9 0.0 collective-permute-done.5
  61.0 0.1 collective-permute-start.7
  61.1 0.0 copy-start
  61.1 0.0 copy-start.1
  61.1 0.0 copy-start.2
  61.1 0.0 copy-start.6
  61.1 0.0 copy-start.10
  61.1 0.0 copy-start.16
  61.2 0.0 copy-start.20
  61.2 0.0 copy-start.22
  61.2 2.3 %collective-permute-start.6 = (bf16[4,40,384]{2,1,0:T(8,128)(2,1)S(1)}, bf16[4,40,384]{2,1,0:T(8,128)(2,1)S(1)}, u32[]{:S(2)}, u32[]{:S(2)}) collective-permute-start(bf16[4,40,384]{2,1,0:T(8,128)(2,1)S(1)} %pad_maximum_fusion.2), channel_id=1, source_target_pairs={{0,1},{1,16},{16,17},{17,0},{2,3},{3,18},{18,19},{19,2},{4,5},{5,2... | collective-permute-start | bytes 368648 | tf_op jit(solution)/shard_map/ppermute | solution.py:545
  63.5 8.1 %bias_table.5 = f32[2,2560,128]{2,1,0:T(8,128)S(1)} custom-call(s32[160,160]{1,0:T(8,128)S(1)} %get-tuple-element.18.refs_0_, f32[12,2,3312]{2,1,0:T(2,128)S(1)} %bitcast.55), custom_call_target="tpu_custom_call" | custom-call | flops 21810380800 | bytes 1048576 | tf_op jit(solution)/shard_map/bias_table/pallas_call | solution.py:257
  71.6 0.0 collective-permute-done.7
  71.6 0.0 collective-permute-done.6
  71.7 7.9 %coarse_shifted_expand.1 = bf16[576,192]{1,0:T(8,128)(2,1)} custom-call(bf16[160,384]{1,0:T(8,128)(2,1)S(1)} %copy-done.11, bf16[80,384]{1,0:T(8,128)(2,1)S(1)} %bitcast.48, bf16[80,384]{1,0:T(8,128)(2,1)S(1)} %bitcast.49, bf16[160,384]{1,0:T(8,128)(2,1)S(1)} %bitcast.51, bf16[160,384]{1,0:T(8,128)(2,1)S(1)} %bitcast.50, f32[2,2,384]{2,1,0:T(2,128)S(1)} %copy-done.16, ...), custom_call_target="tpu_custom_call" | custom-call | tf_op jit(solution)/shard_map/coarse_shifted_expand/pallas_call | solution.py:628
  (32 shorter events, 0.2 us)
Async XLA Ops:
  0.0 0.9 %copy-start.24 = (f32[2,6,3312]{2,0,1:T(2,128)S(1)}, f32[2,6,3312]{2,0,1:T(2,128)}, u32[]{:S(2)}) copy-start(f32[2,6,3312]{2,0,1:T(2,128)} %param.30) | copy-start | bytes 476932
  0.9 0.9 %copy-start.26 = (s32[144,144]{1,0:T(8,128)S(1)}, s32[144,144]{1,0:T(8,128)}, u32[]{:S(2)}) copy-start(s32[144,144]{1,0:T(8,128)} %refs_0_.1) | copy-start | bytes 248836
  1.8 0.9 %copy-start.27 = (bf16[160,144]{1,0:T(8,128)(2,1)S(1)}, bf16[160,144]{1,0:T(8,128)(2,1)}, u32[]{:S(2)}) copy-start(bf16[160,144]{1,0:T(8,128)(2,1)} %constant.12.clone.refs_1_) | copy-start | bytes 138244
  2.7 5.9 %copy-start.4 = (bf16[2,192,768]{2,1,0:T(8,128)(2,1)S(1)}, bf16[2,192,768]{2,1,0:T(8,128)(2,1)}, u32[]{:S(2)}) copy-start(bf16[2,192,768]{2,1,0:T(8,128)(2,1)} %widen_hbm.4) | copy-start | bytes 1769476
  2.7 5.9 %copy-start.5 = (bf16[2,768,192]{1,2,0:T(8,128)(2,1)S(1)}, bf16[2,768,192]{1,2,0:T(8,128)(2,1)}, u32[]{:S(2)}) copy-start(bf16[2,768,192]{1,2,0:T(8,128)(2,1)} %param.35) | copy-start | bytes 1769476
  2.7 5.9 %copy-start.7 = (bf16[2,192,576]{2,1,0:T(8,128)(2,1)S(1)}, bf16[2,192,576]{2,1,0:T(8,128)(2,1)}, u32[]{:S(2)}) copy-start(bf16[2,192,576]{2,1,0:T(8,128)(2,1)} %triple_hbm.4) | copy-start | bytes 1327108
  2.7 5.9 %copy-start.8 = (bf16[2,192,192]{2,1,0:T(8,128)(2,1)S(1)}, bf16[2,192,192]{2,1,0:T(8,128)(2,1)}, u32[]{:S(2)}) copy-start(bf16[2,192,192]{2,1,0:T(8,128)(2,1)} %project_hbm.4) | copy-start | bytes 442372
  2.7 5.9 %copy-start.13 = (bf16[2,12,24,192]{3,2,1,0:T(8,128)(2,1)S(1)}, bf16[2,12,24,192]{3,2,1,0:T(8,128)(2,1)}, u32[]{:S(2)}) copy-start(bf16[2,12,24,192]{3,2,1,0:T(8,128)(2,1)} %param.26) | copy-start | bytes 663556
  2.7 5.9 %copy-start.14 = (bf16[640,12]{1,0:T(8,128)(2,1)S(1)}, bf16[640,12]{1,0:T(8,128)(2,1)}, u32[]{:S(2)}) copy-start(bf16[640,12]{1,0:T(8,128)(2,1)} %constant.14.clone.of_row_ref) | copy-start | bytes 46084
  2.7 5.9 %copy-start.15 = (bf16[640,24]{1,0:T(8,128)(2,1)S(1)}, bf16[640,24]{1,0:T(8,128)(2,1)}, u32[]{:S(2)}) copy-start(bf16[640,24]{1,0:T(8,128)(2,1)} %constant.15.clone.of_col_ref) | copy-start | bytes 92164
  2.8 5.9 %copy-start.17 = (f32[2,2,192]{2,1,0:T(2,128)S(1)}, f32[2,2,192]{2,1,0:T(2,128)}, u32[]{:S(2)}) copy-start(f32[2,2,192]{2,1,0:T(2,128)} %gains_ref.4) | copy-start | bytes 9220
  2.8 5.9 %copy-start.18 = (s32[12,24]{1,0:T(8,128)S(1)}, s32[12,24]{1,0:T(8,128)}, u32[]{:S(2)}) copy-start(s32[12,24]{1,0:T(8,128)} %land_ref.1) | copy-start | bytes 3460
  2.8 5.9 %copy-start.19 = (s32[1,576]{1,0:T(1,128)S(1)}, s32[1,576]{1,0:T(1,128)}, u32[]{:S(2)}) copy-start(s32[1,576]{1,0:T(1,128)} %constant.13.clone.order_ref) | copy-start | bytes 6916
  2.8 5.9 %copy-start.21 = (f32[192]{0:T(256)S(1)}, f32[192]{0:T(256)}, u32[]{:S(2)}) copy-start(f32[192]{0:T(256)} %param.28) | copy-start | bytes 2308
  8.7 17.5 %copy-start.23 = (f32[2,12,3312]{2,0,1:T(2,128)S(1)}, f32[2,12,3312]{2,0,1:T(2,128)}, u32[]{:S(2)}) copy-start(f32[2,12,3312]{2,0,1:T(2,128)} %param.38) | copy-start | bytes 953860
  8.7 17.5 %copy-start.25 = (f32[2,6,3312]{2,0,1:T(2,128)S(1)}, f32[2,6,3312]{2,0,1:T(2,128)}, u32[]{:S(2)}) copy-start(f32[2,6,3312]{2,0,1:T(2,128)} %param.30) | copy-start | bytes 476932
  14.6 23.6 %copy-start.9 = (bf16[640,192]{1,0:T(8,128)(2,1)}, bf16[640,192]{1,0:T(8,128)(2,1)S(1)}, u32[]{:S(2)}) copy-start(bf16[640,192]{1,0:T(8,128)(2,1)S(1)} %get-tuple-element.15.own_ref) | copy-start | bytes 737284
  14.6 8.6 %collective-permute-start = (bf16[4,40,192]{2,1,0:T(8,128)(2,1)S(1)}, bf16[4,40,192]{2,1,0:T(8,128)(2,1)S(1)}, u32[]{:S(2)}, u32[]{:S(2)}) collective-permute-start(bf16[4,40,192]{2,1,0:T(8,128)(2,1)S(1)} %bitcast.59), channel_id=1, source_target_pairs={{0,2},{2,4},{4,6},{6,8},{8,10},{10,12},{12,14},{14,0},{1,3},{3,5},... | collective-permute-start | bytes 184328 | tf_op jit(solution)/shard_map/ppermute | solution.py:539
  17.6 6.2 %collective-permute-start.1 = (bf16[4,40,192]{2,1,0:T(8,128)(2,1)S(1)}, bf16[4,40,192]{2,1,0:T(8,128)(2,1)S(1)}, u32[]{:S(2)}, u32[]{:S(2)}) collective-permute-start(bf16[4,40,192]{2,1,0:T(8,128)(2,1)S(1)} %bitcast.58), channel_id=1, source_target_pairs={{2,0},{4,2},{6,4},{8,6},{10,8},{12,10},{14,12},{0,14},{3,1},{5,3},... | collective-permute-start | bytes 184328 | tf_op jit(solution)/shard_map/ppermute | solution.py:540
  23.2 15.0 %copy-start.28 = (bf16[4,40,192]{2,1,0:T(8,128)(2,1)}, bf16[4,40,192]{2,1,0:T(8,128)(2,1)S(1)}, u32[]{:S(2)}) copy-start(bf16[4,40,192]{2,1,0:T(8,128)(2,1)S(1)} %collective-permute-done) | copy-start | bytes 184324
  23.8 14.4 %copy-start.29 = (bf16[4,40,192]{2,1,0:T(8,128)(2,1)}, bf16[4,40,192]{2,1,0:T(8,128)(2,1)S(1)}, u32[]{:S(2)}) copy-start(bf16[4,40,192]{2,1,0:T(8,128)(2,1)S(1)} %collective-permute-done.1) | copy-start | bytes 184324
  23.9 16.3 %collective-permute-start.3 = (bf16[6,40,192]{2,1,0:T(8,128)(2,1)S(1)}, bf16[6,40,192]{2,1,0:T(8,128)(2,1)S(1)}, u32[]{:S(2)}, u32[]{:S(2)}) collective-permute-start(bf16[6,40,192]{2,1,0:T(8,128)(2,1)S(1)} %pad_maximum_fusion.1), channel_id=1, source_target_pairs={{1,0},{16,1},{17,16},{0,17},{3,2},{18,3},{19,18},{2,19},{5,4},{20,... | collective-permute-start | bytes 276488 | tf_op jit(solution)/shard_map/ppermute | solution.py:546
  24.0 16.2 %collective-permute-start.2 = (bf16[6,40,192]{2,1,0:T(8,128)(2,1)S(1)}, bf16[6,40,192]{2,1,0:T(8,128)(2,1)S(1)}, u32[]{:S(2)}, u32[]{:S(2)}) collective-permute-start(bf16[6,40,192]{2,1,0:T(8,128)(2,1)S(1)} %pad_maximum_fusion), channel_id=1, source_target_pairs={{0,1},{1,16},{16,17},{17,0},{2,3},{3,18},{18,19},{19,2},{4,5},{5,2... | collective-permute-start | bytes 276488 | tf_op jit(solution)/shard_map/ppermute | solution.py:545
  38.3 1.9 %copy-start.3 = (f32[2,3840,128]{2,1,0:T(8,128)}, f32[2,3840,128]{2,1,0:T(8,128)S(1)}, u32[]{:S(2)}) copy-start(f32[2,3840,128]{2,1,0:T(8,128)S(1)} %bias_table.4) | copy-start | bytes 11796484
  40.1 0.7 copy-start.30
  40.1 0.7 copy-start.31
  53.7 7.2 %collective-permute-start.4 = (bf16[2,40,384]{2,1,0:T(8,128)(2,1)}, bf16[2,40,384]{2,1,0:T(8,128)(2,1)S(1)}, u32[]{:S(2)}, u32[]{:S(2)}) collective-permute-start(bf16[2,40,384]{2,1,0:T(8,128)(2,1)} %bitcast.65), channel_id=1, source_target_pairs={{0,2},{2,4},{4,6},{6,8},{8,10},{10,12},{12,14},{14,0},{1,3},{3,5},... | collective-permute-start | bytes 184328 | tf_op jit(solution)/shard_map/ppermute | solution.py:539
  54.5 6.5 %collective-permute-start.5 = (bf16[2,40,384]{2,1,0:T(8,128)(2,1)}, bf16[2,40,384]{2,1,0:T(8,128)(2,1)S(1)}, u32[]{:S(2)}, u32[]{:S(2)}) collective-permute-start(bf16[2,40,384]{2,1,0:T(8,128)(2,1)} %bitcast.64), channel_id=1, source_target_pairs={{2,0},{4,2},{6,4},{8,6},{10,8},{12,10},{14,12},{0,14},{3,1},{5,3},... | collective-permute-start | bytes 184328 | tf_op jit(solution)/shard_map/ppermute | solution.py:540
  61.0 10.6 %collective-permute-start.7 = (bf16[4,40,384]{2,1,0:T(8,128)(2,1)S(1)}, bf16[4,40,384]{2,1,0:T(8,128)(2,1)S(1)}, u32[]{:S(2)}, u32[]{:S(2)}) collective-permute-start(bf16[4,40,384]{2,1,0:T(8,128)(2,1)S(1)} %pad_maximum_fusion.3), channel_id=1, source_target_pairs={{1,0},{16,1},{17,16},{0,17},{3,2},{18,3},{19,18},{2,19},{5,4},{20,... | collective-permute-start | bytes 368648 | tf_op jit(solution)/shard_map/ppermute | solution.py:546
  61.1 10.5 %copy-start = (bf16[2,384,1536]{2,1,0:T(8,128)(2,1)S(1)}, bf16[2,384,1536]{2,1,0:T(8,128)(2,1)}, u32[]{:S(2)}) copy-start(bf16[2,384,1536]{2,1,0:T(8,128)(2,1)} %widen_hbm.5) | copy-start | bytes 7077892
  61.1 10.5 %copy-start.1 = (bf16[2,1536,384]{2,1,0:T(8,128)(2,1)S(1)}, bf16[2,1536,384]{2,1,0:T(8,128)(2,1)}, u32[]{:S(2)}) copy-start(bf16[2,1536,384]{2,1,0:T(8,128)(2,1)} %narrow_hbm.1) | copy-start | bytes 7077892
  61.1 10.5 %copy-start.2 = (bf16[2,384,1152]{2,1,0:T(8,128)(2,1)S(1)}, bf16[2,384,1152]{2,1,0:T(8,128)(2,1)}, u32[]{:S(2)}) copy-start(bf16[2,384,1152]{2,1,0:T(8,128)(2,1)} %triple_hbm.5) | copy-start | bytes 5308420
  61.1 10.5 %copy-start.6 = (bf16[2,384,384]{2,1,0:T(8,128)(2,1)S(1)}, bf16[2,384,384]{2,1,0:T(8,128)(2,1)}, u32[]{:S(2)}) copy-start(bf16[2,384,384]{2,1,0:T(8,128)(2,1)} %project_hbm.5) | copy-start | bytes 1769476
  61.1 10.5 %copy-start.10 = (bf16[384,768]{1,0:T(8,128)(2,1)S(1)}, bf16[384,768]{1,0:T(8,128)(2,1)}, u32[]{:S(2)}) copy-start(bf16[384,768]{1,0:T(8,128)(2,1)} %expand_weight_hbm.1) | copy-start | bytes 1769476
  61.1 10.5 %copy-start.11 = (bf16[160,384]{1,0:T(8,128)(2,1)S(1)}, bf16[160,384]{1,0:T(8,128)(2,1)}, u32[]{:S(2)}) copy-start(bf16[160,384]{1,0:T(8,128)(2,1)} %get-tuple-element.19.own_ref) | copy-start | bytes 368644
  61.1 10.5 %copy-start.12 = (bf16[640,192]{1,0:T(8,128)(2,1)S(1)}, bf16[640,192]{1,0:T(8,128)(2,1)}, u32[]{:S(2)}) copy-start(bf16[640,192]{1,0:T(8,128)(2,1)} %get-tuple-element.22.parts_ref) | copy-start | bytes 737284
  61.1 10.5 %copy-start.16 = (f32[2,2,384]{2,1,0:T(2,128)S(1)}, f32[2,2,384]{2,1,0:T(2,128)}, u32[]{:S(2)}) copy-start(f32[2,2,384]{2,1,0:T(2,128)} %gains_ref.5) | copy-start | bytes 18436
  61.2 10.5 %copy-start.20 = (s32[1,640]{1,0:T(1,128)S(1)}, s32[1,640]{1,0:T(1,128)}, u32[]{:S(2)}) copy-start(s32[1,640]{1,0:T(1,128)} %constant.17.clone.expand_order_ref) | copy-start | bytes 7684
  61.2 10.5 %copy-start.22 = (f32[192]{0:T(256)S(1)}, f32[192]{0:T(256)}, u32[]{:S(2)}) copy-start(f32[192]{0:T(256)} %param.45) | copy-start | bytes 2308
  61.2 10.4 %collective-permute-start.6 = (bf16[4,40,384]{2,1,0:T(8,128)(2,1)S(1)}, bf16[4,40,384]{2,1,0:T(8,128)(2,1)S(1)}, u32[]{:S(2)}, u32[]{:S(2)}) collective-permute-start(bf16[4,40,384]{2,1,0:T(8,128)(2,1)S(1)} %pad_maximum_fusion.2), channel_id=1, source_target_pairs={{0,1},{1,16},{16,17},{17,0},{2,3},{3,18},{18,19},{19,2},{4,5},{5,2... | collective-permute-start | bytes 368648 | tf_op jit(solution)/shard_map/ppermute | solution.py:545

commit v5 on v4

--- a/solution.py
+++ b/solution.py
@@ -112,7 +112,7 @@
     return centered * lax.rsqrt(variance + 1e-05) * gain
 
 
-def attend(q, k, v, bias_ref, first, key_mask):
+def attend(q, k, v, bias_ref, firsts, key_mask):
     n = q.shape[0]
     channels = q.shape[1]
     scale = HEAD**-0.5 * LOG2E
@@ -130,8 +130,11 @@
             head = tile // HEAD + h
             bias = jnp.concatenate(
                 [
-                    bias_ref[0, head, first : first + n, :],
-                    bias_ref[1, head, first : first + n, : WP - 128],
+                    jnp.concatenate(
+                        [bias_ref[half, head, f : f + n // len(firsts), :width] for f in firsts],
+                        axis=0,
+                    )
+                    for half, width in ((0, 128), (1, WP - 128))
                 ],
                 axis=1,
             )
@@ -168,6 +171,21 @@
     return -(-heads // 8) * 8
 
 
+def halved(heads):
+    return heads % 8 == 4
+
+
+def row_groups(head_counts):
+    groups = []
+    at = 0
+    for heads in head_counts:
+        count = padded(heads) // 8
+        for g in range(count):
+            groups.append((at + g * 8, 2 if halved(heads) and g == count - 1 else 1))
+        at += padded(heads)
+    return groups
+
+
 def bias_kernel(*refs, picks, fresh):
     if fresh:
         index_ref, spread_ref, *table_refs, out_ref, index, table, left = refs
@@ -175,6 +193,7 @@
         index, *table_refs, out_ref, table, left = refs
     rows = table.shape[0]
     bias_len = table_refs[0].shape[-1]
+    groups = row_groups([t.shape[0] for t in table_refs])
 
     @pl.when(pl.program_id(0) == 0)
     def _():
@@ -194,59 +213,80 @@
         for table_ref, block in zip(table_refs, picks):
             heads = table_ref.shape[0]
             for h in range(heads):
-                table[at + h : at + h + 1, :bias_len] = (
-                    table_ref[h, block : block + 1, :] * LOG2E
-                )
+                line = table_ref[h, block : block + 1, :] * LOG2E
+                table[at + h : at + h + 1, :bias_len] = line
+                if halved(heads) and h >= heads - 4:
+                    table[at + h + 4 : at + h + 5, : bias_len - 256] = line[:, 256:]
             at += padded(heads)
         values = table[...]
         big = values.astype(BF16)
         small = (values - big.astype(F32)).astype(BF16)
         for n, part in enumerate((big, small)):
             left[:, n * 256 : (n + 1) * 256] = jnp.concatenate(
-                [part[:, i * 256 : (i + 1) * 256] for i in range(LO_COUNT)], axis=0
+                [
+                    part[row : row + 8, i * 256 : (i + 1) * 256]
+                    for row, stride in groups
+                    for i in range(0, LO_COUNT, stride)
+                ],
+                axis=0,
             )
 
     ladder = lax.broadcasted_iota(jnp.int32, (256, 256), 0).astype(F32).astype(BF16)
     lane = lax.broadcasted_iota(jnp.int32, (8, 256), 1) // 32
     sublane = lax.broadcasted_iota(jnp.int32, (8, 256), 0)
+    low_half = lax.broadcasted_iota(jnp.int32, (8, 256), 0) // 4
     span = out_ref.shape[1] // rows
     for group in range(span // 8):
         first = pl.multiple_of(pl.program_id(0) * span + group * 8, 8)
+        count = min(8, QUAD - group * 8)
         entries = index[pl.ds(first, 8), :]
         rest = jnp.concatenate([entries[:, 128:]] * 8, axis=1)
         rest = jnp.sum(jnp.where(lane == sublane, rest, 0).astype(F32), axis=0, keepdims=True)
         pieces = [
             jnp.concatenate([entries[j : j + 1, :128], entries[j + 1 : j + 2, :128]], axis=1)
-            for j in range(0, 8, 2)
+            for j in range(0, count, 2)
         ] + [rest.astype(jnp.int32)]
         for t, entry in enumerate(pieces):
             near = (entry & 255).astype(F32).astype(BF16)
             far = entry >> 8
             chosen = jnp.where(ladder == near, jnp.ones((), BF16), jnp.zeros((), BF16))
             found = dot(left[...], jnp.concatenate([chosen, chosen], axis=0))
-            total = found[:rows]
-            for i in range(1, LO_COUNT):
-                total = jnp.where(far == i, found[i * rows : (i + 1) * rows], total)
-            for h in range(0, rows, 8):
-                part = total[h : h + 8]
-                at = h * span + group * 8
-                if t < 4:
+            shifted_far = far - low_half
+            unit = 0
+            for row, stride in groups:
+                part = found[unit : unit + 8]
+                unit += 8
+                for i in range(stride, LO_COUNT, stride):
+                    here = (far if stride == 1 else shifted_far) == i
+                    part = jnp.where(here, found[unit : unit + 8], part)
+                    unit += 8
+                if stride == 2:
+                    part = jnp.where((far & 1) == 0, part, pltpu.roll(part, 4, 0))
+                at = row * span + group * 8
+                if t < len(pieces) - 1:
                     for j in range(2):
                         out_ref[0, pl.ds(at + 2 * t + j, 8, stride=span), :] = (
                             part[:, j * 128 : (j + 1) * 128]
                         )
                 else:
-                    for j in range(8):
+                    for j in range(count):
                         moved_part = part[:, j // 4 * 128 : (j // 4 + 1) * 128]
                         if j % 4:
                             moved_part = pltpu.roll(moved_part, 128 - 32 * (j % 4), 1)
                         out_ref[1, pl.ds(at + j, 8, stride=span), :] = moved_part
-
-
-def bias_of(picks, order, vmem, span=32):
+        for row, _ in groups:
+            for j in range(count, 8):
+                for half in range(2):
+                    out_ref[half, pl.ds(row * span + group * 8 + j, 8, stride=span), :] = (
+                        jnp.zeros((8, 128), F32)
+                    )
+
+
+def bias_of(picks, order, vmem, span=QP):
     tables = [t.transpose(1, 0, 2) for t, _ in picks]
     rows = sum(padded(t.shape[0]) for t in tables)
-    flops = 2 * WP * 256 * WP * LO_COUNT * rows * 4
+    units = sum(-(-LO_COUNT // stride) for _, stride in row_groups([t.shape[0] for t in tables]))
+    flops = 2 * WP * 256 * WP * units * 8 * 4
     steps = WP // span
     fresh = len(order) == 2
     out_shape = [jax.ShapeDtypeStruct((2, steps * rows * span, 128), F32)]
@@ -262,7 +302,7 @@
         out_specs=out_specs,
         scratch_shapes=[
             pltpu.VMEM((rows, LO_COUNT * 256), F32),
-            pltpu.VMEM((rows * LO_COUNT, 512), BF16),
+            pltpu.VMEM((units * 8, 512), BF16),
         ],
         compiler_params=pltpu.CompilerParams(vmem_limit_bytes=vmem << 20),
         cost_estimate=pl.CostEstimate(flops=2 * flops, bytes_accessed=1 << 20, transcendentals=0),
@@ -333,7 +373,7 @@
                 window[:, :channels],
                 window[:, channels : 2 * channels],
                 window[:, 2 * channels :],
-                bias, 0, None,
+                bias, [0], None,
             ).astype(BF16)
             context[top : top + 2 * QP] = mixed[: 2 * QP]
             context[below : below + 2 * QP] = mixed[2 * QP :]
@@ -399,17 +439,13 @@
                 ]
                 for r in rows
             ]
-            if len(cols) == 2:
-                groups = [(rows, jnp.concatenate(qs, axis=0) if len(qs) == 2 else qs[0])]
-            else:
-                groups = [([r], part) for r, part in zip(rows, qs)]
-            for group, q in groups:
-                out = attend(
-                    q.astype(BF16), k, v, bias, (2 * group[0] + cols[0]) * QP, mask
-                )
-                for n, r in enumerate(group):
-                    to = ((2 * wa + r - 1) * across + 2 * wb + cols[0] - 1) * QP
-                    context[to : to + size] = out[n * size : (n + 1) * size]
+            out = attend(
+                jnp.concatenate(qs, axis=0).astype(BF16), k, v, bias,
+                [(2 * r + cols[0]) * QP for r in rows], mask,
+            )
+            for n, r in enumerate(rows):
+                to = ((2 * wa + r - 1) * across + 2 * wb + cols[0] - 1) * QP
+                context[to : to + size] = out[n * size : (n + 1) * size]
     fetched.wait(2, 3, 4)
     return finish(
         own_ref[...].astype(F32), context[...].astype(BF16), gains_ref[1, 1:2],
@@ -475,7 +511,7 @@
     fetched.wait(6, 7)
     triple = dot(normed, c_triple[...]).astype(BF16)
     mixed = attend(
-        triple[:, :wide], triple[:, wide : 2 * wide], triple[:, 2 * wide :], c_bias, 0, None
+        triple[:, :wide], triple[:, wide : 2 * wide], triple[:, 2 * wide :], c_bias, [0], None
     ).astype(BF16)
     fetched.wait(8, 9, 10)
     done = finish(

time: 80 us -> 70.7 us (0.88)
  Pallas kernels: 52.5 us -> 43.2 us
    pallas_call x3, Pallas kernels: 25.9 us -> 17.7 us  [bias_of(): pl.pallas_call(functools.partial(bias_kernel, picks=tuple((b for _, b in...]
    pallas_call x1, Pallas kernels: 12.9 us -> 11.9 us  [on_device(): pl.pallas_call(middle_kernel, out_shape=[jax.ShapeDtypeStruct((tokens, ch...]
  transfers between devices with their start and end apart: 8 -> 8, of which waited for: 3 -> 3; matrix products, arithmetic and copies ran while one was open for 1% -> 1% of each run, Pallas kernels for 25% -> 19%
where the time goes in v5:
time: 70.7 us; the launch traced here: 70.4 us
  Pallas kernels  43.2 us (61%)
  starting transfers between devices  15.5 us (22%)
  local copies, waits for them, and re-layouts  6.3 us (9%)
  waiting for transfers between devices  4.61 us (7%)
    pallas_call x3, Pallas kernels, bias_of(): pl.pallas_call(functools.partial(bias_kernel, picks=tuple((b for _, b in...  17.7 us
    pallas_call x1, Pallas kernels, on_device(): pl.pallas_call(middle_kernel, out_shape=[jax.ShapeDtypeStruct((tokens, ch...  11.9 us
    pallas_call x1, Pallas kernels, on_device(): pl.pallas_call(last_kernel, out_shape=jax.ShapeDtypeStruct((LEVELS * rows...  7.79 us
    ppermute x2, starting transfers between devices, halo(): south = lax.ppermute(top, 'lat', up)  7.17 us
    pallas_call x1, Pallas kernels, on_device(): pl.pallas_call(first_kernel, out_shape=[jax.ShapeDtypeStruct((tokens, cha...  5.82 us
    unnamed x64, local copies, waits for them, and re-layouts  5.39 us
    ppermute x2, starting transfers between devices, halo(): from_west = lax.ppermute(side(cols - 1), LON, east)  4.52 us
    ppermute x2, waiting for transfers between devices, halo(): north = lax.ppermute(bottom, 'lat', down)  4 us
  transfers between devices with their start and end apart: 8, of which 3 were waited for; matrix products, arithmetic and copies ran while one was open for 1% of the time, Pallas kernels for 19%

profile of v5, /device:TPU:0, one launch (start us, length us, event | category | flops | bytes accessed | tf_op | source)
XLA Modules:
  0.0 70.4 jit_solution(10026794198402979235)
XLA Ops:
  0.0 0.9 %copy-done.24 = f32[2,6,3312]{2,0,1:T(2,128)S(1)} copy-done((f32[2,6,3312]{2,0,1:T(2,128)S(1)}, f32[2,6,3312]{2,0,1:T(2,128)}, u32[]{:S(2)}) %copy-start.24) | copy-done | bytes 159000
  0.9 0.9 %copy-done.26 = s32[144,144]{1,0:T(8,128)S(1)} copy-done((s32[144,144]{1,0:T(8,128)S(1)}, s32[144,144]{1,0:T(8,128)}, u32[]{:S(2)}) %copy-start.26) | copy-done | bytes 82968
  1.8 0.9 %copy-done.27 = bf16[160,144]{1,0:T(8,128)(2,1)S(1)} copy-done((bf16[160,144]{1,0:T(8,128)(2,1)S(1)}, bf16[160,144]{1,0:T(8,128)(2,1)}, u32[]{:S(2)}) %copy-start.27) | copy-done | bytes 46104
  2.7 0.0 copy-start.13
  2.7 0.0 copy-start.14
  2.7 0.0 copy-start.15
  2.8 0.0 copy-start.17
  2.8 0.0 copy-start.18
  2.8 0.0 copy-start.19
  2.8 0.0 copy-start.21
  2.8 4.7 %bias_table.3 = (f32[2,1280,128]{2,1,0:T(8,128)S(1)}, s32[160,160]{1,0:T(8,128)S(1)}) custom-call(s32[144,144]{1,0:T(8,128)S(1)} %copy-done.26, bf16[160,144]{1,0:T(8,128)(2,1)S(1)} %copy-done.27, f32[6,2,3312]{2,1,0:T(2,128)S(1)} %bitcast.56), custom_call_target="tpu_custom_call" | custom-call | flops 10905190400 | bytes 1048576 | tf_op jit(solution)/shard_map/bias_table/pallas_call | solution.py:297
  7.5 0.0 copy-done.4
  7.5 0.0 copy-done.5
  7.5 0.0 copy-done.7
  7.5 0.0 copy-done.8
  7.5 0.0 copy-done.13
  7.5 0.0 copy-done.14
  7.5 0.0 copy-done.15
  7.5 0.0 copy-done.17
  7.5 0.0 copy-done.18
  7.6 0.0 copy-done.19
  7.6 0.0 copy-done.21
  7.6 0.0 copy-start.23
  7.6 0.0 copy-start.25
  7.6 5.8 %fine_plain.1 = (bf16[640,192]{1,0:T(8,128)(2,1)S(1)}, bf16[160,192]{1,0:T(8,128)(2,1)S(1)}, bf16[160,192]{1,0:T(8,128)(2,1)S(1)}) custom-call(bf16[576,192]{1,0:T(8,128)(2,1)S(1)} %bitcast.47, s32[12,24]{1,0:T(8,128)S(1)} %copy-done.18, f32[1,192]{1,0:T(1,128)S(1)} %bitcast.52, s32[1,576]{1,0:T(1,128)S(1)} %copy-done.19, bf16[640,12]{1,0:T(8,128)(2,1)S(1)} %copy-done.14, ...), custom_call_target="tpu_custom_call" | custom-call | tf_op jit(solution)/shard_map/fine_plain/pallas_call | solution.py:624
  13.4 0.0 copy-start.9
  13.4 3.0 %collective-permute-start = (bf16[4,40,192]{2,1,0:T(8,128)(2,1)S(1)}, bf16[4,40,192]{2,1,0:T(8,128)(2,1)S(1)}, u32[]{:S(2)}, u32[]{:S(2)}) collective-permute-start(bf16[4,40,192]{2,1,0:T(8,128)(2,1)S(1)} %bitcast.59), channel_id=1, source_target_pairs={{0,2},{2,4},{4,6},{6,8},{8,10},{10,12},{12,14},{14,0},{1,3},{3,5},... | collective-permute-start | bytes 184328 | tf_op jit(solution)/shard_map/ppermute | solution.py:575
  16.5 3.1 %collective-permute-start.1 = (bf16[4,40,192]{2,1,0:T(8,128)(2,1)S(1)}, bf16[4,40,192]{2,1,0:T(8,128)(2,1)S(1)}, u32[]{:S(2)}, u32[]{:S(2)}) collective-permute-start(bf16[4,40,192]{2,1,0:T(8,128)(2,1)S(1)} %bitcast.58), channel_id=1, source_target_pairs={{2,0},{4,2},{6,4},{8,6},{10,8},{12,10},{14,12},{0,14},{3,1},{5,3},... | collective-permute-start | bytes 184328 | tf_op jit(solution)/shard_map/ppermute | solution.py:576
  19.6 2.5 %collective-permute-done = bf16[4,40,192]{2,1,0:T(8,128)(2,1)S(1)} collective-permute-done((bf16[4,40,192]{2,1,0:T(8,128)(2,1)S(1)}, bf16[4,40,192]{2,1,0:T(8,128)(2,1)S(1)}, u32[]{:S(2)}, u32[]{:S(2)}) %collective-permute-start) | collective-permute-done | bytes 61472 | tf_op jit(solution)/shard_map/ppermute | solution.py:575
  22.1 0.6 collective-permute-done.1
  22.7 0.1 collective-permute-start.3
  22.8 2.2 %collective-permute-start.2 = (bf16[6,40,192]{2,1,0:T(8,128)(2,1)S(1)}, bf16[6,40,192]{2,1,0:T(8,128)(2,1)S(1)}, u32[]{:S(2)}, u32[]{:S(2)}) collective-permute-start(bf16[6,40,192]{2,1,0:T(8,128)(2,1)S(1)} %pad_maximum_fusion), channel_id=1, source_target_pairs={{0,1},{1,16},{16,17},{17,0},{2,3},{3,18},{18,19},{19,2},{4,5},{5,2... | collective-permute-start | bytes 276488 | tf_op jit(solution)/shard_map/ppermute | solution.py:581
  25.0 0.0 copy-done.23
  25.0 0.0 copy-done.25
  25.0 7.9 %bias_table.4 = f32[2,3840,128]{2,1,0:T(8,128)S(1)} custom-call(s32[160,160]{1,0:T(8,128)S(1)} %get-tuple-element.18.refs_0_, f32[6,2,3312]{2,1,0:T(2,128)S(1)} %bitcast.57, f32[12,2,3312]{2,1,0:T(2,128)S(1)} %bitcast.54), custom_call_target="tpu_custom_call" | custom-call | flops 27682406400 | bytes 1048576 | tf_op jit(solution)/shard_map/bias_table/pallas_call | solution.py:297
  33.0 0.0 copy-done.9
  33.0 0.0 copy-done.28
  33.0 0.0 copy-done.29
  33.0 1.9 %copy-done.3 = f32[2,3840,128]{2,1,0:T(8,128)} copy-done((f32[2,3840,128]{2,1,0:T(8,128)}, f32[2,3840,128]{2,1,0:T(8,128)S(1)}, u32[]{:S(2)}) %copy-start.3) | copy-done | bytes 3932184
  34.9 0.0 collective-permute-done.3
  34.9 0.0 collective-permute-done.2
  34.9 0.0 copy-start.31
  34.9 0.6 copy-done.30
  35.5 0.0 copy-done.31
  35.6 11.9 %fine_shifted_coarse_plain.1 = (bf16[640,192]{1,0:T(8,128)(2,1)}, bf16[160,384]{1,0:T(8,128)(2,1)}, bf16[80,384]{1,0:T(8,128)(2,1)}, bf16[80,384]{1,0:T(8,128)(2,1)}) custom-call(bf16[640,192]{1,0:T(8,128)(2,1)} %copy-done.9, bf16[160,192]{1,0:T(8,128)(2,1)} %bitcast.60, bf16[160,192]{1,0:T(8,128)(2,1)} %bitcast.61, bf16[240,192]{1,0:T(8,128)(2,1)} %bitcast.63, ...), custom_call_target="tpu_custom_call" | custom-call | tf_op jit(solution)/shard_map/fine_shifted_coarse_plain/pallas_call | solution.py:642
  47.5 0.7 %collective-permute-start.4 = (bf16[2,40,384]{2,1,0:T(8,128)(2,1)}, bf16[2,40,384]{2,1,0:T(8,128)(2,1)S(1)}, u32[]{:S(2)}, u32[]{:S(2)}) collective-permute-start(bf16[2,40,384]{2,1,0:T(8,128)(2,1)} %bitcast.65), channel_id=1, source_target_pairs={{0,2},{2,4},{4,6},{6,8},{8,10},{10,12},{12,14},{14,0},{1,3},{3,5},... | collective-permute-start | bytes 184328 | tf_op jit(solution)/shard_map/ppermute | solution.py:575
  48.2 4.1 %collective-permute-start.5 = (bf16[2,40,384]{2,1,0:T(8,128)(2,1)}, bf16[2,40,384]{2,1,0:T(8,128)(2,1)S(1)}, u32[]{:S(2)}, u32[]{:S(2)}) collective-permute-start(bf16[2,40,384]{2,1,0:T(8,128)(2,1)} %bitcast.64), channel_id=1, source_target_pairs={{2,0},{4,2},{6,4},{8,6},{10,8},{12,10},{14,12},{0,14},{3,1},{5,3},... | collective-permute-start | bytes 184328 | tf_op jit(solution)/shard_map/ppermute | solution.py:576
  52.2 0.9 %slice_bitcast_fusion.2 = (bf16[2,40,384]{2,1,0:T(8,128)(2,1)S(1)}, bf16[2,40,384]{2,1,0:T(8,128)(2,1)S(1)}) fusion(bf16[2,2,40,384]{3,2,1,0:T(8,128)(2,1)} %bitcast.46), kind=kLoop, calls=%fused_computation.6 | loop fusion | bytes 245760 | tf_op jit(solution)/shard_map/squeeze | solution.py:579
  53.1 1.5 %collective-permute-done.4 = bf16[2,40,384]{2,1,0:T(8,128)(2,1)S(1)} collective-permute-done((bf16[2,40,384]{2,1,0:T(8,128)(2,1)}, bf16[2,40,384]{2,1,0:T(8,128)(2,1)S(1)}, u32[]{:S(2)}, u32[]{:S(2)}) %collective-permute-start.4) | collective-permute-done | bytes 61472 | tf_op jit(solution)/shard_map/ppermute | solution.py:575
  54.6 0.0 collective-permute-done.5
  54.7 0.1 collective-permute-start.7
  54.8 0.0 copy-start
  54.8 0.0 copy-start.1
  54.8 0.0 copy-start.2
  54.8 0.0 copy-start.6
  54.8 0.0 copy-start.10
  54.9 0.0 copy-start.16
  54.9 0.0 copy-start.20
  54.9 0.0 copy-start.22
  54.9 2.3 %collective-permute-start.6 = (bf16[4,40,384]{2,1,0:T(8,128)(2,1)S(1)}, bf16[4,40,384]{2,1,0:T(8,128)(2,1)S(1)}, u32[]{:S(2)}, u32[]{:S(2)}) collective-permute-start(bf16[4,40,384]{2,1,0:T(8,128)(2,1)S(1)} %pad_maximum_fusion.2), channel_id=1, source_target_pairs={{0,1},{1,16},{16,17},{17,0},{2,3},{3,18},{18,19},{19,2},{4,5},{5,2... | collective-permute-start | bytes 368648 | tf_op jit(solution)/shard_map/ppermute | solution.py:581
  57.2 5.1 %bias_table.5 = f32[2,2560,128]{2,1,0:T(8,128)S(1)} custom-call(s32[160,160]{1,0:T(8,128)S(1)} %get-tuple-element.18.refs_0_, f32[12,2,3312]{2,1,0:T(2,128)S(1)} %bitcast.55), custom_call_target="tpu_custom_call" | custom-call | flops 16777216000 | bytes 1048576 | tf_op jit(solution)/shard_map/bias_table/pallas_call | solution.py:297
  62.3 0.0 collective-permute-done.7
  62.3 0.0 collective-permute-done.6
  62.5 7.8 %coarse_shifted_expand.1 = bf16[576,192]{1,0:T(8,128)(2,1)} custom-call(bf16[160,384]{1,0:T(8,128)(2,1)S(1)} %copy-done.11, bf16[80,384]{1,0:T(8,128)(2,1)S(1)} %bitcast.48, bf16[80,384]{1,0:T(8,128)(2,1)S(1)} %bitcast.49, bf16[160,384]{1,0:T(8,128)(2,1)S(1)} %bitcast.51, bf16[160,384]{1,0:T(8,128)(2,1)S(1)} %bitcast.50, f32[2,2,384]{2,1,0:T(2,128)S(1)} %copy-done.16, ...), custom_call_target="tpu_custom_call" | custom-call | tf_op jit(solution)/shard_map/coarse_shifted_expand/pallas_call | solution.py:664
  (32 shorter events, 0.2 us)
Async XLA Ops:
  0.0 0.9 %copy-start.24 = (f32[2,6,3312]{2,0,1:T(2,128)S(1)}, f32[2,6,3312]{2,0,1:T(2,128)}, u32[]{:S(2)}) copy-start(f32[2,6,3312]{2,0,1:T(2,128)} %param.30) | copy-start | bytes 476932
  0.9 0.9 %copy-start.26 = (s32[144,144]{1,0:T(8,128)S(1)}, s32[144,144]{1,0:T(8,128)}, u32[]{:S(2)}) copy-start(s32[144,144]{1,0:T(8,128)} %refs_0_.1) | copy-start | bytes 248836
  1.8 0.9 %copy-start.27 = (bf16[160,144]{1,0:T(8,128)(2,1)S(1)}, bf16[160,144]{1,0:T(8,128)(2,1)}, u32[]{:S(2)}) copy-start(bf16[160,144]{1,0:T(8,128)(2,1)} %constant.12.clone.refs_1_) | copy-start | bytes 138244
  2.7 4.8 %copy-start.4 = (bf16[2,192,768]{2,1,0:T(8,128)(2,1)S(1)}, bf16[2,192,768]{2,1,0:T(8,128)(2,1)}, u32[]{:S(2)}) copy-start(bf16[2,192,768]{2,1,0:T(8,128)(2,1)} %widen_hbm.4) | copy-start | bytes 1769476
  2.7 4.8 %copy-start.5 = (bf16[2,768,192]{1,2,0:T(8,128)(2,1)S(1)}, bf16[2,768,192]{1,2,0:T(8,128)(2,1)}, u32[]{:S(2)}) copy-start(bf16[2,768,192]{1,2,0:T(8,128)(2,1)} %param.35) | copy-start | bytes 1769476
  2.7 4.8 %copy-start.7 = (bf16[2,192,576]{2,1,0:T(8,128)(2,1)S(1)}, bf16[2,192,576]{2,1,0:T(8,128)(2,1)}, u32[]{:S(2)}) copy-start(bf16[2,192,576]{2,1,0:T(8,128)(2,1)} %triple_hbm.4) | copy-start | bytes 1327108
  2.7 4.8 %copy-start.8 = (bf16[2,192,192]{2,1,0:T(8,128)(2,1)S(1)}, bf16[2,192,192]{2,1,0:T(8,128)(2,1)}, u32[]{:S(2)}) copy-start(bf16[2,192,192]{2,1,0:T(8,128)(2,1)} %project_hbm.4) | copy-start | bytes 442372
  2.7 4.8 %copy-start.13 = (bf16[2,12,24,192]{3,2,1,0:T(8,128)(2,1)S(1)}, bf16[2,12,24,192]{3,2,1,0:T(8,128)(2,1)}, u32[]{:S(2)}) copy-start(bf16[2,12,24,192]{3,2,1,0:T(8,128)(2,1)} %param.26) | copy-start | bytes 663556
  2.7 4.8 %copy-start.14 = (bf16[640,12]{1,0:T(8,128)(2,1)S(1)}, bf16[640,12]{1,0:T(8,128)(2,1)}, u32[]{:S(2)}) copy-start(bf16[640,12]{1,0:T(8,128)(2,1)} %constant.14.clone.of_row_ref) | copy-start | bytes 46084
  2.7 4.8 %copy-start.15 = (bf16[640,24]{1,0:T(8,128)(2,1)S(1)}, bf16[640,24]{1,0:T(8,128)(2,1)}, u32[]{:S(2)}) copy-start(bf16[640,24]{1,0:T(8,128)(2,1)} %constant.15.clone.of_col_ref) | copy-start | bytes 92164
  2.8 4.8 %copy-start.17 = (f32[2,2,192]{2,1,0:T(2,128)S(1)}, f32[2,2,192]{2,1,0:T(2,128)}, u32[]{:S(2)}) copy-start(f32[2,2,192]{2,1,0:T(2,128)} %gains_ref.4) | copy-start | bytes 9220
  2.8 4.8 %copy-start.18 = (s32[12,24]{1,0:T(8,128)S(1)}, s32[12,24]{1,0:T(8,128)}, u32[]{:S(2)}) copy-start(s32[12,24]{1,0:T(8,128)} %land_ref.1) | copy-start | bytes 3460
  2.8 4.8 %copy-start.19 = (s32[1,576]{1,0:T(1,128)S(1)}, s32[1,576]{1,0:T(1,128)}, u32[]{:S(2)}) copy-start(s32[1,576]{1,0:T(1,128)} %constant.13.clone.order_ref) | copy-start | bytes 6916
  2.8 4.8 %copy-start.21 = (f32[192]{0:T(256)S(1)}, f32[192]{0:T(256)}, u32[]{:S(2)}) copy-start(f32[192]{0:T(256)} %param.28) | copy-start | bytes 2308
  7.6 17.5 %copy-start.23 = (f32[2,12,3312]{2,0,1:T(2,128)S(1)}, f32[2,12,3312]{2,0,1:T(2,128)}, u32[]{:S(2)}) copy-start(f32[2,12,3312]{2,0,1:T(2,128)} %param.38) | copy-start | bytes 953860
  7.6 17.5 %copy-start.25 = (f32[2,6,3312]{2,0,1:T(2,128)S(1)}, f32[2,6,3312]{2,0,1:T(2,128)}, u32[]{:S(2)}) copy-start(f32[2,6,3312]{2,0,1:T(2,128)} %param.30) | copy-start | bytes 476932
  13.4 19.5 %copy-start.9 = (bf16[640,192]{1,0:T(8,128)(2,1)}, bf16[640,192]{1,0:T(8,128)(2,1)S(1)}, u32[]{:S(2)}) copy-start(bf16[640,192]{1,0:T(8,128)(2,1)S(1)} %get-tuple-element.15.own_ref) | copy-start | bytes 737284
  13.4 8.6 %collective-permute-start = (bf16[4,40,192]{2,1,0:T(8,128)(2,1)S(1)}, bf16[4,40,192]{2,1,0:T(8,128)(2,1)S(1)}, u32[]{:S(2)}, u32[]{:S(2)}) collective-permute-start(bf16[4,40,192]{2,1,0:T(8,128)(2,1)S(1)} %bitcast.59), channel_id=1, source_target_pairs={{0,2},{2,4},{4,6},{6,8},{8,10},{10,12},{12,14},{14,0},{1,3},{3,5},... | collective-permute-start | bytes 184328 | tf_op jit(solution)/shard_map/ppermute | solution.py:575
  16.5 6.2 %collective-permute-start.1 = (bf16[4,40,192]{2,1,0:T(8,128)(2,1)S(1)}, bf16[4,40,192]{2,1,0:T(8,128)(2,1)S(1)}, u32[]{:S(2)}, u32[]{:S(2)}) collective-permute-start(bf16[4,40,192]{2,1,0:T(8,128)(2,1)S(1)} %bitcast.58), channel_id=1, source_target_pairs={{2,0},{4,2},{6,4},{8,6},{10,8},{12,10},{14,12},{0,14},{3,1},{5,3},... | collective-permute-start | bytes 184328 | tf_op jit(solution)/shard_map/ppermute | solution.py:576
  22.1 10.9 %copy-start.28 = (bf16[4,40,192]{2,1,0:T(8,128)(2,1)}, bf16[4,40,192]{2,1,0:T(8,128)(2,1)S(1)}, u32[]{:S(2)}) copy-start(bf16[4,40,192]{2,1,0:T(8,128)(2,1)S(1)} %collective-permute-done) | copy-start | bytes 184324
  22.7 10.3 %copy-start.29 = (bf16[4,40,192]{2,1,0:T(8,128)(2,1)}, bf16[4,40,192]{2,1,0:T(8,128)(2,1)S(1)}, u32[]{:S(2)}) copy-start(bf16[4,40,192]{2,1,0:T(8,128)(2,1)S(1)} %collective-permute-done.1) | copy-start | bytes 184324
  22.7 12.2 %collective-permute-start.3 = (bf16[6,40,192]{2,1,0:T(8,128)(2,1)S(1)}, bf16[6,40,192]{2,1,0:T(8,128)(2,1)S(1)}, u32[]{:S(2)}, u32[]{:S(2)}) collective-permute-start(bf16[6,40,192]{2,1,0:T(8,128)(2,1)S(1)} %pad_maximum_fusion.1), channel_id=1, source_target_pairs={{1,0},{16,1},{17,16},{0,17},{3,2},{18,3},{19,18},{2,19},{5,4},{20,... | collective-permute-start | bytes 276488 | tf_op jit(solution)/shard_map/ppermute | solution.py:582
  22.8 12.1 %collective-permute-start.2 = (bf16[6,40,192]{2,1,0:T(8,128)(2,1)S(1)}, bf16[6,40,192]{2,1,0:T(8,128)(2,1)S(1)}, u32[]{:S(2)}, u32[]{:S(2)}) collective-permute-start(bf16[6,40,192]{2,1,0:T(8,128)(2,1)S(1)} %pad_maximum_fusion), channel_id=1, source_target_pairs={{0,1},{1,16},{16,17},{17,0},{2,3},{3,18},{18,19},{19,2},{4,5},{5,2... | collective-permute-start | bytes 276488 | tf_op jit(solution)/shard_map/ppermute | solution.py:581
  33.0 1.9 %copy-start.3 = (f32[2,3840,128]{2,1,0:T(8,128)}, f32[2,3840,128]{2,1,0:T(8,128)S(1)}, u32[]{:S(2)}) copy-start(f32[2,3840,128]{2,1,0:T(8,128)S(1)} %bias_table.4) | copy-start | bytes 11796484
  34.9 0.7 copy-start.30
  34.9 0.7 copy-start.31
  47.5 7.2 %collective-permute-start.4 = (bf16[2,40,384]{2,1,0:T(8,128)(2,1)}, bf16[2,40,384]{2,1,0:T(8,128)(2,1)S(1)}, u32[]{:S(2)}, u32[]{:S(2)}) collective-permute-start(bf16[2,40,384]{2,1,0:T(8,128)(2,1)} %bitcast.65), channel_id=1, source_target_pairs={{0,2},{2,4},{4,6},{6,8},{8,10},{10,12},{12,14},{14,0},{1,3},{3,5},... | collective-permute-start | bytes 184328 | tf_op jit(solution)/shard_map/ppermute | solution.py:575
  48.2 6.5 %collective-permute-start.5 = (bf16[2,40,384]{2,1,0:T(8,128)(2,1)}, bf16[2,40,384]{2,1,0:T(8,128)(2,1)S(1)}, u32[]{:S(2)}, u32[]{:S(2)}) collective-permute-start(bf16[2,40,384]{2,1,0:T(8,128)(2,1)} %bitcast.64), channel_id=1, source_target_pairs={{2,0},{4,2},{6,4},{8,6},{10,8},{12,10},{14,12},{0,14},{3,1},{5,3},... | collective-permute-start | bytes 184328 | tf_op jit(solution)/shard_map/ppermute | solution.py:576
  54.7 7.6 %collective-permute-start.7 = (bf16[4,40,384]{2,1,0:T(8,128)(2,1)S(1)}, bf16[4,40,384]{2,1,0:T(8,128)(2,1)S(1)}, u32[]{:S(2)}, u32[]{:S(2)}) collective-permute-start(bf16[4,40,384]{2,1,0:T(8,128)(2,1)S(1)} %pad_maximum_fusion.3), channel_id=1, source_target_pairs={{1,0},{16,1},{17,16},{0,17},{3,2},{18,3},{19,18},{2,19},{5,4},{20,... | collective-permute-start | bytes 368648 | tf_op jit(solution)/shard_map/ppermute | solution.py:582
  54.8 7.6 %copy-start = (bf16[2,384,1536]{2,1,0:T(8,128)(2,1)S(1)}, bf16[2,384,1536]{2,1,0:T(8,128)(2,1)}, u32[]{:S(2)}) copy-start(bf16[2,384,1536]{2,1,0:T(8,128)(2,1)} %widen_hbm.5) | copy-start | bytes 7077892
  54.8 7.6 %copy-start.1 = (bf16[2,1536,384]{2,1,0:T(8,128)(2,1)S(1)}, bf16[2,1536,384]{2,1,0:T(8,128)(2,1)}, u32[]{:S(2)}) copy-start(bf16[2,1536,384]{2,1,0:T(8,128)(2,1)} %narrow_hbm.1) | copy-start | bytes 7077892
  54.8 7.6 %copy-start.2 = (bf16[2,384,1152]{2,1,0:T(8,128)(2,1)S(1)}, bf16[2,384,1152]{2,1,0:T(8,128)(2,1)}, u32[]{:S(2)}) copy-start(bf16[2,384,1152]{2,1,0:T(8,128)(2,1)} %triple_hbm.5) | copy-start | bytes 5308420
  54.8 7.6 %copy-start.6 = (bf16[2,384,384]{2,1,0:T(8,128)(2,1)S(1)}, bf16[2,384,384]{2,1,0:T(8,128)(2,1)}, u32[]{:S(2)}) copy-start(bf16[2,384,384]{2,1,0:T(8,128)(2,1)} %project_hbm.5) | copy-start | bytes 1769476
  54.8 7.6 %copy-start.10 = (bf16[384,768]{1,0:T(8,128)(2,1)S(1)}, bf16[384,768]{1,0:T(8,128)(2,1)}, u32[]{:S(2)}) copy-start(bf16[384,768]{1,0:T(8,128)(2,1)} %expand_weight_hbm.1) | copy-start | bytes 1769476
  54.8 7.6 %copy-start.11 = (bf16[160,384]{1,0:T(8,128)(2,1)S(1)}, bf16[160,384]{1,0:T(8,128)(2,1)}, u32[]{:S(2)}) copy-start(bf16[160,384]{1,0:T(8,128)(2,1)} %get-tuple-element.19.own_ref) | copy-start | bytes 368644
  54.9 7.6 %copy-start.12 = (bf16[640,192]{1,0:T(8,128)(2,1)S(1)}, bf16[640,192]{1,0:T(8,128)(2,1)}, u32[]{:S(2)}) copy-start(bf16[640,192]{1,0:T(8,128)(2,1)} %get-tuple-element.22.parts_ref) | copy-start | bytes 737284
  54.9 7.6 %copy-start.16 = (f32[2,2,384]{2,1,0:T(2,128)S(1)}, f32[2,2,384]{2,1,0:T(2,128)}, u32[]{:S(2)}) copy-start(f32[2,2,384]{2,1,0:T(2,128)} %gains_ref.5) | copy-start | bytes 18436
  54.9 7.6 %copy-start.20 = (s32[1,640]{1,0:T(1,128)S(1)}, s32[1,640]{1,0:T(1,128)}, u32[]{:S(2)}) copy-start(s32[1,640]{1,0:T(1,128)} %constant.17.clone.expand_order_ref) | copy-start | bytes 7684
  54.9 7.6 %copy-start.22 = (f32[192]{0:T(256)S(1)}, f32[192]{0:T(256)}, u32[]{:S(2)}) copy-start(f32[192]{0:T(256)} %param.45) | copy-start | bytes 2308
  54.9 7.4 %collective-permute-start.6 = (bf16[4,40,384]{2,1,0:T(8,128)(2,1)S(1)}, bf16[4,40,384]{2,1,0:T(8,128)(2,1)S(1)}, u32[]{:S(2)}, u32[]{:S(2)}) collective-permute-start(bf16[4,40,384]{2,1,0:T(8,128)(2,1)S(1)} %pad_maximum_fusion.2), channel_id=1, source_target_pairs={{0,1},{1,16},{16,17},{17,0},{2,3},{3,18},{18,19},{19,2},{4,5},{5,2... | collective-permute-start | bytes 368648 | tf_op jit(solution)/shard_map/ppermute | solution.py:581

commit v6 on v5

--- a/solution.py
+++ b/solution.py
@@ -171,6 +171,24 @@
     return -(-heads // 8) * 8
 
 
+def window_order():
+    token = lax.broadcasted_iota(jnp.int32, (WP, WIN_TOK), 1)
+    level = jnp.where(token >= WIN_LAT * WIN_LON, 1, 0)
+    token = token - level * (WIN_LAT * WIN_LON)
+    row = sum(jnp.where(token >= WIN_LON * r, 1, 0) for r in range(1, WIN_LAT))
+    col = token - row * WIN_LON
+    down = jnp.where(row >= HALF_LAT, 1, 0)
+    across = jnp.where(col >= HALF_LON, 1, 0)
+    slot = (
+        (2 * down + across) * QP
+        + level * (HALF_LAT * HALF_LON)
+        + (row - down * HALF_LAT) * HALF_LON
+        + (col - across * HALF_LON)
+    )
+    place = lax.broadcasted_iota(jnp.int32, (WP, WIN_TOK), 0)
+    return jnp.where(slot == place, 1.0, 0.0).astype(BF16)
+
+
 def halved(heads):
     return heads % 8 == 4
 
@@ -188,7 +206,7 @@
 
 def bias_kernel(*refs, picks, fresh):
     if fresh:
-        index_ref, spread_ref, *table_refs, out_ref, index, table, left = refs
+        index_ref, *table_refs, out_ref, index, table, left = refs
     else:
         index, *table_refs, out_ref, table, left = refs
     rows = table.shape[0]
@@ -198,7 +216,7 @@
     @pl.when(pl.program_id(0) == 0)
     def _():
         if fresh:
-            spread = spread_ref[...]
+            spread = window_order()
             plain = index_ref[...]
             high = (plain >> 4).astype(F32).astype(BF16)
             low = (plain & 15).astype(F32).astype(BF16)
@@ -282,13 +300,14 @@
                     )
 
 
-def bias_of(picks, order, vmem, span=QP):
+def bias_of(picks, order, vmem, fresh=False, span=QP):
     tables = [t.transpose(1, 0, 2) for t, _ in picks]
+    if fresh:
+        order, tables = in_hbm(order), [in_hbm(t) for t in tables]
     rows = sum(padded(t.shape[0]) for t in tables)
     units = sum(-(-LO_COUNT // stride) for _, stride in row_groups([t.shape[0] for t in tables]))
     flops = 2 * WP * 256 * WP * units * 8 * 4
     steps = WP // span
-    fresh = len(order) == 2
     out_shape = [jax.ShapeDtypeStruct((2, steps * rows * span, 128), F32)]
     out_specs = [pl.BlockSpec((2, rows * span, 128), lambda i: (0, i, 0))]
     if fresh:
@@ -298,7 +317,7 @@
         functools.partial(bias_kernel, picks=tuple(b for _, b in picks), fresh=fresh),
         out_shape=out_shape,
         grid=(steps,),
-        in_specs=[pl.BlockSpec(memory_space=pltpu.VMEM)] * (len(order) + len(tables)),
+        in_specs=[pl.BlockSpec(memory_space=pltpu.VMEM)] * (1 + len(tables)),
         out_specs=out_specs,
         scratch_shapes=[
             pltpu.VMEM((rows, LO_COUNT * 256), F32),
@@ -307,7 +326,7 @@
         compiler_params=pltpu.CompilerParams(vmem_limit_bytes=vmem << 20),
         cost_estimate=pl.CostEstimate(flops=2 * flops, bytes_accessed=1 << 20, transcendentals=0),
         name="bias_table",
-    )(*order, *tables)
+    )(order, *tables)
     return [out[0].reshape(2, steps, rows, span, 128)] + list(out[1:])
 
 
@@ -462,14 +481,13 @@
 
 def middle_kernel(
     own_ref, north_ref, south_ref, west_ref, east_ref, gains_ref, merge_gain_ref,
-    coarse_gains_ref, merge_order_ref, bias_hbm, triple_hbm, project_hbm, widen_hbm, narrow_hbm,
+    coarse_gains_ref, merge_order_ref, bias_hbm, c_bias_hbm, triple_hbm, project_hbm, widen_hbm, narrow_hbm,
     merge_weight_hbm, c_triple_hbm, c_project_hbm, c_widen_hbm, c_narrow_hbm,
     parts_ref, coarse_ref, top_ref, bottom_ref,
     query, key, value, context, bias, c_bias, w_triple, w_project, w_widen, w_narrow,
     merge_weight, c_triple, c_project, c_widen, c_narrow, sems, bias_sems,
 ):
     steps = bias_hbm.shape[1]
-    heads = bias.shape[1]
     fetched = Fetched(
         [bias_copies(bias_hbm, bias, 0, bias_sems, 0)]
         + block_copies(
@@ -478,7 +496,7 @@
         )
         + [
             [pltpu.make_async_copy(merge_weight_hbm, merge_weight, sems.at[4])],
-            bias_copies(bias_hbm, c_bias, padded(heads), bias_sems, 2 * steps),
+            bias_copies(c_bias_hbm, c_bias, 0, bias_sems, 2 * steps),
         ]
         + block_copies(
             [(c_triple_hbm, c_triple), (c_project_hbm, c_project),
@@ -558,11 +576,15 @@
 APART = pl.BlockSpec(memory_space=pltpu.HBM)
 
 
+def in_hbm(array):
+    return pltpu.with_memory_space_constraint(array, pltpu.HBM)
+
+
 def weight_scratch(weights):
     return [pltpu.VMEM(w.shape[1:], BF16) for w in weights]
 
 
-def halo(own, top, bottom):
+def halo(own, top, bottom, beside=None):
     rows, cols, _, channels = own.shape
     top = top.reshape(own.shape[1:])
     bottom = bottom.reshape(own.shape[1:])
@@ -574,13 +596,16 @@
     west = [((i + 1) % lon, i) for i in range(lon)]
     north = lax.ppermute(bottom, "lat", down)
     south = lax.ppermute(top, "lat", up)
+    if beside is not None:
+        north, south, beside = lax.optimization_barrier((north, south, beside))
 
     def side(c):
         return jnp.concatenate([north[c : c + 1], own[:, c], south[c : c + 1]], axis=0)
 
     from_west = lax.ppermute(side(cols - 1), LON, east)
     from_east = lax.ppermute(side(0), LON, west)
-    return [v.reshape(-1, channels) for v in (own, north, south, from_west, from_east)]
+    halos = [v.reshape(-1, channels) for v in (own, north, south, from_west, from_east)]
+    return halos if beside is None else (halos, beside)
 
 
 def shifted_scratch(rows, cols, channels):
@@ -602,15 +627,11 @@
     quad_rows, quad_cols = rows // HALF_LAT, cols // HALF_LON
     tokens = quad_rows * quad_cols * QP
     wide = merge_weight.shape[1]
-    spread = one_hot(
-        [None if s is None else (s[0] * WIN_LAT + s[1]) * WIN_LON + s[2]
-         for s in quad_sources(WIN_LAT, WIN_LON)],
-        WIN_TOK,
-    )
     order, of_row, of_col = fine_tables(rows, cols)
-    bias_first, ordered = bias_of([(fine_bias, 0)], (bias_index, spread), 16)
-    (bias_middle,) = bias_of([(fine_bias, 1), (coarse_bias, 0)], (ordered,), 16)
-    (bias_last,) = bias_of([(coarse_bias, 1)], (ordered,), 16)
+    bias_first, ordered = bias_of([(fine_bias, 0)], bias_index, 16, fresh=True)
+    (bias_second,) = bias_of([(fine_bias, 1)], ordered, 16)
+    (bias_third,) = bias_of([(coarse_bias, 0)], ordered, 16)
+    (bias_last,) = bias_of([(coarse_bias, 1)], ordered, 16)
     fine_weights = (
         fine_query_key_value, fine_project, fine_widen, fine_narrow.transpose(0, 2, 1)
     )
@@ -639,6 +660,9 @@
         fine_gains, bias_first, *fine_weights,
     )
 
+    halos, bias_second = halo(
+        first.reshape(quad_rows, quad_cols, QP, channels), top, bottom, bias_second
+    )
     parts, coarse, top, bottom = pl.pallas_call(
         middle_kernel,
         out_shape=[
@@ -647,18 +671,19 @@
             jax.ShapeDtypeStruct((line // 2, wide), BF16),
             jax.ShapeDtypeStruct((line // 2, wide), BF16),
         ],
-        in_specs=[WHOLE] * 9 + [APART] * 10,
+        in_specs=[WHOLE] * 9 + [APART] * 11,
         out_specs=[WHOLE] * 4,
         scratch_shapes=shifted_scratch(quad_rows, quad_cols, channels)
         + [fine_scratch, coarse_scratch] + weight_scratch(fine_weights)
         + [pltpu.VMEM(merge_weight.shape, BF16)]
         + weight_scratch(coarse_weights) + [dma((9,)), dma((4 * steps,))],
-        compiler_params=pltpu.CompilerParams(vmem_limit_bytes=60 << 20),
+        compiler_params=pltpu.CompilerParams(vmem_limit_bytes=36 << 20),
         name="fine_shifted_coarse_plain",
     )(
-        *halo(first.reshape(quad_rows, quad_cols, QP, channels), top, bottom),
-        fine_gains, merge_gain, coarse_gains,
-        merge_table(rows, cols), bias_middle, *fine_weights, merge_weight, *coarse_weights,
+        *halos, fine_gains, merge_gain, coarse_gains,
+        merge_table(rows, cols), bias_second, bias_third,
+        *[in_hbm(w) for w in fine_weights], in_hbm(merge_weight),
+        *[in_hbm(w) for w in coarse_weights],
     )
 
     out = pl.pallas_call(

time: 70.7 us -> 62.5 us (0.88)
  local copies, waits for them, and re-layouts: 6.3 us -> 0.16 us
  waiting for transfers between devices: 4.61 us -> 2.2 us
    unnamed x64 -> x46, local copies, waits for them, and re-layouts: 5.39 us -> 0.11 us
    pallas_call x3 -> x4, Pallas kernels: 17.7 us -> 20.5 us  [bias_of(): pl.pallas_call(functools.partial(bias_kernel, picks=tuple((b for _, b in...]
    pallas_call x1, Pallas kernels: 11.9 us -> 9.61 us  [on_device(): pl.pallas_call(middle_kernel, out_shape=[jax.ShapeDtypeStruct((tokens, ch...]
    ppermute x2, waiting for transfers between devices: 4 us -> 2.18 us  [halo(): north = lax.ppermute(bottom, 'lat', down)]
    ppermute x2, starting transfers between devices: 0.12 us -> 1.06 us  [halo(): from_east = lax.ppermute(side(0), LON, west)]
    ppermute x2, starting transfers between devices: 4.52 us -> 3.6 us  [halo(): from_west = lax.ppermute(side(cols - 1), LON, east)]
    squeeze x2, local copies, waits for them, and re-layouts: 0.88 us -> 0.02 us  [side(): return jnp.concatenate([north[c:c + 1], own[:, c], south[c:c + 1]], axis=0)]
  transfers between devices with their start and end apart: 8 -> 8, of which waited for: 3 -> 1; matrix products, arithmetic and copies ran while one was open for 1% -> 0% of each run, Pallas kernels for 19% -> 23%
where the time goes in v6:
time: 62.5 us; the launch traced here: 62.4 us
  Pallas kernels  43.8 us (70%)
  starting transfers between devices  15.6 us (25%)
  waiting for transfers between devices  2.2 us (4%)
    pallas_call x4, Pallas kernels, bias_of(): pl.pallas_call(functools.partial(bias_kernel, picks=tuple((b for _, b in...  20.5 us
    pallas_call x1, Pallas kernels, on_device(): pl.pallas_call(middle_kernel, out_shape=[jax.ShapeDtypeStruct((tokens, ch...  9.61 us
    ppermute x2, starting transfers between devices, halo(): south = lax.ppermute(top, 'lat', up)  7.82 us
    pallas_call x1, Pallas kernels, on_device(): pl.pallas_call(last_kernel, out_shape=jax.ShapeDtypeStruct((LEVELS * rows...  7.8 us
    pallas_call x1, Pallas kernels, on_device(): pl.pallas_call(first_kernel, out_shape=[jax.ShapeDtypeStruct((tokens, cha...  5.83 us
    ppermute x2, starting transfers between devices, halo(): from_west = lax.ppermute(side(cols - 1), LON, east)  3.6 us
    ppermute x2, starting transfers between devices, halo(): north = lax.ppermute(bottom, 'lat', down)  3.09 us
    ppermute x2, waiting for transfers between devices, halo(): north = lax.ppermute(bottom, 'lat', down)  2.18 us
  transfers between devices with their start and end apart: 8, of which 1 were waited for; matrix products, arithmetic and copies ran while one was open for 0% of the time, Pallas kernels for 23%

profile of v6, /device:TPU:0, one launch (start us, length us, event | category | flops | bytes accessed | tf_op | source)
XLA Modules:
  0.0 62.4 jit_solution(14258368794832566843)
XLA Ops:
  0.0 0.0 copy-start.3
  0.0 0.0 copy-start.4
  0.0 0.0 copy-start.6
  0.0 0.0 copy-start.7
  0.0 0.0 copy-start.9
  0.0 0.0 copy-start.10
  0.0 0.0 copy-start.11
  0.0 0.0 copy-start.13
  0.0 0.0 copy-start.14
  0.1 0.0 copy-start.17
  0.1 0.0 copy-start.19
  0.1 5.9 %bias_table.4 = (f32[2,1280,128]{2,1,0:T(8,128)S(1)}, s32[160,160]{1,0:T(8,128)S(1)}) custom-call(s32[144,144]{1,0:T(8,128)} %refs_0_.1, f32[6,2,3312]{2,1,0:T(2,128)} %bitcast.62), custom_call_target="tpu_custom_call" | custom-call | flops 10905190400 | bytes 1048576 | tf_op jit(solution)/shard_map/bias_table/pallas_call | solution.py:316
  6.0 0.0 copy-done.3
  6.0 0.0 copy-done.4
  6.0 0.0 copy-done.6
  6.0 0.0 copy-done.7
  6.0 0.0 copy-done.9
  6.0 0.0 copy-done.10
  6.0 0.0 copy-done.11
  6.0 0.0 copy-done.13
  6.0 0.0 copy-done.14
  6.1 0.0 copy-done.17
  6.1 0.0 copy-done.19
  6.1 5.8 %fine_plain.1 = (bf16[640,192]{1,0:T(8,128)(2,1)S(1)}, bf16[160,192]{1,0:T(8,128)(2,1)S(1)}, bf16[160,192]{1,0:T(8,128)(2,1)S(1)}) custom-call(bf16[576,192]{1,0:T(8,128)(2,1)S(1)} %bitcast.49, s32[12,24]{1,0:T(8,128)S(1)} %copy-done.14, f32[1,192]{1,0:T(1,128)S(1)} %bitcast.58, s32[1,576]{1,0:T(1,128)S(1)} %copy-done.17, bf16[640,12]{1,0:T(8,128)(2,1)S(1)} %copy-done.10, ...), custom_call_target="tpu_custom_call" | custom-call | tf_op jit(solution)/shard_map/fine_plain/pallas_call | solution.py:645
  11.9 3.0 %collective-permute-start = (bf16[4,40,192]{2,1,0:T(8,128)(2,1)S(1)}, bf16[4,40,192]{2,1,0:T(8,128)(2,1)S(1)}, u32[]{:S(2)}, u32[]{:S(2)}) collective-permute-start(bf16[4,40,192]{2,1,0:T(8,128)(2,1)S(1)} %bitcast.65), channel_id=1, source_target_pairs={{0,2},{2,4},{4,6},{6,8},{8,10},{10,12},{12,14},{14,0},{1,3},{3,5},... | collective-permute-start | bytes 184328 | tf_op jit(solution)/shard_map/ppermute | solution.py:597
  14.9 3.1 %collective-permute-start.1 = (bf16[4,40,192]{2,1,0:T(8,128)(2,1)S(1)}, bf16[4,40,192]{2,1,0:T(8,128)(2,1)S(1)}, u32[]{:S(2)}, u32[]{:S(2)}) collective-permute-start(bf16[4,40,192]{2,1,0:T(8,128)(2,1)S(1)} %bitcast.64), channel_id=1, source_target_pairs={{2,0},{4,2},{6,4},{8,6},{10,8},{12,10},{14,12},{0,14},{3,1},{5,3},... | collective-permute-start | bytes 184328 | tf_op jit(solution)/shard_map/ppermute | solution.py:598
  18.1 0.0 copy-done.22
  18.1 4.3 %bias_table.5 = f32[2,1280,128]{2,1,0:T(8,128)S(1)} custom-call(s32[160,160]{1,0:T(8,128)S(1)} %get-tuple-element.21.refs_0_, f32[6,2,3312]{2,1,0:T(2,128)S(1)} %bitcast.63), custom_call_target="tpu_custom_call" | custom-call | flops 10905190400 | bytes 1048576 | tf_op jit(solution)/shard_map/bias_table/pallas_call | solution.py:316
  22.4 0.0 collective-permute-done
  22.4 0.0 collective-permute-done.1
  22.5 0.7 %collective-permute-start.3 = (bf16[6,40,192]{2,1,0:T(8,128)(2,1)S(1)}, bf16[6,40,192]{2,1,0:T(8,128)(2,1)S(1)}, u32[]{:S(2)}, u32[]{:S(2)}) collective-permute-start(bf16[6,40,192]{2,1,0:T(8,128)(2,1)S(1)} %pad_maximum_fusion.1), channel_id=1, source_target_pairs={{1,0},{16,1},{17,16},{0,17},{3,2},{18,3},{19,18},{2,19},{5,4},{20,... | collective-permute-start | bytes 276488 | tf_op jit(solution)/shard_map/ppermute | solution.py:606
  23.2 1.6 %collective-permute-start.2 = (bf16[6,40,192]{2,1,0:T(8,128)(2,1)S(1)}, bf16[6,40,192]{2,1,0:T(8,128)(2,1)S(1)}, u32[]{:S(2)}, u32[]{:S(2)}) collective-permute-start(bf16[6,40,192]{2,1,0:T(8,128)(2,1)S(1)} %pad_maximum_fusion), channel_id=1, source_target_pairs={{0,1},{1,16},{16,17},{17,0},{2,3},{3,18},{18,19},{19,2},{4,5},{5,2... | collective-permute-start | bytes 276488 | tf_op jit(solution)/shard_map/ppermute | solution.py:605
  24.8 0.0 copy-done.21
  24.9 5.2 %bias_table.6 = f32[2,2560,128]{2,1,0:T(8,128)S(1)} custom-call(s32[160,160]{1,0:T(8,128)S(1)} %get-tuple-element.21.refs_0_, f32[12,2,3312]{2,1,0:T(2,128)S(1)} %bitcast.60), custom_call_target="tpu_custom_call" | custom-call | flops 16777216000 | bytes 1048576 | tf_op jit(solution)/shard_map/bias_table/pallas_call | solution.py:316
  30.0 0.0 collective-permute-done.3
  30.0 0.0 collective-permute-done.2
  30.0 0.0 copy-done.12
  30.1 0.0 copy-done.15
  30.1 0.0 copy-done.16
  30.1 9.6 %fine_shifted_coarse_plain.1 = (bf16[640,192]{1,0:T(8,128)(2,1)S(1)}, bf16[160,384]{1,0:T(8,128)(2,1)S(1)}, bf16[80,384]{1,0:T(8,128)(2,1)S(1)}, bf16[80,384]{1,0:T(8,128)(2,1)S(1)}) custom-call(bf16[640,192]{1,0:T(8,128)(2,1)S(1)} %get-tuple-element.18.own_ref, bf16[160,192]{1,0:T(8,128)(2,1)S(1)} %bitcast.52, bf16[160,192]{1,0:T(8,128)(2,1)S(1)} %bitcast.53, ...), custom_call_target="tpu_custom_call" | custom-call | tf_op jit(solution)/shard_map/fine_shifted_coarse_plain/pallas_call | solution.py:666
  39.7 0.1 collective-permute-start.4
  39.8 4.7 %collective-permute-start.5 = (bf16[2,40,384]{2,1,0:T(8,128)(2,1)S(1)}, bf16[2,40,384]{2,1,0:T(8,128)(2,1)S(1)}, u32[]{:S(2)}, u32[]{:S(2)}) collective-permute-start(bf16[2,40,384]{2,1,0:T(8,128)(2,1)S(1)} %bitcast.66), channel_id=1, source_target_pairs={{2,0},{4,2},{6,4},{8,6},{10,8},{12,10},{14,12},{0,14},{3,1},{5,3},... | collective-permute-start | bytes 184328 | tf_op jit(solution)/shard_map/ppermute | solution.py:598
  44.5 2.2 %collective-permute-done.4 = bf16[2,40,384]{2,1,0:T(8,128)(2,1)S(1)} collective-permute-done((bf16[2,40,384]{2,1,0:T(8,128)(2,1)S(1)}, bf16[2,40,384]{2,1,0:T(8,128)(2,1)S(1)}, u32[]{:S(2)}, u32[]{:S(2)}) %collective-permute-start.4) | collective-permute-done | bytes 61472 | tf_op jit(solution)/shard_map/ppermute | solution.py:597
  46.7 0.0 collective-permute-done.5
  46.7 0.3 collective-permute-start.7
  47.1 0.0 copy-start
  47.1 0.0 copy-start.1
  47.1 0.0 copy-start.2
  47.1 0.0 copy-start.5
  47.1 0.0 copy-start.8
  47.1 0.0 copy-start.18
  47.2 0.0 copy-start.20
  47.2 2.0 %collective-permute-start.6 = (bf16[4,40,384]{2,1,0:T(8,128)(2,1)S(1)}, bf16[4,40,384]{2,1,0:T(8,128)(2,1)S(1)}, u32[]{:S(2)}, u32[]{:S(2)}) collective-permute-start(bf16[4,40,384]{2,1,0:T(8,128)(2,1)S(1)} %pad_maximum_fusion.2), channel_id=1, source_target_pairs={{0,1},{1,16},{16,17},{17,0},{2,3},{3,18},{18,19},{19,2},{4,5},{5,2... | collective-permute-start | bytes 368648 | tf_op jit(solution)/shard_map/ppermute | solution.py:605
  49.2 5.1 %bias_table.7 = f32[2,2560,128]{2,1,0:T(8,128)S(1)} custom-call(s32[160,160]{1,0:T(8,128)S(1)} %get-tuple-element.21.refs_0_, f32[12,2,3312]{2,1,0:T(2,128)S(1)} %bitcast.61), custom_call_target="tpu_custom_call" | custom-call | flops 16777216000 | bytes 1048576 | tf_op jit(solution)/shard_map/bias_table/pallas_call | solution.py:316
  54.3 0.0 collective-permute-done.7
  54.3 0.0 collective-permute-done.6
  54.3 0.0 copy-done
  54.3 0.0 copy-done.1
  54.4 0.0 copy-done.2
  54.4 0.0 copy-done.5
  54.4 0.0 copy-done.8
  54.4 0.0 copy-done.18
  54.4 0.0 copy-done.20
  54.4 7.8 %coarse_shifted_expand.1 = bf16[576,192]{1,0:T(8,128)(2,1)} custom-call(bf16[160,384]{1,0:T(8,128)(2,1)S(1)} %get-tuple-element.25.own_ref, bf16[80,384]{1,0:T(8,128)(2,1)S(1)} %bitcast.50, bf16[80,384]{1,0:T(8,128)(2,1)S(1)} %bitcast.51, bf16[160,384]{1,0:T(8,128)(2,1)S(1)} %bitcast.57, bf16[160,384]{1,0:T(8,128)(2,1)S(1)} %bitcast.56, ...), custom_call_target="tpu_custom_call" | custom-call | tf_op jit(solution)/shard_map/coarse_shifted_expand/pallas_call | solution.py:689
  (14 shorter events, 0.2 us)
Async XLA Ops:
  0.0 6.0 %copy-start.3 = (bf16[2,192,768]{2,1,0:T(8,128)(2,1)S(1)}, bf16[2,192,768]{2,1,0:T(8,128)(2,1)}, u32[]{:S(2)}) copy-start(bf16[2,192,768]{2,1,0:T(8,128)(2,1)} %widen_hbm.4) | copy-start | bytes 1769476
  0.0 6.0 %copy-start.4 = (bf16[2,768,192]{1,2,0:T(8,128)(2,1)S(1)}, bf16[2,768,192]{1,2,0:T(8,128)(2,1)}, u32[]{:S(2)}) copy-start(bf16[2,768,192]{1,2,0:T(8,128)(2,1)} %param.34) | copy-start | bytes 1769476
  0.0 6.0 %copy-start.6 = (bf16[2,192,576]{2,1,0:T(8,128)(2,1)S(1)}, bf16[2,192,576]{2,1,0:T(8,128)(2,1)}, u32[]{:S(2)}) copy-start(bf16[2,192,576]{2,1,0:T(8,128)(2,1)} %triple_hbm.4) | copy-start | bytes 1327108
  0.0 6.0 %copy-start.7 = (bf16[2,192,192]{2,1,0:T(8,128)(2,1)S(1)}, bf16[2,192,192]{2,1,0:T(8,128)(2,1)}, u32[]{:S(2)}) copy-start(bf16[2,192,192]{2,1,0:T(8,128)(2,1)} %project_hbm.4) | copy-start | bytes 442372
  0.0 6.0 %copy-start.9 = (bf16[2,12,24,192]{3,2,1,0:T(8,128)(2,1)S(1)}, bf16[2,12,24,192]{3,2,1,0:T(8,128)(2,1)}, u32[]{:S(2)}) copy-start(bf16[2,12,24,192]{3,2,1,0:T(8,128)(2,1)} %param.25) | copy-start | bytes 663556
  0.0 6.0 %copy-start.10 = (bf16[640,12]{1,0:T(8,128)(2,1)S(1)}, bf16[640,12]{1,0:T(8,128)(2,1)}, u32[]{:S(2)}) copy-start(bf16[640,12]{1,0:T(8,128)(2,1)} %constant.11.clone.of_row_ref) | copy-start | bytes 46084
  0.0 6.0 %copy-start.11 = (bf16[640,24]{1,0:T(8,128)(2,1)S(1)}, bf16[640,24]{1,0:T(8,128)(2,1)}, u32[]{:S(2)}) copy-start(bf16[640,24]{1,0:T(8,128)(2,1)} %constant.12.clone.of_col_ref) | copy-start | bytes 92164
  0.0 6.0 %copy-start.13 = (f32[2,2,192]{2,1,0:T(2,128)S(1)}, f32[2,2,192]{2,1,0:T(2,128)}, u32[]{:S(2)}) copy-start(f32[2,2,192]{2,1,0:T(2,128)} %gains_ref.4) | copy-start | bytes 9220
  0.0 6.0 %copy-start.14 = (s32[12,24]{1,0:T(8,128)S(1)}, s32[12,24]{1,0:T(8,128)}, u32[]{:S(2)}) copy-start(s32[12,24]{1,0:T(8,128)} %land_ref.1) | copy-start | bytes 3460
  0.1 6.0 %copy-start.17 = (s32[1,576]{1,0:T(1,128)S(1)}, s32[1,576]{1,0:T(1,128)}, u32[]{:S(2)}) copy-start(s32[1,576]{1,0:T(1,128)} %constant.10.clone.order_ref) | copy-start | bytes 6916
  0.1 6.0 %copy-start.19 = (f32[192]{0:T(256)S(1)}, f32[192]{0:T(256)}, u32[]{:S(2)}) copy-start(f32[192]{0:T(256)} %param.27) | copy-start | bytes 2308
  6.0 12.1 %copy-start.22 = (f32[2,6,3312]{2,0,1:T(2,128)S(1)}, f32[2,6,3312]{2,0,1:T(2,128)}, u32[]{:S(2)}) copy-start(f32[2,6,3312]{2,0,1:T(2,128)} %param.29) | copy-start | bytes 476932
  11.9 10.5 %collective-permute-start = (bf16[4,40,192]{2,1,0:T(8,128)(2,1)S(1)}, bf16[4,40,192]{2,1,0:T(8,128)(2,1)S(1)}, u32[]{:S(2)}, u32[]{:S(2)}) collective-permute-start(bf16[4,40,192]{2,1,0:T(8,128)(2,1)S(1)} %bitcast.65), channel_id=1, source_target_pairs={{0,2},{2,4},{4,6},{6,8},{8,10},{10,12},{12,14},{14,0},{1,3},{3,5},... | collective-permute-start | bytes 184328 | tf_op jit(solution)/shard_map/ppermute | solution.py:597
  14.9 7.5 %collective-permute-start.1 = (bf16[4,40,192]{2,1,0:T(8,128)(2,1)S(1)}, bf16[4,40,192]{2,1,0:T(8,128)(2,1)S(1)}, u32[]{:S(2)}, u32[]{:S(2)}) collective-permute-start(bf16[4,40,192]{2,1,0:T(8,128)(2,1)S(1)} %bitcast.64), channel_id=1, source_target_pairs={{2,0},{4,2},{6,4},{8,6},{10,8},{12,10},{14,12},{0,14},{3,1},{5,3},... | collective-permute-start | bytes 184328 | tf_op jit(solution)/shard_map/ppermute | solution.py:598
  18.1 6.8 %copy-start.21 = (f32[2,12,3312]{2,0,1:T(2,128)S(1)}, f32[2,12,3312]{2,0,1:T(2,128)}, u32[]{:S(2)}) copy-start(f32[2,12,3312]{2,0,1:T(2,128)} %param.37) | copy-start | bytes 953860
  22.5 7.5 %collective-permute-start.3 = (bf16[6,40,192]{2,1,0:T(8,128)(2,1)S(1)}, bf16[6,40,192]{2,1,0:T(8,128)(2,1)S(1)}, u32[]{:S(2)}, u32[]{:S(2)}) collective-permute-start(bf16[6,40,192]{2,1,0:T(8,128)(2,1)S(1)} %pad_maximum_fusion.1), channel_id=1, source_target_pairs={{1,0},{16,1},{17,16},{0,17},{3,2},{18,3},{19,18},{2,19},{5,4},{20,... | collective-permute-start | bytes 276488 | tf_op jit(solution)/shard_map/ppermute | solution.py:606
  23.2 6.8 %collective-permute-start.2 = (bf16[6,40,192]{2,1,0:T(8,128)(2,1)S(1)}, bf16[6,40,192]{2,1,0:T(8,128)(2,1)S(1)}, u32[]{:S(2)}, u32[]{:S(2)}) collective-permute-start(bf16[6,40,192]{2,1,0:T(8,128)(2,1)S(1)} %pad_maximum_fusion), channel_id=1, source_target_pairs={{0,1},{1,16},{16,17},{17,0},{2,3},{3,18},{18,19},{19,2},{4,5},{5,2... | collective-permute-start | bytes 276488 | tf_op jit(solution)/shard_map/ppermute | solution.py:605
  24.8 5.2 %copy-start.12 = (f32[2,2,384]{2,1,0:T(2,128)S(1)}, f32[2,2,384]{2,1,0:T(2,128)}, u32[]{:S(2)}) copy-start(f32[2,2,384]{2,1,0:T(2,128)} %gains_ref.5) | copy-start | bytes 18436
  24.8 5.2 %copy-start.15 = (f32[768]{0:T(1024)S(1)}, f32[768]{0:T(1024)}, u32[]{:S(2)}) copy-start(f32[768]{0:T(1024)} %merge_gain_ref.1) | copy-start | bytes 9220
  24.8 5.2 %copy-start.16 = (s32[1,640]{1,0:T(1,128)S(1)}, s32[1,640]{1,0:T(1,128)}, u32[]{:S(2)}) copy-start(s32[1,640]{1,0:T(1,128)} %constant.13.clone.merge_order_ref) | copy-start | bytes 7684
  39.7 7.0 %collective-permute-start.4 = (bf16[2,40,384]{2,1,0:T(8,128)(2,1)S(1)}, bf16[2,40,384]{2,1,0:T(8,128)(2,1)S(1)}, u32[]{:S(2)}, u32[]{:S(2)}) collective-permute-start(bf16[2,40,384]{2,1,0:T(8,128)(2,1)S(1)} %bitcast.67), channel_id=1, source_target_pairs={{0,2},{2,4},{4,6},{6,8},{8,10},{10,12},{12,14},{14,0},{1,3},{3,5},... | collective-permute-start | bytes 184328 | tf_op jit(solution)/shard_map/ppermute | solution.py:597
  39.8 6.9 %collective-permute-start.5 = (bf16[2,40,384]{2,1,0:T(8,128)(2,1)S(1)}, bf16[2,40,384]{2,1,0:T(8,128)(2,1)S(1)}, u32[]{:S(2)}, u32[]{:S(2)}) collective-permute-start(bf16[2,40,384]{2,1,0:T(8,128)(2,1)S(1)} %bitcast.66), channel_id=1, source_target_pairs={{2,0},{4,2},{6,4},{8,6},{10,8},{12,10},{14,12},{0,14},{3,1},{5,3},... | collective-permute-start | bytes 184328 | tf_op jit(solution)/shard_map/ppermute | solution.py:598
  46.7 7.6 %collective-permute-start.7 = (bf16[4,40,384]{2,1,0:T(8,128)(2,1)S(1)}, bf16[4,40,384]{2,1,0:T(8,128)(2,1)S(1)}, u32[]{:S(2)}, u32[]{:S(2)}) collective-permute-start(bf16[4,40,384]{2,1,0:T(8,128)(2,1)S(1)} %pad_maximum_fusion.3), channel_id=1, source_target_pairs={{1,0},{16,1},{17,16},{0,17},{3,2},{18,3},{19,18},{2,19},{5,4},{20,... | collective-permute-start | bytes 368648 | tf_op jit(solution)/shard_map/ppermute | solution.py:606
  47.1 7.3 %copy-start = (bf16[2,384,1536]{2,1,0:T(8,128)(2,1)S(1)}, bf16[2,384,1536]{2,1,0:T(8,128)(2,1)}, u32[]{:S(2)}) copy-start(bf16[2,384,1536]{2,1,0:T(8,128)(2,1)} %widen_hbm.5) | copy-start | bytes 7077892
  47.1 7.3 %copy-start.1 = (bf16[2,1536,384]{2,1,0:T(8,128)(2,1)S(1)}, bf16[2,1536,384]{2,1,0:T(8,128)(2,1)}, u32[]{:S(2)}) copy-start(bf16[2,1536,384]{2,1,0:T(8,128)(2,1)} %narrow_hbm.1) | copy-start | bytes 7077892
  47.1 7.3 %copy-start.2 = (bf16[2,384,1152]{2,1,0:T(8,128)(2,1)S(1)}, bf16[2,384,1152]{2,1,0:T(8,128)(2,1)}, u32[]{:S(2)}) copy-start(bf16[2,384,1152]{2,1,0:T(8,128)(2,1)} %triple_hbm.5) | copy-start | bytes 5308420
  47.1 7.3 %copy-start.5 = (bf16[2,384,384]{2,1,0:T(8,128)(2,1)S(1)}, bf16[2,384,384]{2,1,0:T(8,128)(2,1)}, u32[]{:S(2)}) copy-start(bf16[2,384,384]{2,1,0:T(8,128)(2,1)} %project_hbm.5) | copy-start | bytes 1769476
  47.1 7.2 %copy-start.8 = (bf16[384,768]{1,0:T(8,128)(2,1)S(1)}, bf16[384,768]{1,0:T(8,128)(2,1)}, u32[]{:S(2)}) copy-start(bf16[384,768]{1,0:T(8,128)(2,1)} %expand_weight_hbm.1) | copy-start | bytes 1769476
  47.1 7.2 %copy-start.18 = (s32[1,640]{1,0:T(1,128)S(1)}, s32[1,640]{1,0:T(1,128)}, u32[]{:S(2)}) copy-start(s32[1,640]{1,0:T(1,128)} %constant.14.clone.expand_order_ref) | copy-start | bytes 7684
  47.2 7.2 %copy-start.20 = (f32[192]{0:T(256)S(1)}, f32[192]{0:T(256)}, u32[]{:S(2)}) copy-start(f32[192]{0:T(256)} %param.44) | copy-start | bytes 2308
  47.2 7.2 %collective-permute-start.6 = (bf16[4,40,384]{2,1,0:T(8,128)(2,1)S(1)}, bf16[4,40,384]{2,1,0:T(8,128)(2,1)S(1)}, u32[]{:S(2)}, u32[]{:S(2)}) collective-permute-start(bf16[4,40,384]{2,1,0:T(8,128)(2,1)S(1)} %pad_maximum_fusion.2), channel_id=1, source_target_pairs={{0,1},{1,16},{16,17},{17,0},{2,3},{3,18},{18,19},{19,2},{4,5},{5,2... | collective-permute-start | bytes 368648 | tf_op jit(solution)/shard_map/ppermute | solution.py:605

commit v7 on v6

--- a/solution.py
+++ b/solution.py
@@ -131,7 +131,11 @@
             bias = jnp.concatenate(
                 [
                     jnp.concatenate(
-                        [bias_ref[half, head, f : f + n // len(firsts), :width] for f in firsts],
+                        [
+                            bias_ref[half, f // QP + i, head, :, :width]
+                            for f in firsts
+                            for i in range(n // len(firsts) // QP)
+                        ],
                         axis=0,
                     )
                     for half, width in ((0, 128), (1, WP - 128))
@@ -330,23 +334,10 @@
     return [out[0].reshape(2, steps, rows, span, 128)] + list(out[1:])
 
 
-def bias_copies(source_ref, bias, first, sems, at):
-    steps, span, heads = source_ref.shape[1], source_ref.shape[3], bias.shape[1]
-    return [
-        pltpu.make_async_copy(
-            source_ref.at[half, step, pl.ds(first, heads)],
-            bias.at[half, :, pl.ds(step * span, span)],
-            sems.at[at + half * steps + step],
-        )
-        for half in range(2)
-        for step in range(steps)
-    ]
-
-
 class Fetched:
     def __init__(self, copies):
         self.copies = copies
-        for group in copies[1:2] + copies[:1] + copies[2:]:
+        for group in copies:
             for copy in group:
                 copy.start()
 
@@ -358,18 +349,9 @@
 
 def first_kernel(
     fields_ref, land_ref, embed_ref, order_ref, of_row_ref, of_col_ref, gains_ref,
-    bias_hbm, triple_hbm, project_hbm, widen_hbm, narrow_hbm,
-    out_ref, top_ref, bottom_ref,
-    context, bias, w_triple, w_project, w_widen, w_narrow, sems, bias_sems,
+    bias, triple_ref, project_ref, widen_ref, narrow_ref, out_ref, top_ref, bottom_ref, context,
 ):
     channels = fields_ref.shape[1]
-    fetched = Fetched(
-        [bias_copies(bias_hbm, bias, 0, bias_sems, 0)]
-        + block_copies(
-            [(triple_hbm, w_triple), (project_hbm, w_project),
-             (widen_hbm, w_widen), (narrow_hbm, w_narrow)], 0, sems, 0,
-        )
-    )
     land = land_ref[...].astype(F32).astype(BF16)
     on_row = dot(of_row_ref[...], land)
     on_land = jnp.sum(on_row * of_col_ref[...].astype(F32), axis=-1, keepdims=True)
@@ -377,9 +359,7 @@
     start = dot(sent_to(order_ref, rows), fields_ref[...]) + on_land * embed_ref[...]
     x = start.astype(BF16).astype(F32)
     normed = norm(x, gains_ref[0, 0:1]).astype(BF16)
-    fetched.wait(1)
-    triple = dot(normed, w_triple[...]).astype(BF16)
-    fetched.wait(0)
+    triple = dot(normed, triple_ref[0]).astype(BF16)
     inner = top_ref.shape[0]
     for a in range(rows // inner // 2):
         for b in range(inner // QP // 2):
@@ -396,9 +376,8 @@
             ).astype(BF16)
             context[top : top + 2 * QP] = mixed[: 2 * QP]
             context[below : below + 2 * QP] = mixed[2 * QP :]
-    fetched.wait(2, 3, 4)
     done = finish(
-        x, context[...], gains_ref[0, 1:2], w_project[...], w_widen[...], w_narrow[...]
+        x, context[...], gains_ref[0, 1:2], project_ref[0], widen_ref[0], narrow_ref[0]
     )
     out_ref[...] = done
     top_ref[...] = done[:inner]
@@ -428,7 +407,7 @@
             east_ref[i * QP : (i + 1) * QP].astype(F32),
         ]
     normed = norm(jnp.concatenate(pieces, axis=0), gains_ref[1, 0:1]).astype(BF16)
-    fetched.wait(1)
+    fetched.wait(0)
     query[...] = dot(normed[line : (down + 1) * line], w_triple[:, :channels])
     both = dot(normed, w_triple[:, channels:]).astype(BF16)
     key[...] = both[:, :channels]
@@ -437,7 +416,6 @@
     place = lax.axis_index("lat")
     on_top = jnp.where(place == 0, MASKED, 0.0).astype(F32)
     on_bottom = jnp.where(place == lax.axis_size("lat") - 1, MASKED, 0.0).astype(F32)
-    fetched.wait(0)
     for wa in range(down // 2 + 1):
         mask = None
         if wa == 0:
@@ -465,7 +443,7 @@
             for n, r in enumerate(rows):
                 to = ((2 * wa + r - 1) * across + 2 * wb + cols[0] - 1) * QP
                 context[to : to + size] = out[n * size : (n + 1) * size]
-    fetched.wait(2, 3, 4)
+    fetched.wait(1, 2, 3)
     return finish(
         own_ref[...].astype(F32), context[...].astype(BF16), gains_ref[1, 1:2],
         w_project[...], w_widen[...], w_narrow[...],
@@ -481,23 +459,18 @@
 
 def middle_kernel(
     own_ref, north_ref, south_ref, west_ref, east_ref, gains_ref, merge_gain_ref,
-    coarse_gains_ref, merge_order_ref, bias_hbm, c_bias_hbm, triple_hbm, project_hbm, widen_hbm, narrow_hbm,
+    coarse_gains_ref, merge_order_ref, bias, c_bias, triple_hbm, project_hbm, widen_hbm, narrow_hbm,
     merge_weight_hbm, c_triple_hbm, c_project_hbm, c_widen_hbm, c_narrow_hbm,
     parts_ref, coarse_ref, top_ref, bottom_ref,
-    query, key, value, context, bias, c_bias, w_triple, w_project, w_widen, w_narrow,
-    merge_weight, c_triple, c_project, c_widen, c_narrow, sems, bias_sems,
+    query, key, value, context, w_triple, w_project, w_widen, w_narrow,
+    merge_weight, c_triple, c_project, c_widen, c_narrow, sems,
 ):
-    steps = bias_hbm.shape[1]
     fetched = Fetched(
-        [bias_copies(bias_hbm, bias, 0, bias_sems, 0)]
-        + block_copies(
+        block_copies(
             [(triple_hbm, w_triple), (project_hbm, w_project),
              (widen_hbm, w_widen), (narrow_hbm, w_narrow)], 1, sems, 0,
         )
-        + [
-            [pltpu.make_async_copy(merge_weight_hbm, merge_weight, sems.at[4])],
-            bias_copies(c_bias_hbm, c_bias, 0, bias_sems, 2 * steps),
-        ]
+        + [[pltpu.make_async_copy(merge_weight_hbm, merge_weight, sems.at[4])]]
         + block_copies(
             [(c_triple_hbm, c_triple), (c_project_hbm, c_project),
              (c_widen_hbm, c_widen), (c_narrow_hbm, c_narrow)], 0, sems, 5,
@@ -517,7 +490,7 @@
     variance = sum(jnp.sum(p * p, axis=-1, keepdims=True) for p in parts) / width
     factor = lax.rsqrt(variance + 1e-05)
     merge_gain = merge_gain_ref[...].reshape(1, width)
-    fetched.wait(5)
+    fetched.wait(4)
     coarse = jnp.zeros((WP, merge_weight.shape[1]), F32)
     for i, p in enumerate(parts):
         gain = merge_gain[:, i * channels : (i + 1) * channels]
@@ -526,12 +499,12 @@
     x = coarse.astype(BF16).astype(F32)
     wide = x.shape[1]
     normed = norm(x, coarse_gains_ref[0, 0:1]).astype(BF16)
-    fetched.wait(6, 7)
+    fetched.wait(5)
     triple = dot(normed, c_triple[...]).astype(BF16)
     mixed = attend(
         triple[:, :wide], triple[:, wide : 2 * wide], triple[:, 2 * wide :], c_bias, [0], None
     ).astype(BF16)
-    fetched.wait(8, 9, 10)
+    fetched.wait(6, 7, 8)
     done = finish(
         x, mixed, coarse_gains_ref[0, 1:2], c_project[...], c_widen[...], c_narrow[...]
     )
@@ -543,26 +516,20 @@
 
 def last_kernel(
     own_ref, north_ref, south_ref, west_ref, east_ref, gains_ref, parts_ref, expand_gain_ref,
-    expand_order_ref, bias_hbm, triple_hbm, project_hbm, widen_hbm, narrow_hbm, expand_weight_hbm,
+    expand_order_ref, bias, triple_ref, project_ref, widen_ref, narrow_ref, expand_weight_ref,
     out_ref,
-    query, key, value, context, bias, w_triple, w_project, w_widen, w_narrow,
-    expand_weight, sems, bias_sems,
+    query, key, value, context,
 ):
-    fetched = Fetched(
-        [bias_copies(bias_hbm, bias, 0, bias_sems, 0)]
-        + block_copies(
-            [(triple_hbm, w_triple), (project_hbm, w_project),
-             (widen_hbm, w_widen), (narrow_hbm, w_narrow)], 1, sems, 0,
-        )
-        + [[pltpu.make_async_copy(expand_weight_hbm, expand_weight, sems.at[4])]]
+    fetched = Fetched([[]] * 4)
+    w_triple, w_project, w_widen, w_narrow = (
+        ref.at[1] for ref in (triple_ref, project_ref, widen_ref, narrow_ref)
     )
     deep = shifted_block(
         own_ref, north_ref, south_ref, west_ref, east_ref, gains_ref, fetched,
         bias, w_triple, w_project, w_widen, w_narrow, query, key, value, context,
     )
     channels = parts_ref.shape[1]
-    fetched.wait(5)
-    widened = dot(deep, expand_weight[...])
+    widened = dot(deep, expand_weight_ref[...])
     outs = []
     for i in range(4):
         shuffled = widened[:, i * channels : (i + 1) * channels]
@@ -636,10 +603,7 @@
         fine_query_key_value, fine_project, fine_widen, fine_narrow.transpose(0, 2, 1)
     )
     coarse_weights = (coarse_query_key_value, coarse_project, coarse_widen, coarse_narrow)
-    steps = bias_first.shape[1]
     dma = pltpu.SemaphoreType.DMA
-    fine_scratch = pltpu.VMEM((2, HF, WP, 128), F32)
-    coarse_scratch = pltpu.VMEM((2, HC, WP, 128), F32)
     line = quad_cols * QP
 
     first, top, bottom = pl.pallas_call(
@@ -649,10 +613,9 @@
             jax.ShapeDtypeStruct((line, channels), BF16),
             jax.ShapeDtypeStruct((line, channels), BF16),
         ],
-        in_specs=[WHOLE] * 7 + [APART] * 5,
+        in_specs=[WHOLE] * 12,
         out_specs=[WHOLE] * 3,
-        scratch_shapes=[pltpu.VMEM((tokens, channels), BF16), fine_scratch]
-        + weight_scratch(fine_weights) + [dma((4,)), dma((2 * steps,))],
+        scratch_shapes=[pltpu.VMEM((tokens, channels), BF16)],
         compiler_params=pltpu.CompilerParams(vmem_limit_bytes=20 << 20),
         name="fine_plain",
     )(
@@ -671,12 +634,12 @@
             jax.ShapeDtypeStruct((line // 2, wide), BF16),
             jax.ShapeDtypeStruct((line // 2, wide), BF16),
         ],
-        in_specs=[WHOLE] * 9 + [APART] * 11,
+        in_specs=[WHOLE] * 11 + [APART] * 9,
         out_specs=[WHOLE] * 4,
         scratch_shapes=shifted_scratch(quad_rows, quad_cols, channels)
-        + [fine_scratch, coarse_scratch] + weight_scratch(fine_weights)
+        + weight_scratch(fine_weights)
         + [pltpu.VMEM(merge_weight.shape, BF16)]
-        + weight_scratch(coarse_weights) + [dma((9,)), dma((4 * steps,))],
+        + weight_scratch(coarse_weights) + [dma((9,))],
         compiler_params=pltpu.CompilerParams(vmem_limit_bytes=36 << 20),
         name="fine_shifted_coarse_plain",
     )(
@@ -689,12 +652,9 @@
     out = pl.pallas_call(
         last_kernel,
         out_shape=jax.ShapeDtypeStruct((LEVELS * rows * cols, channels), BF16),
-        in_specs=[WHOLE] * 9 + [APART] * 6,
+        in_specs=[WHOLE] * 15,
         out_specs=WHOLE,
-        scratch_shapes=shifted_scratch(quad_rows // 2, quad_cols // 2, wide)
-        + [coarse_scratch] + weight_scratch(coarse_weights)
-        + [pltpu.VMEM(expand_weight.shape, BF16)]
-        + [dma((5,)), dma((2 * steps,))],
+        scratch_shapes=shifted_scratch(quad_rows // 2, quad_cols // 2, wide),
         compiler_params=pltpu.CompilerParams(vmem_limit_bytes=28 << 20),
         name="coarse_shifted_expand",
     )(

time: 62.5 us -> 58.5 us (0.936)
  Pallas kernels: 43.8 us -> 39.9 us
    pallas_call x1, Pallas kernels: 5.83 us -> 3.91 us  [on_device(): pl.pallas_call(first_kernel, out_shape=[jax.ShapeDtypeStruct((tokens, cha...]
    pallas_call x1, Pallas kernels: 7.8 us -> 6.08 us  [on_device(): pl.pallas_call(last_kernel, out_shape=jax.ShapeDtypeStruct((LEVELS * rows...]
  transfers between devices with their start and end apart: 8 -> 8, of which waited for: 1 -> 1; matrix products, arithmetic and copies ran while one was open for 0% -> 0% of each run, Pallas kernels for 23% -> 25%
where the time goes in v7:
time: 58.5 us; the launch traced here: 58.3 us
  Pallas kernels  39.9 us (68%)
  starting transfers between devices  15.6 us (27%)
  waiting for transfers between devices  2.2 us (4%)
    pallas_call x4, Pallas kernels, bias_of(): pl.pallas_call(functools.partial(bias_kernel, picks=tuple((b for _, b in...  20.5 us
    pallas_call x1, Pallas kernels, on_device(): pl.pallas_call(middle_kernel, out_shape=[jax.ShapeDtypeStruct((tokens, ch...  9.37 us
    ppermute x2, starting transfers between devices, halo(): south = lax.ppermute(top, 'lat', up)  7.81 us
    pallas_call x1, Pallas kernels, on_device(): pl.pallas_call(last_kernel, out_shape=jax.ShapeDtypeStruct((LEVELS * rows...  6.08 us
    pallas_call x1, Pallas kernels, on_device(): pl.pallas_call(first_kernel, out_shape=[jax.ShapeDtypeStruct((tokens, cha...  3.91 us
    ppermute x2, starting transfers between devices, halo(): from_west = lax.ppermute(side(cols - 1), LON, east)  3.65 us
    ppermute x2, starting transfers between devices, halo(): north = lax.ppermute(bottom, 'lat', down)  3.1 us
    ppermute x2, waiting for transfers between devices, halo(): north = lax.ppermute(bottom, 'lat', down)  2.18 us
  transfers between devices with their start and end apart: 8, of which 1 were waited for; matrix products, arithmetic and copies ran while one was open for 0% of the time, Pallas kernels for 25%

profile of v7, /device:TPU:0, one launch (start us, length us, event | category | flops | bytes accessed | tf_op | source)
XLA Modules:
  0.0 58.3 jit_solution(5742496215628050642)
XLA Ops:
  0.0 0.0 copy-start.3
  0.0 0.0 copy-start.4
  0.0 0.0 copy-start.6
  0.0 0.0 copy-start.7
  0.0 0.0 copy-start.9
  0.0 0.0 copy-start.10
  0.0 0.0 copy-start.11
  0.0 0.0 copy-start.13
  0.0 0.0 copy-start.14
  0.1 0.0 copy-start.17
  0.1 0.0 copy-start.19
  0.1 5.9 %bias_table.4 = (f32[2,1280,128]{2,1,0:T(8,128)S(1)}, s32[160,160]{1,0:T(8,128)S(1)}) custom-call(s32[144,144]{1,0:T(8,128)} %refs_0_.1, f32[6,2,3312]{2,1,0:T(2,128)} %bitcast.62), custom_call_target="tpu_custom_call" | custom-call | flops 10905190400 | bytes 1048576 | tf_op jit(solution)/shard_map/bias_table/pallas_call | solution.py:320
  6.0 0.0 copy-done.3
  6.0 0.0 copy-done.4
  6.0 0.0 copy-done.6
  6.0 0.0 copy-done.7
  6.0 0.0 copy-done.9
  6.0 0.0 copy-done.10
  6.0 0.0 copy-done.11
  6.0 0.0 copy-done.13
  6.0 0.0 copy-done.14
  6.1 0.0 copy-done.17
  6.1 0.0 copy-done.19
  6.1 3.9 %fine_plain.1 = (bf16[640,192]{1,0:T(8,128)(2,1)S(1)}, bf16[160,192]{1,0:T(8,128)(2,1)S(1)}, bf16[160,192]{1,0:T(8,128)(2,1)S(1)}) custom-call(bf16[576,192]{1,0:T(8,128)(2,1)S(1)} %bitcast.49, s32[12,24]{1,0:T(8,128)S(1)} %copy-done.14, f32[1,192]{1,0:T(1,128)S(1)} %bitcast.58, s32[1,576]{1,0:T(1,128)S(1)} %copy-done.17, bf16[640,12]{1,0:T(8,128)(2,1)S(1)} %copy-done.10, ...), custom_call_target="tpu_custom_call" | custom-call | tf_op jit(solution)/shard_map/fine_plain/pallas_call | solution.py:609
  10.0 3.0 %collective-permute-start = (bf16[4,40,192]{2,1,0:T(8,128)(2,1)S(1)}, bf16[4,40,192]{2,1,0:T(8,128)(2,1)S(1)}, u32[]{:S(2)}, u32[]{:S(2)}) collective-permute-start(bf16[4,40,192]{2,1,0:T(8,128)(2,1)S(1)} %bitcast.65), channel_id=1, source_target_pairs={{0,2},{2,4},{4,6},{6,8},{8,10},{10,12},{12,14},{14,0},{1,3},{3,5},... | collective-permute-start | bytes 184328 | tf_op jit(solution)/shard_map/ppermute | solution.py:564
  13.0 3.1 %collective-permute-start.1 = (bf16[4,40,192]{2,1,0:T(8,128)(2,1)S(1)}, bf16[4,40,192]{2,1,0:T(8,128)(2,1)S(1)}, u32[]{:S(2)}, u32[]{:S(2)}) collective-permute-start(bf16[4,40,192]{2,1,0:T(8,128)(2,1)S(1)} %bitcast.64), channel_id=1, source_target_pairs={{2,0},{4,2},{6,4},{8,6},{10,8},{12,10},{14,12},{0,14},{3,1},{5,3},... | collective-permute-start | bytes 184328 | tf_op jit(solution)/shard_map/ppermute | solution.py:565
  16.1 0.0 copy-done.22
  16.1 4.4 %bias_table.5 = f32[2,1280,128]{2,1,0:T(8,128)S(1)} custom-call(s32[160,160]{1,0:T(8,128)S(1)} %get-tuple-element.21.refs_0_, f32[6,2,3312]{2,1,0:T(2,128)S(1)} %bitcast.63), custom_call_target="tpu_custom_call" | custom-call | flops 10905190400 | bytes 1048576 | tf_op jit(solution)/shard_map/bias_table/pallas_call | solution.py:320
  20.5 0.0 collective-permute-done
  20.5 0.0 collective-permute-done.1
  20.6 0.7 %collective-permute-start.3 = (bf16[6,40,192]{2,1,0:T(8,128)(2,1)S(1)}, bf16[6,40,192]{2,1,0:T(8,128)(2,1)S(1)}, u32[]{:S(2)}, u32[]{:S(2)}) collective-permute-start(bf16[6,40,192]{2,1,0:T(8,128)(2,1)S(1)} %pad_maximum_fusion.1), channel_id=1, source_target_pairs={{1,0},{16,1},{17,16},{0,17},{3,2},{18,3},{19,18},{2,19},{5,4},{20,... | collective-permute-start | bytes 276488 | tf_op jit(solution)/shard_map/ppermute | solution.py:573
  21.3 1.6 %collective-permute-start.2 = (bf16[6,40,192]{2,1,0:T(8,128)(2,1)S(1)}, bf16[6,40,192]{2,1,0:T(8,128)(2,1)S(1)}, u32[]{:S(2)}, u32[]{:S(2)}) collective-permute-start(bf16[6,40,192]{2,1,0:T(8,128)(2,1)S(1)} %pad_maximum_fusion), channel_id=1, source_target_pairs={{0,1},{1,16},{16,17},{17,0},{2,3},{3,18},{18,19},{19,2},{4,5},{5,2... | collective-permute-start | bytes 276488 | tf_op jit(solution)/shard_map/ppermute | solution.py:572
  22.9 0.0 copy-done.21
  22.9 5.2 %bias_table.6 = f32[2,2560,128]{2,1,0:T(8,128)S(1)} custom-call(s32[160,160]{1,0:T(8,128)S(1)} %get-tuple-element.21.refs_0_, f32[12,2,3312]{2,1,0:T(2,128)S(1)} %bitcast.60), custom_call_target="tpu_custom_call" | custom-call | flops 16777216000 | bytes 1048576 | tf_op jit(solution)/shard_map/bias_table/pallas_call | solution.py:320
  28.1 0.0 collective-permute-done.3
  28.1 0.0 collective-permute-done.2
  28.1 0.0 copy-done.12
  28.2 0.0 copy-done.15
  28.2 0.0 copy-done.16
  28.2 9.4 %fine_shifted_coarse_plain.1 = (bf16[640,192]{1,0:T(8,128)(2,1)S(1)}, bf16[160,384]{1,0:T(8,128)(2,1)S(1)}, bf16[80,384]{1,0:T(8,128)(2,1)S(1)}, bf16[80,384]{1,0:T(8,128)(2,1)S(1)}) custom-call(bf16[640,192]{1,0:T(8,128)(2,1)S(1)} %get-tuple-element.18.own_ref, bf16[160,192]{1,0:T(8,128)(2,1)S(1)} %bitcast.52, bf16[160,192]{1,0:T(8,128)(2,1)S(1)} %bitcast.53, ...), custom_call_target="tpu_custom_call" | custom-call | tf_op jit(solution)/shard_map/fine_shifted_coarse_plain/pallas_call | solution.py:629
  37.6 0.1 collective-permute-start.4
  37.6 4.7 %collective-permute-start.5 = (bf16[2,40,384]{2,1,0:T(8,128)(2,1)S(1)}, bf16[2,40,384]{2,1,0:T(8,128)(2,1)S(1)}, u32[]{:S(2)}, u32[]{:S(2)}) collective-permute-start(bf16[2,40,384]{2,1,0:T(8,128)(2,1)S(1)} %bitcast.66), channel_id=1, source_target_pairs={{2,0},{4,2},{6,4},{8,6},{10,8},{12,10},{14,12},{0,14},{3,1},{5,3},... | collective-permute-start | bytes 184328 | tf_op jit(solution)/shard_map/ppermute | solution.py:565
  42.3 2.2 %collective-permute-done.4 = bf16[2,40,384]{2,1,0:T(8,128)(2,1)S(1)} collective-permute-done((bf16[2,40,384]{2,1,0:T(8,128)(2,1)S(1)}, bf16[2,40,384]{2,1,0:T(8,128)(2,1)S(1)}, u32[]{:S(2)}, u32[]{:S(2)}) %collective-permute-start.4) | collective-permute-done | bytes 61472 | tf_op jit(solution)/shard_map/ppermute | solution.py:564
  44.5 0.0 collective-permute-done.5
  44.6 0.3 collective-permute-start.7
  44.9 0.0 copy-start
  44.9 0.0 copy-start.1
  44.9 0.0 copy-start.2
  45.0 0.0 copy-start.5
  45.0 0.0 copy-start.8
  45.0 0.0 copy-start.18
  45.0 0.0 copy-start.20
  45.0 2.0 %collective-permute-start.6 = (bf16[4,40,384]{2,1,0:T(8,128)(2,1)S(1)}, bf16[4,40,384]{2,1,0:T(8,128)(2,1)S(1)}, u32[]{:S(2)}, u32[]{:S(2)}) collective-permute-start(bf16[4,40,384]{2,1,0:T(8,128)(2,1)S(1)} %pad_maximum_fusion.2), channel_id=1, source_target_pairs={{0,1},{1,16},{16,17},{17,0},{2,3},{3,18},{18,19},{19,2},{4,5},{5,2... | collective-permute-start | bytes 368648 | tf_op jit(solution)/shard_map/ppermute | solution.py:572
  47.0 5.1 %bias_table.7 = f32[2,2560,128]{2,1,0:T(8,128)S(1)} custom-call(s32[160,160]{1,0:T(8,128)S(1)} %get-tuple-element.21.refs_0_, f32[12,2,3312]{2,1,0:T(2,128)S(1)} %bitcast.61), custom_call_target="tpu_custom_call" | custom-call | flops 16777216000 | bytes 1048576 | tf_op jit(solution)/shard_map/bias_table/pallas_call | solution.py:320
  52.2 0.0 collective-permute-done.7
  52.2 0.0 collective-permute-done.6
  52.2 0.0 copy-done
  52.2 0.0 copy-done.1
  52.2 0.0 copy-done.2
  52.2 0.0 copy-done.5
  52.2 0.0 copy-done.8
  52.2 0.0 copy-done.18
  52.3 0.0 copy-done.20
  52.3 6.1 %coarse_shifted_expand.1 = bf16[576,192]{1,0:T(8,128)(2,1)} custom-call(bf16[160,384]{1,0:T(8,128)(2,1)S(1)} %get-tuple-element.25.own_ref, bf16[80,384]{1,0:T(8,128)(2,1)S(1)} %bitcast.50, bf16[80,384]{1,0:T(8,128)(2,1)S(1)} %bitcast.51, bf16[160,384]{1,0:T(8,128)(2,1)S(1)} %bitcast.57, bf16[160,384]{1,0:T(8,128)(2,1)S(1)} %bitcast.56, ...), custom_call_target="tpu_custom_call" | custom-call | tf_op jit(solution)/shard_map/coarse_shifted_expand/pallas_call | solution.py:652
  (14 shorter events, 0.2 us)
Async XLA Ops:
  0.0 6.0 %copy-start.3 = (bf16[2,192,768]{2,1,0:T(8,128)(2,1)S(1)}, bf16[2,192,768]{2,1,0:T(8,128)(2,1)}, u32[]{:S(2)}) copy-start(bf16[2,192,768]{2,1,0:T(8,128)(2,1)} %widen_hbm.1) | copy-start | bytes 1769476
  0.0 6.0 %copy-start.4 = (bf16[2,768,192]{1,2,0:T(8,128)(2,1)S(1)}, bf16[2,768,192]{1,2,0:T(8,128)(2,1)}, u32[]{:S(2)}) copy-start(bf16[2,768,192]{1,2,0:T(8,128)(2,1)} %param.34) | copy-start | bytes 1769476
  0.0 6.0 %copy-start.6 = (bf16[2,192,576]{2,1,0:T(8,128)(2,1)S(1)}, bf16[2,192,576]{2,1,0:T(8,128)(2,1)}, u32[]{:S(2)}) copy-start(bf16[2,192,576]{2,1,0:T(8,128)(2,1)} %triple_hbm.1) | copy-start | bytes 1327108
  0.0 6.0 %copy-start.7 = (bf16[2,192,192]{2,1,0:T(8,128)(2,1)S(1)}, bf16[2,192,192]{2,1,0:T(8,128)(2,1)}, u32[]{:S(2)}) copy-start(bf16[2,192,192]{2,1,0:T(8,128)(2,1)} %project_hbm.1) | copy-start | bytes 442372
  0.0 6.0 %copy-start.9 = (bf16[2,12,24,192]{3,2,1,0:T(8,128)(2,1)S(1)}, bf16[2,12,24,192]{3,2,1,0:T(8,128)(2,1)}, u32[]{:S(2)}) copy-start(bf16[2,12,24,192]{3,2,1,0:T(8,128)(2,1)} %param.25) | copy-start | bytes 663556
  0.0 6.0 %copy-start.10 = (bf16[640,12]{1,0:T(8,128)(2,1)S(1)}, bf16[640,12]{1,0:T(8,128)(2,1)}, u32[]{:S(2)}) copy-start(bf16[640,12]{1,0:T(8,128)(2,1)} %constant.11.clone.of_row_ref) | copy-start | bytes 46084
  0.0 6.0 %copy-start.11 = (bf16[640,24]{1,0:T(8,128)(2,1)S(1)}, bf16[640,24]{1,0:T(8,128)(2,1)}, u32[]{:S(2)}) copy-start(bf16[640,24]{1,0:T(8,128)(2,1)} %constant.12.clone.of_col_ref) | copy-start | bytes 92164
  0.0 6.0 %copy-start.13 = (f32[2,2,192]{2,1,0:T(2,128)S(1)}, f32[2,2,192]{2,1,0:T(2,128)}, u32[]{:S(2)}) copy-start(f32[2,2,192]{2,1,0:T(2,128)} %gains_ref.4) | copy-start | bytes 9220
  0.0 6.0 %copy-start.14 = (s32[12,24]{1,0:T(8,128)S(1)}, s32[12,24]{1,0:T(8,128)}, u32[]{:S(2)}) copy-start(s32[12,24]{1,0:T(8,128)} %land_ref.1) | copy-start | bytes 3460
  0.1 6.0 %copy-start.17 = (s32[1,576]{1,0:T(1,128)S(1)}, s32[1,576]{1,0:T(1,128)}, u32[]{:S(2)}) copy-start(s32[1,576]{1,0:T(1,128)} %constant.10.clone.order_ref) | copy-start | bytes 6916
  0.1 6.0 %copy-start.19 = (f32[192]{0:T(256)S(1)}, f32[192]{0:T(256)}, u32[]{:S(2)}) copy-start(f32[192]{0:T(256)} %param.27) | copy-start | bytes 2308
  6.0 10.2 %copy-start.22 = (f32[2,6,3312]{2,0,1:T(2,128)S(1)}, f32[2,6,3312]{2,0,1:T(2,128)}, u32[]{:S(2)}) copy-start(f32[2,6,3312]{2,0,1:T(2,128)} %param.29) | copy-start | bytes 476932
  10.0 10.5 %collective-permute-start = (bf16[4,40,192]{2,1,0:T(8,128)(2,1)S(1)}, bf16[4,40,192]{2,1,0:T(8,128)(2,1)S(1)}, u32[]{:S(2)}, u32[]{:S(2)}) collective-permute-start(bf16[4,40,192]{2,1,0:T(8,128)(2,1)S(1)} %bitcast.65), channel_id=1, source_target_pairs={{0,2},{2,4},{4,6},{6,8},{8,10},{10,12},{12,14},{14,0},{1,3},{3,5},... | collective-permute-start | bytes 184328 | tf_op jit(solution)/shard_map/ppermute | solution.py:564
  13.0 7.5 %collective-permute-start.1 = (bf16[4,40,192]{2,1,0:T(8,128)(2,1)S(1)}, bf16[4,40,192]{2,1,0:T(8,128)(2,1)S(1)}, u32[]{:S(2)}, u32[]{:S(2)}) collective-permute-start(bf16[4,40,192]{2,1,0:T(8,128)(2,1)S(1)} %bitcast.64), channel_id=1, source_target_pairs={{2,0},{4,2},{6,4},{8,6},{10,8},{12,10},{14,12},{0,14},{3,1},{5,3},... | collective-permute-start | bytes 184328 | tf_op jit(solution)/shard_map/ppermute | solution.py:565
  16.1 6.8 %copy-start.21 = (f32[2,12,3312]{2,0,1:T(2,128)S(1)}, f32[2,12,3312]{2,0,1:T(2,128)}, u32[]{:S(2)}) copy-start(f32[2,12,3312]{2,0,1:T(2,128)} %param.37) | copy-start | bytes 953860
  20.6 7.5 %collective-permute-start.3 = (bf16[6,40,192]{2,1,0:T(8,128)(2,1)S(1)}, bf16[6,40,192]{2,1,0:T(8,128)(2,1)S(1)}, u32[]{:S(2)}, u32[]{:S(2)}) collective-permute-start(bf16[6,40,192]{2,1,0:T(8,128)(2,1)S(1)} %pad_maximum_fusion.1), channel_id=1, source_target_pairs={{1,0},{16,1},{17,16},{0,17},{3,2},{18,3},{19,18},{2,19},{5,4},{20,... | collective-permute-start | bytes 276488 | tf_op jit(solution)/shard_map/ppermute | solution.py:573
  21.3 6.8 %collective-permute-start.2 = (bf16[6,40,192]{2,1,0:T(8,128)(2,1)S(1)}, bf16[6,40,192]{2,1,0:T(8,128)(2,1)S(1)}, u32[]{:S(2)}, u32[]{:S(2)}) collective-permute-start(bf16[6,40,192]{2,1,0:T(8,128)(2,1)S(1)} %pad_maximum_fusion), channel_id=1, source_target_pairs={{0,1},{1,16},{16,17},{17,0},{2,3},{3,18},{18,19},{19,2},{4,5},{5,2... | collective-permute-start | bytes 276488 | tf_op jit(solution)/shard_map/ppermute | solution.py:572
  22.9 5.2 %copy-start.12 = (f32[2,2,384]{2,1,0:T(2,128)S(1)}, f32[2,2,384]{2,1,0:T(2,128)}, u32[]{:S(2)}) copy-start(f32[2,2,384]{2,1,0:T(2,128)} %gains_ref.5) | copy-start | bytes 18436
  22.9 5.2 %copy-start.15 = (f32[768]{0:T(1024)S(1)}, f32[768]{0:T(1024)}, u32[]{:S(2)}) copy-start(f32[768]{0:T(1024)} %merge_gain_ref.1) | copy-start | bytes 9220
  22.9 5.2 %copy-start.16 = (s32[1,640]{1,0:T(1,128)S(1)}, s32[1,640]{1,0:T(1,128)}, u32[]{:S(2)}) copy-start(s32[1,640]{1,0:T(1,128)} %constant.13.clone.merge_order_ref) | copy-start | bytes 7684
  37.6 7.0 %collective-permute-start.4 = (bf16[2,40,384]{2,1,0:T(8,128)(2,1)S(1)}, bf16[2,40,384]{2,1,0:T(8,128)(2,1)S(1)}, u32[]{:S(2)}, u32[]{:S(2)}) collective-permute-start(bf16[2,40,384]{2,1,0:T(8,128)(2,1)S(1)} %bitcast.67), channel_id=1, source_target_pairs={{0,2},{2,4},{4,6},{6,8},{8,10},{10,12},{12,14},{14,0},{1,3},{3,5},... | collective-permute-start | bytes 184328 | tf_op jit(solution)/shard_map/ppermute | solution.py:564
  37.6 6.9 %collective-permute-start.5 = (bf16[2,40,384]{2,1,0:T(8,128)(2,1)S(1)}, bf16[2,40,384]{2,1,0:T(8,128)(2,1)S(1)}, u32[]{:S(2)}, u32[]{:S(2)}) collective-permute-start(bf16[2,40,384]{2,1,0:T(8,128)(2,1)S(1)} %bitcast.66), channel_id=1, source_target_pairs={{2,0},{4,2},{6,4},{8,6},{10,8},{12,10},{14,12},{0,14},{3,1},{5,3},... | collective-permute-start | bytes 184328 | tf_op jit(solution)/shard_map/ppermute | solution.py:565
  44.6 7.6 %collective-permute-start.7 = (bf16[4,40,384]{2,1,0:T(8,128)(2,1)S(1)}, bf16[4,40,384]{2,1,0:T(8,128)(2,1)S(1)}, u32[]{:S(2)}, u32[]{:S(2)}) collective-permute-start(bf16[4,40,384]{2,1,0:T(8,128)(2,1)S(1)} %pad_maximum_fusion.3), channel_id=1, source_target_pairs={{1,0},{16,1},{17,16},{0,17},{3,2},{18,3},{19,18},{2,19},{5,4},{20,... | collective-permute-start | bytes 368648 | tf_op jit(solution)/shard_map/ppermute | solution.py:573
  44.9 7.3 %copy-start = (bf16[2,384,1536]{2,1,0:T(8,128)(2,1)S(1)}, bf16[2,384,1536]{2,1,0:T(8,128)(2,1)}, u32[]{:S(2)}) copy-start(bf16[2,384,1536]{2,1,0:T(8,128)(2,1)} %widen_ref.3) | copy-start | bytes 7077892
  44.9 7.3 %copy-start.1 = (bf16[2,1536,384]{2,1,0:T(8,128)(2,1)S(1)}, bf16[2,1536,384]{2,1,0:T(8,128)(2,1)}, u32[]{:S(2)}) copy-start(bf16[2,1536,384]{2,1,0:T(8,128)(2,1)} %narrow_ref.1) | copy-start | bytes 7077892
  44.9 7.3 %copy-start.2 = (bf16[2,384,1152]{2,1,0:T(8,128)(2,1)S(1)}, bf16[2,384,1152]{2,1,0:T(8,128)(2,1)}, u32[]{:S(2)}) copy-start(bf16[2,384,1152]{2,1,0:T(8,128)(2,1)} %triple_ref.3) | copy-start | bytes 5308420
  45.0 7.3 %copy-start.5 = (bf16[2,384,384]{2,1,0:T(8,128)(2,1)S(1)}, bf16[2,384,384]{2,1,0:T(8,128)(2,1)}, u32[]{:S(2)}) copy-start(bf16[2,384,384]{2,1,0:T(8,128)(2,1)} %project_ref.3) | copy-start | bytes 1769476
  45.0 7.3 %copy-start.8 = (bf16[384,768]{1,0:T(8,128)(2,1)S(1)}, bf16[384,768]{1,0:T(8,128)(2,1)}, u32[]{:S(2)}) copy-start(bf16[384,768]{1,0:T(8,128)(2,1)} %expand_weight_ref.1) | copy-start | bytes 1769476
  45.0 7.3 %copy-start.18 = (s32[1,640]{1,0:T(1,128)S(1)}, s32[1,640]{1,0:T(1,128)}, u32[]{:S(2)}) copy-start(s32[1,640]{1,0:T(1,128)} %constant.14.clone.expand_order_ref) | copy-start | bytes 7684
  45.0 7.3 %copy-start.20 = (f32[192]{0:T(256)S(1)}, f32[192]{0:T(256)}, u32[]{:S(2)}) copy-start(f32[192]{0:T(256)} %param.44) | copy-start | bytes 2308
  45.0 7.2 %collective-permute-start.6 = (bf16[4,40,384]{2,1,0:T(8,128)(2,1)S(1)}, bf16[4,40,384]{2,1,0:T(8,128)(2,1)S(1)}, u32[]{:S(2)}, u32[]{:S(2)}) collective-permute-start(bf16[4,40,384]{2,1,0:T(8,128)(2,1)S(1)} %pad_maximum_fusion.2), channel_id=1, source_target_pairs={{0,1},{1,16},{16,17},{17,0},{2,3},{3,18},{18,19},{19,2},{4,5},{5,2... | collective-permute-start | bytes 368648 | tf_op jit(solution)/shard_map/ppermute | solution.py:572

commit v8 on v7

--- a/solution.py
+++ b/solution.py
@@ -459,22 +459,21 @@
 
 def middle_kernel(
     own_ref, north_ref, south_ref, west_ref, east_ref, gains_ref, merge_gain_ref,
-    coarse_gains_ref, merge_order_ref, bias, c_bias, triple_hbm, project_hbm, widen_hbm, narrow_hbm,
+    coarse_gains_ref, merge_order_ref, bias, c_bias, triple_ref, project_ref, widen_ref, narrow_ref,
     merge_weight_hbm, c_triple_hbm, c_project_hbm, c_widen_hbm, c_narrow_hbm,
     parts_ref, coarse_ref, top_ref, bottom_ref,
-    query, key, value, context, w_triple, w_project, w_widen, w_narrow,
-    merge_weight, c_triple, c_project, c_widen, c_narrow, sems,
+    query, key, value, context, merge_weight, c_triple, c_project, c_widen, c_narrow, sems,
 ):
     fetched = Fetched(
-        block_copies(
-            [(triple_hbm, w_triple), (project_hbm, w_project),
-             (widen_hbm, w_widen), (narrow_hbm, w_narrow)], 1, sems, 0,
-        )
+        [[]] * 4
         + [[pltpu.make_async_copy(merge_weight_hbm, merge_weight, sems.at[4])]]
         + block_copies(
             [(c_triple_hbm, c_triple), (c_project_hbm, c_project),
              (c_widen_hbm, c_widen), (c_narrow_hbm, c_narrow)], 0, sems, 5,
         )
+    )
+    w_triple, w_project, w_widen, w_narrow = (
+        ref.at[1] for ref in (triple_ref, project_ref, widen_ref, narrow_ref)
     )
     skip = shifted_block(
         own_ref, north_ref, south_ref, west_ref, east_ref, gains_ref, fetched,
@@ -634,10 +633,9 @@
             jax.ShapeDtypeStruct((line // 2, wide), BF16),
             jax.ShapeDtypeStruct((line // 2, wide), BF16),
         ],
-        in_specs=[WHOLE] * 11 + [APART] * 9,
+        in_specs=[WHOLE] * 15 + [APART] * 5,
         out_specs=[WHOLE] * 4,
         scratch_shapes=shifted_scratch(quad_rows, quad_cols, channels)
-        + weight_scratch(fine_weights)
         + [pltpu.VMEM(merge_weight.shape, BF16)]
         + weight_scratch(coarse_weights) + [dma((9,))],
         compiler_params=pltpu.CompilerParams(vmem_limit_bytes=36 << 20),
@@ -645,7 +643,7 @@
     )(
         *halos, fine_gains, merge_gain, coarse_gains,
         merge_table(rows, cols), bias_second, bias_third,
-        *[in_hbm(w) for w in fine_weights], in_hbm(merge_weight),
+        *fine_weights, in_hbm(merge_weight),
         *[in_hbm(w) for w in coarse_weights],
     )
 

time: 58.5 us -> 58.8 us (level)
  no operation moved by 1% of the time
where the time goes in v8:
time: 58.8 us; the launch traced here: 58.6 us
  Pallas kernels  40.2 us (68%)
  starting transfers between devices  15.6 us (27%)
  waiting for transfers between devices  2.2 us (4%)
    pallas_call x4, Pallas kernels, bias_of(): pl.pallas_call(functools.partial(bias_kernel, picks=tuple((b for _, b in...  20.5 us
    pallas_call x1, Pallas kernels, on_device(): pl.pallas_call(middle_kernel, out_shape=[jax.ShapeDtypeStruct((tokens, ch...  9.68 us
    ppermute x2, starting transfers between devices, halo(): south = lax.ppermute(top, 'lat', up)  7.82 us
    pallas_call x1, Pallas kernels, on_device(): pl.pallas_call(last_kernel, out_shape=jax.ShapeDtypeStruct((LEVELS * rows...  6.08 us
    pallas_call x1, Pallas kernels, on_device(): pl.pallas_call(first_kernel, out_shape=[jax.ShapeDtypeStruct((tokens, cha...  3.92 us
    ppermute x2, starting transfers between devices, halo(): from_west = lax.ppermute(side(cols - 1), LON, east)  3.6 us
    ppermute x2, starting transfers between devices, halo(): north = lax.ppermute(bottom, 'lat', down)  3.08 us
    ppermute x2, waiting for transfers between devices, halo(): north = lax.ppermute(bottom, 'lat', down)  2.18 us
  transfers between devices with their start and end apart: 8, of which 1 were waited for; matrix products, arithmetic and copies ran while one was open for 0% of the time, Pallas kernels for 25%

profile of v8, /device:TPU:0, one launch (start us, length us, event | category | flops | bytes accessed | tf_op | source)
XLA Modules:
  0.0 58.6 jit_solution(2991029107788092919)
XLA Ops:
  0.0 0.0 copy-start.3
  0.0 0.0 copy-start.4
  0.0 0.0 copy-start.6
  0.0 0.0 copy-start.7
  0.0 0.0 copy-start.9
  0.0 0.0 copy-start.10
  0.0 0.0 copy-start.11
  0.0 0.0 copy-start.13
  0.0 0.0 copy-start.14
  0.1 0.0 copy-start.17
  0.1 0.0 copy-start.19
  0.1 5.9 %bias_table.4 = (f32[2,1280,128]{2,1,0:T(8,128)S(1)}, s32[160,160]{1,0:T(8,128)S(1)}) custom-call(s32[144,144]{1,0:T(8,128)} %refs_0_.1, f32[6,2,3312]{2,1,0:T(2,128)} %bitcast.62), custom_call_target="tpu_custom_call" | custom-call | flops 10905190400 | bytes 1048576 | tf_op jit(solution)/shard_map/bias_table/pallas_call | solution.py:320
  6.0 0.0 copy-done.3
  6.0 0.0 copy-done.4
  6.0 0.0 copy-done.6
  6.0 0.0 copy-done.7
  6.0 0.0 copy-done.9
  6.0 0.0 copy-done.10
  6.0 0.0 copy-done.11
  6.0 0.0 copy-done.13
  6.0 0.0 copy-done.14
  6.1 0.0 copy-done.17
  6.1 0.0 copy-done.19
  6.1 3.9 %fine_plain.1 = (bf16[640,192]{1,0:T(8,128)(2,1)S(1)}, bf16[160,192]{1,0:T(8,128)(2,1)S(1)}, bf16[160,192]{1,0:T(8,128)(2,1)S(1)}) custom-call(bf16[576,192]{1,0:T(8,128)(2,1)S(1)} %bitcast.49, s32[12,24]{1,0:T(8,128)S(1)} %copy-done.14, f32[1,192]{1,0:T(1,128)S(1)} %bitcast.58, s32[1,576]{1,0:T(1,128)S(1)} %copy-done.17, bf16[640,12]{1,0:T(8,128)(2,1)S(1)} %copy-done.10, ...), custom_call_target="tpu_custom_call" | custom-call | tf_op jit(solution)/shard_map/fine_plain/pallas_call | solution.py:608
  10.0 3.0 %collective-permute-start = (bf16[4,40,192]{2,1,0:T(8,128)(2,1)S(1)}, bf16[4,40,192]{2,1,0:T(8,128)(2,1)S(1)}, u32[]{:S(2)}, u32[]{:S(2)}) collective-permute-start(bf16[4,40,192]{2,1,0:T(8,128)(2,1)S(1)} %bitcast.65), channel_id=1, source_target_pairs={{0,2},{2,4},{4,6},{6,8},{8,10},{10,12},{12,14},{14,0},{1,3},{3,5},... | collective-permute-start | bytes 184328 | tf_op jit(solution)/shard_map/ppermute | solution.py:563
  13.0 3.1 %collective-permute-start.1 = (bf16[4,40,192]{2,1,0:T(8,128)(2,1)S(1)}, bf16[4,40,192]{2,1,0:T(8,128)(2,1)S(1)}, u32[]{:S(2)}, u32[]{:S(2)}) collective-permute-start(bf16[4,40,192]{2,1,0:T(8,128)(2,1)S(1)} %bitcast.64), channel_id=1, source_target_pairs={{2,0},{4,2},{6,4},{8,6},{10,8},{12,10},{14,12},{0,14},{3,1},{5,3},... | collective-permute-start | bytes 184328 | tf_op jit(solution)/shard_map/ppermute | solution.py:564
  16.1 0.0 copy-done.22
  16.1 4.3 %bias_table.5 = f32[2,1280,128]{2,1,0:T(8,128)S(1)} custom-call(s32[160,160]{1,0:T(8,128)S(1)} %get-tuple-element.21.refs_0_, f32[6,2,3312]{2,1,0:T(2,128)S(1)} %bitcast.63), custom_call_target="tpu_custom_call" | custom-call | flops 10905190400 | bytes 1048576 | tf_op jit(solution)/shard_map/bias_table/pallas_call | solution.py:320
  20.5 0.0 collective-permute-done
  20.5 0.0 collective-permute-done.1
  20.6 0.7 %collective-permute-start.3 = (bf16[6,40,192]{2,1,0:T(8,128)(2,1)S(1)}, bf16[6,40,192]{2,1,0:T(8,128)(2,1)S(1)}, u32[]{:S(2)}, u32[]{:S(2)}) collective-permute-start(bf16[6,40,192]{2,1,0:T(8,128)(2,1)S(1)} %pad_maximum_fusion.1), channel_id=1, source_target_pairs={{1,0},{16,1},{17,16},{0,17},{3,2},{18,3},{19,18},{2,19},{5,4},{20,... | collective-permute-start | bytes 276488 | tf_op jit(solution)/shard_map/ppermute | solution.py:572
  21.3 1.6 %collective-permute-start.2 = (bf16[6,40,192]{2,1,0:T(8,128)(2,1)S(1)}, bf16[6,40,192]{2,1,0:T(8,128)(2,1)S(1)}, u32[]{:S(2)}, u32[]{:S(2)}) collective-permute-start(bf16[6,40,192]{2,1,0:T(8,128)(2,1)S(1)} %pad_maximum_fusion), channel_id=1, source_target_pairs={{0,1},{1,16},{16,17},{17,0},{2,3},{3,18},{18,19},{19,2},{4,5},{5,2... | collective-permute-start | bytes 276488 | tf_op jit(solution)/shard_map/ppermute | solution.py:571
  22.9 0.0 copy-done.21
  22.9 5.2 %bias_table.6 = f32[2,2560,128]{2,1,0:T(8,128)S(1)} custom-call(s32[160,160]{1,0:T(8,128)S(1)} %get-tuple-element.21.refs_0_, f32[12,2,3312]{2,1,0:T(2,128)S(1)} %bitcast.60), custom_call_target="tpu_custom_call" | custom-call | flops 16777216000 | bytes 1048576 | tf_op jit(solution)/shard_map/bias_table/pallas_call | solution.py:320
  28.1 0.0 collective-permute-done.3
  28.1 0.0 collective-permute-done.2
  28.1 0.0 copy-done.12
  28.1 0.0 copy-done.15
  28.1 0.0 copy-done.16
  28.1 9.7 %fine_shifted_coarse_plain.1 = (bf16[640,192]{1,0:T(8,128)(2,1)S(1)}, bf16[160,384]{1,0:T(8,128)(2,1)S(1)}, bf16[80,384]{1,0:T(8,128)(2,1)S(1)}, bf16[80,384]{1,0:T(8,128)(2,1)S(1)}) custom-call(bf16[640,192]{1,0:T(8,128)(2,1)S(1)} %get-tuple-element.18.own_ref, bf16[160,192]{1,0:T(8,128)(2,1)S(1)} %bitcast.52, bf16[160,192]{1,0:T(8,128)(2,1)S(1)} %bitcast.53, ...), custom_call_target="tpu_custom_call" | custom-call | tf_op jit(solution)/shard_map/fine_shifted_coarse_plain/pallas_call | solution.py:628
  37.8 0.1 collective-permute-start.4
  37.9 4.7 %collective-permute-start.5 = (bf16[2,40,384]{2,1,0:T(8,128)(2,1)S(1)}, bf16[2,40,384]{2,1,0:T(8,128)(2,1)S(1)}, u32[]{:S(2)}, u32[]{:S(2)}) collective-permute-start(bf16[2,40,384]{2,1,0:T(8,128)(2,1)S(1)} %bitcast.66), channel_id=1, source_target_pairs={{2,0},{4,2},{6,4},{8,6},{10,8},{12,10},{14,12},{0,14},{3,1},{5,3},... | collective-permute-start | bytes 184328 | tf_op jit(solution)/shard_map/ppermute | solution.py:564
  42.6 2.2 %collective-permute-done.4 = bf16[2,40,384]{2,1,0:T(8,128)(2,1)S(1)} collective-permute-done((bf16[2,40,384]{2,1,0:T(8,128)(2,1)S(1)}, bf16[2,40,384]{2,1,0:T(8,128)(2,1)S(1)}, u32[]{:S(2)}, u32[]{:S(2)}) %collective-permute-start.4) | collective-permute-done | bytes 61472 | tf_op jit(solution)/shard_map/ppermute | solution.py:563
  44.8 0.0 collective-permute-done.5
  44.9 0.3 collective-permute-start.7
  45.2 0.0 copy-start
  45.3 0.0 copy-start.1
  45.3 0.0 copy-start.2
  45.3 0.0 copy-start.5
  45.3 0.0 copy-start.8
  45.3 0.0 copy-start.18
  45.3 0.0 copy-start.20
  45.3 2.0 %collective-permute-start.6 = (bf16[4,40,384]{2,1,0:T(8,128)(2,1)S(1)}, bf16[4,40,384]{2,1,0:T(8,128)(2,1)S(1)}, u32[]{:S(2)}, u32[]{:S(2)}) collective-permute-start(bf16[4,40,384]{2,1,0:T(8,128)(2,1)S(1)} %pad_maximum_fusion.2), channel_id=1, source_target_pairs={{0,1},{1,16},{16,17},{17,0},{2,3},{3,18},{18,19},{19,2},{4,5},{5,2... | collective-permute-start | bytes 368648 | tf_op jit(solution)/shard_map/ppermute | solution.py:571
  47.3 5.1 %bias_table.7 = f32[2,2560,128]{2,1,0:T(8,128)S(1)} custom-call(s32[160,160]{1,0:T(8,128)S(1)} %get-tuple-element.21.refs_0_, f32[12,2,3312]{2,1,0:T(2,128)S(1)} %bitcast.61), custom_call_target="tpu_custom_call" | custom-call | flops 16777216000 | bytes 1048576 | tf_op jit(solution)/shard_map/bias_table/pallas_call | solution.py:320
  52.5 0.0 collective-permute-done.7
  52.5 0.0 collective-permute-done.6
  52.5 0.0 copy-done
  52.5 0.0 copy-done.1
  52.5 0.0 copy-done.2
  52.5 0.0 copy-done.5
  52.5 0.0 copy-done.8
  52.5 0.0 copy-done.18
  52.6 0.0 copy-done.20
  52.6 6.1 %coarse_shifted_expand.1 = bf16[576,192]{1,0:T(8,128)(2,1)} custom-call(bf16[160,384]{1,0:T(8,128)(2,1)S(1)} %get-tuple-element.25.own_ref, bf16[80,384]{1,0:T(8,128)(2,1)S(1)} %bitcast.50, bf16[80,384]{1,0:T(8,128)(2,1)S(1)} %bitcast.51, bf16[160,384]{1,0:T(8,128)(2,1)S(1)} %bitcast.57, bf16[160,384]{1,0:T(8,128)(2,1)S(1)} %bitcast.56, ...), custom_call_target="tpu_custom_call" | custom-call | tf_op jit(solution)/shard_map/coarse_shifted_expand/pallas_call | solution.py:650
  (14 shorter events, 0.2 us)
Async XLA Ops:
  0.0 6.0 %copy-start.3 = (bf16[2,192,768]{2,1,0:T(8,128)(2,1)S(1)}, bf16[2,192,768]{2,1,0:T(8,128)(2,1)}, u32[]{:S(2)}) copy-start(bf16[2,192,768]{2,1,0:T(8,128)(2,1)} %widen_ref.4) | copy-start | bytes 1769476
  0.0 6.0 %copy-start.4 = (bf16[2,768,192]{1,2,0:T(8,128)(2,1)S(1)}, bf16[2,768,192]{1,2,0:T(8,128)(2,1)}, u32[]{:S(2)}) copy-start(bf16[2,768,192]{1,2,0:T(8,128)(2,1)} %param.34) | copy-start | bytes 1769476
  0.0 6.0 %copy-start.6 = (bf16[2,192,576]{2,1,0:T(8,128)(2,1)S(1)}, bf16[2,192,576]{2,1,0:T(8,128)(2,1)}, u32[]{:S(2)}) copy-start(bf16[2,192,576]{2,1,0:T(8,128)(2,1)} %triple_ref.4) | copy-start | bytes 1327108
  0.0 6.0 %copy-start.7 = (bf16[2,192,192]{2,1,0:T(8,128)(2,1)S(1)}, bf16[2,192,192]{2,1,0:T(8,128)(2,1)}, u32[]{:S(2)}) copy-start(bf16[2,192,192]{2,1,0:T(8,128)(2,1)} %project_ref.4) | copy-start | bytes 442372
  0.0 6.0 %copy-start.9 = (bf16[2,12,24,192]{3,2,1,0:T(8,128)(2,1)S(1)}, bf16[2,12,24,192]{3,2,1,0:T(8,128)(2,1)}, u32[]{:S(2)}) copy-start(bf16[2,12,24,192]{3,2,1,0:T(8,128)(2,1)} %param.25) | copy-start | bytes 663556
  0.0 6.0 %copy-start.10 = (bf16[640,12]{1,0:T(8,128)(2,1)S(1)}, bf16[640,12]{1,0:T(8,128)(2,1)}, u32[]{:S(2)}) copy-start(bf16[640,12]{1,0:T(8,128)(2,1)} %constant.11.clone.of_row_ref) | copy-start | bytes 46084
  0.0 6.0 %copy-start.11 = (bf16[640,24]{1,0:T(8,128)(2,1)S(1)}, bf16[640,24]{1,0:T(8,128)(2,1)}, u32[]{:S(2)}) copy-start(bf16[640,24]{1,0:T(8,128)(2,1)} %constant.12.clone.of_col_ref) | copy-start | bytes 92164
  0.0 6.0 %copy-start.13 = (f32[2,2,192]{2,1,0:T(2,128)S(1)}, f32[2,2,192]{2,1,0:T(2,128)}, u32[]{:S(2)}) copy-start(f32[2,2,192]{2,1,0:T(2,128)} %gains_ref.4) | copy-start | bytes 9220
  0.0 6.0 %copy-start.14 = (s32[12,24]{1,0:T(8,128)S(1)}, s32[12,24]{1,0:T(8,128)}, u32[]{:S(2)}) copy-start(s32[12,24]{1,0:T(8,128)} %land_ref.1) | copy-start | bytes 3460
  0.1 6.0 %copy-start.17 = (s32[1,576]{1,0:T(1,128)S(1)}, s32[1,576]{1,0:T(1,128)}, u32[]{:S(2)}) copy-start(s32[1,576]{1,0:T(1,128)} %constant.10.clone.order_ref) | copy-start | bytes 6916
  0.1 6.0 %copy-start.19 = (f32[192]{0:T(256)S(1)}, f32[192]{0:T(256)}, u32[]{:S(2)}) copy-start(f32[192]{0:T(256)} %param.27) | copy-start | bytes 2308
  6.0 10.2 %copy-start.22 = (f32[2,6,3312]{2,0,1:T(2,128)S(1)}, f32[2,6,3312]{2,0,1:T(2,128)}, u32[]{:S(2)}) copy-start(f32[2,6,3312]{2,0,1:T(2,128)} %param.29) | copy-start | bytes 476932
  10.0 10.5 %collective-permute-start = (bf16[4,40,192]{2,1,0:T(8,128)(2,1)S(1)}, bf16[4,40,192]{2,1,0:T(8,128)(2,1)S(1)}, u32[]{:S(2)}, u32[]{:S(2)}) collective-permute-start(bf16[4,40,192]{2,1,0:T(8,128)(2,1)S(1)} %bitcast.65), channel_id=1, source_target_pairs={{0,2},{2,4},{4,6},{6,8},{8,10},{10,12},{12,14},{14,0},{1,3},{3,5},... | collective-permute-start | bytes 184328 | tf_op jit(solution)/shard_map/ppermute | solution.py:563
  13.0 7.5 %collective-permute-start.1 = (bf16[4,40,192]{2,1,0:T(8,128)(2,1)S(1)}, bf16[4,40,192]{2,1,0:T(8,128)(2,1)S(1)}, u32[]{:S(2)}, u32[]{:S(2)}) collective-permute-start(bf16[4,40,192]{2,1,0:T(8,128)(2,1)S(1)} %bitcast.64), channel_id=1, source_target_pairs={{2,0},{4,2},{6,4},{8,6},{10,8},{12,10},{14,12},{0,14},{3,1},{5,3},... | collective-permute-start | bytes 184328 | tf_op jit(solution)/shard_map/ppermute | solution.py:564
  16.1 6.8 %copy-start.21 = (f32[2,12,3312]{2,0,1:T(2,128)S(1)}, f32[2,12,3312]{2,0,1:T(2,128)}, u32[]{:S(2)}) copy-start(f32[2,12,3312]{2,0,1:T(2,128)} %param.37) | copy-start | bytes 953860
  20.6 7.5 %collective-permute-start.3 = (bf16[6,40,192]{2,1,0:T(8,128)(2,1)S(1)}, bf16[6,40,192]{2,1,0:T(8,128)(2,1)S(1)}, u32[]{:S(2)}, u32[]{:S(2)}) collective-permute-start(bf16[6,40,192]{2,1,0:T(8,128)(2,1)S(1)} %pad_maximum_fusion.1), channel_id=1, source_target_pairs={{1,0},{16,1},{17,16},{0,17},{3,2},{18,3},{19,18},{2,19},{5,4},{20,... | collective-permute-start | bytes 276488 | tf_op jit(solution)/shard_map/ppermute | solution.py:572
  21.3 6.8 %collective-permute-start.2 = (bf16[6,40,192]{2,1,0:T(8,128)(2,1)S(1)}, bf16[6,40,192]{2,1,0:T(8,128)(2,1)S(1)}, u32[]{:S(2)}, u32[]{:S(2)}) collective-permute-start(bf16[6,40,192]{2,1,0:T(8,128)(2,1)S(1)} %pad_maximum_fusion), channel_id=1, source_target_pairs={{0,1},{1,16},{16,17},{17,0},{2,3},{3,18},{18,19},{19,2},{4,5},{5,2... | collective-permute-start | bytes 276488 | tf_op jit(solution)/shard_map/ppermute | solution.py:571
  22.9 5.2 %copy-start.12 = (f32[2,2,384]{2,1,0:T(2,128)S(1)}, f32[2,2,384]{2,1,0:T(2,128)}, u32[]{:S(2)}) copy-start(f32[2,2,384]{2,1,0:T(2,128)} %gains_ref.5) | copy-start | bytes 18436
  22.9 5.2 %copy-start.15 = (f32[768]{0:T(1024)S(1)}, f32[768]{0:T(1024)}, u32[]{:S(2)}) copy-start(f32[768]{0:T(1024)} %merge_gain_ref.1) | copy-start | bytes 9220
  22.9 5.2 %copy-start.16 = (s32[1,640]{1,0:T(1,128)S(1)}, s32[1,640]{1,0:T(1,128)}, u32[]{:S(2)}) copy-start(s32[1,640]{1,0:T(1,128)} %constant.13.clone.merge_order_ref) | copy-start | bytes 7684
  37.8 7.0 %collective-permute-start.4 = (bf16[2,40,384]{2,1,0:T(8,128)(2,1)S(1)}, bf16[2,40,384]{2,1,0:T(8,128)(2,1)S(1)}, u32[]{:S(2)}, u32[]{:S(2)}) collective-permute-start(bf16[2,40,384]{2,1,0:T(8,128)(2,1)S(1)} %bitcast.67), channel_id=1, source_target_pairs={{0,2},{2,4},{4,6},{6,8},{8,10},{10,12},{12,14},{14,0},{1,3},{3,5},... | collective-permute-start | bytes 184328 | tf_op jit(solution)/shard_map/ppermute | solution.py:563
  37.9 6.9 %collective-permute-start.5 = (bf16[2,40,384]{2,1,0:T(8,128)(2,1)S(1)}, bf16[2,40,384]{2,1,0:T(8,128)(2,1)S(1)}, u32[]{:S(2)}, u32[]{:S(2)}) collective-permute-start(bf16[2,40,384]{2,1,0:T(8,128)(2,1)S(1)} %bitcast.66), channel_id=1, source_target_pairs={{2,0},{4,2},{6,4},{8,6},{10,8},{12,10},{14,12},{0,14},{3,1},{5,3},... | collective-permute-start | bytes 184328 | tf_op jit(solution)/shard_map/ppermute | solution.py:564
  44.9 7.6 %collective-permute-start.7 = (bf16[4,40,384]{2,1,0:T(8,128)(2,1)S(1)}, bf16[4,40,384]{2,1,0:T(8,128)(2,1)S(1)}, u32[]{:S(2)}, u32[]{:S(2)}) collective-permute-start(bf16[4,40,384]{2,1,0:T(8,128)(2,1)S(1)} %pad_maximum_fusion.3), channel_id=1, source_target_pairs={{1,0},{16,1},{17,16},{0,17},{3,2},{18,3},{19,18},{2,19},{5,4},{20,... | collective-permute-start | bytes 368648 | tf_op jit(solution)/shard_map/ppermute | solution.py:572
  45.2 7.3 %copy-start = (bf16[2,384,1536]{2,1,0:T(8,128)(2,1)S(1)}, bf16[2,384,1536]{2,1,0:T(8,128)(2,1)}, u32[]{:S(2)}) copy-start(bf16[2,384,1536]{2,1,0:T(8,128)(2,1)} %widen_ref.5) | copy-start | bytes 7077892
  45.3 7.3 %copy-start.1 = (bf16[2,1536,384]{2,1,0:T(8,128)(2,1)S(1)}, bf16[2,1536,384]{2,1,0:T(8,128)(2,1)}, u32[]{:S(2)}) copy-start(bf16[2,1536,384]{2,1,0:T(8,128)(2,1)} %narrow_ref.1) | copy-start | bytes 7077892
  45.3 7.3 %copy-start.2 = (bf16[2,384,1152]{2,1,0:T(8,128)(2,1)S(1)}, bf16[2,384,1152]{2,1,0:T(8,128)(2,1)}, u32[]{:S(2)}) copy-start(bf16[2,384,1152]{2,1,0:T(8,128)(2,1)} %triple_ref.5) | copy-start | bytes 5308420
  45.3 7.3 %copy-start.5 = (bf16[2,384,384]{2,1,0:T(8,128)(2,1)S(1)}, bf16[2,384,384]{2,1,0:T(8,128)(2,1)}, u32[]{:S(2)}) copy-start(bf16[2,384,384]{2,1,0:T(8,128)(2,1)} %project_ref.5) | copy-start | bytes 1769476
  45.3 7.2 %copy-start.8 = (bf16[384,768]{1,0:T(8,128)(2,1)S(1)}, bf16[384,768]{1,0:T(8,128)(2,1)}, u32[]{:S(2)}) copy-start(bf16[384,768]{1,0:T(8,128)(2,1)} %expand_weight_ref.1) | copy-start | bytes 1769476
  45.3 7.2 %copy-start.18 = (s32[1,640]{1,0:T(1,128)S(1)}, s32[1,640]{1,0:T(1,128)}, u32[]{:S(2)}) copy-start(s32[1,640]{1,0:T(1,128)} %constant.14.clone.expand_order_ref) | copy-start | bytes 7684
  45.3 7.2 %copy-start.20 = (f32[192]{0:T(256)S(1)}, f32[192]{0:T(256)}, u32[]{:S(2)}) copy-start(f32[192]{0:T(256)} %param.44) | copy-start | bytes 2308
  45.3 7.2 %collective-permute-start.6 = (bf16[4,40,384]{2,1,0:T(8,128)(2,1)S(1)}, bf16[4,40,384]{2,1,0:T(8,128)(2,1)S(1)}, u32[]{:S(2)}, u32[]{:S(2)}) collective-permute-start(bf16[4,40,384]{2,1,0:T(8,128)(2,1)S(1)} %pad_maximum_fusion.2), channel_id=1, source_target_pairs={{0,1},{1,16},{16,17},{17,0},{2,3},{3,18},{18,19},{19,2},{4,5},{5,2... | collective-permute-start | bytes 368648 | tf_op jit(solution)/shard_map/ppermute | solution.py:571
